TPU v7x, 256 devices: a whole 4x4x8 slice. The times are simulated.
256 devices in a mesh: aux: 8 (over y, core), row: 32 (over x, z).
Axes of the slice: x: 4, y: 4, z: 8, core: 2. Of those that a mesh axis runs over, the one named last changes fastest.
Arguments:
- integrals: bfloat16 [32, 64, 4, 256, 256], P('aux', 'row'), may hold values from -6 to 6
- block_columns: int32 [64, 4], P('row'), may hold values from 0 to 63, as said below
- orbitals: bfloat16 [16384, 2048], P('row'), may hold values from -0.1875 to 0.1875
- occ_mask: int32 [64, 32], replicated, may hold values from 0 to 1, as said below
Outputs:
- exchange: float32 [16384, 1536], P('row', 'aux')
Inputs may be any that keep to these rules, and one draw needn't show every extreme that they name: `block_columns`: each row block has 4 different column blocks, each lying on the same row device as the row block or on the one beside it. `occ_mask`: entry (b, s) is 1 when row block b lies on row device s, and 0 when it lies on a device more than one away from s.
All inputs are finite; a program needn't handle non-finite values.
Results may differ from a plain program's by a relative error of at most 0.0018.
Values may be sent and summed in bfloat16 or wider, within the bound.
No kernel may reach another device: no remote copies, remote signals or barrier semaphores. Data moves between devices by JAX's collectives and lax.ppermute only.
A program may use at most 128 MiB of HBM per device.

v0:
```python
import jax
import jax.numpy as jnp
from jax import lax
from jax.sharding import PartitionSpec as P


def passed_along(block, axis, distance):
    devices = range(lax.axis_size(axis))
    route = [(i - distance, i) for i in devices if i - distance in devices]
    return lax.ppermute(block, axis, route)


def padded_2(block, sides, width):
    for axis, dim in sides:
        count = lax.axis_size(axis)
        forward = [(i, i + 1) for i in range(count - 1)]
        backward = [(target, source) for source, target in forward]
        low = lax.ppermute(
            lax.slice_in_dim(block, block.shape[dim] - width, None, axis=dim), axis, forward
        )
        high = lax.ppermute(lax.slice_in_dim(block, 0, width, axis=dim), axis, backward)
        block = jnp.concatenate([low, block, high], axis=dim)
    return block


def send_slice(masked, position, slice_width, offset):
    outgoing = lax.dynamic_slice_in_dim(masked, (position + offset) * slice_width, slice_width, 1)
    return passed_along(outgoing, "row", offset)


def pass_rows(partial_value, offset):
    return passed_along(partial_value, "row", offset)


def reduce_aux(partial_value):
    return lax.psum_scatter(partial_value, "aux", scatter_dimension=1, tiled=True)


def on_device(integrals, block_columns, orbitals, occ_mask):
    aux_count, row_blocks, kept_blocks, block_size, _ = integrals.shape
    own_rows, occ_count = orbitals.shape
    row_devices = lax.axis_size("row")
    position = lax.axis_index("row")
    slice_width = occ_count // row_devices
    weight_scale = 1.0 / (aux_count * lax.axis_size("aux") * slice_width) ** 0.5
    extended = padded_2(orbitals, (("row", 0),), own_rows)
    ext_blocks = extended.reshape(3 * row_blocks, block_size, occ_count)
    local_columns = block_columns - (position - 1) * row_blocks
    gathered = ext_blocks[local_columns]
    product = jnp.einsum(
        "prkml,rklj->pjrm", integrals, gathered, preferred_element_type=jnp.float32
    )
    mask_rows = lax.dynamic_slice_in_dim(occ_mask, position * row_blocks, row_blocks, 0)
    factor = jnp.repeat(mask_rows.T.astype(jnp.float32), slice_width, axis=0)
    masked = (
        (product * factor[None, :, :, None])
        .astype(jnp.bfloat16)
        .reshape(aux_count, occ_count, own_rows)
    )
    own_slice = lax.dynamic_slice_in_dim(masked, position * slice_width, slice_width, 1)
    from_left = send_slice(masked, position, slice_width, 1)
    from_right = send_slice(masked, position, slice_width, -1)
    window = jnp.concatenate([from_left, own_slice, from_right], 2)
    exchange_slab = (
        jnp.einsum("pjm,pjn->mn", window, window, preferred_element_type=jnp.float32) * weight_scale
    )
    framed = []
    for place in range(3):
        strip = exchange_slab[place * own_rows : (place + 1) * own_rows]
        padded = jnp.pad(strip, ((0, 0), (own_rows, own_rows)))
        framed.append(padded[:, place * own_rows : place * own_rows + 3 * own_rows])
    frames = jnp.stack(framed, 0)
    partial_value = frames[1] + pass_rows(frames[0], -1) + pass_rows(frames[2], 1)
    reduced = reduce_aux(partial_value)
    return reduced


def solution(mesh):
    in_specs = (P("aux", "row", None, None, None), P("row", None), P("row", None), P())
    out_specs = P("row", "aux")
    return jax.shard_map(
        on_device, mesh=mesh, in_specs=in_specs, out_specs=out_specs, check_vma=False
    )
```

profile of v0, /device:TPU:6, one launch (start us, length us, event | category | flops | bytes accessed | tf_op | source)
XLA Modules:
  0.0 241.2 jit_solution(1286651602701420023)
XLA Ops:
  6.5 3.8 %collective-permute-start = (bf16[512,2048]{1,0:T(8,128)(2,1)}, bf16[512,2048]{1,0:T(8,128)(2,1)S(1)}, u32[]{:S(2)}, u32[]{:S(2)}) collective-permute-start(bf16[512,2048]{1,0:T(8,128)(2,1)} %param.6), channel_id=1, source_target_pairs={{0,1},{1,2},{2,3},{3,4},{4,5},{5,6},{6,7},{7,8},{8,9},{9,10},{10,1... | collective-permute-start | bytes 6291464 | tf_op jit(solution)/shard_map/ppermute | solution.py:18
  10.4 6.1 %collective-permute-start.1 = (bf16[512,2048]{1,0:T(8,128)(2,1)}, bf16[512,2048]{1,0:T(8,128)(2,1)}, u32[]{:S(2)}, u32[]{:S(2)}) collective-permute-start(bf16[512,2048]{1,0:T(8,128)(2,1)} %param.6), channel_id=1, source_target_pairs={{1,0},{2,1},{3,2},{4,3},{5,4},{6,5},{7,6},{8,7},{9,8},{10,9},{11,1... | collective-permute-start | bytes 6291464 | tf_op jit(solution)/shard_map/ppermute | solution.py:21
  16.5 0.7 compare_select_fusion
  17.2 0.1 reshape.11
  17.3 0.8 convert_bitcast_fusion
  18.1 0.1 copy.16
  18.2 0.1 mul.33
  18.3 42.0 %collective-permute-done = bf16[512,2048]{1,0:T(8,128)(2,1)S(1)} collective-permute-done((bf16[512,2048]{1,0:T(8,128)(2,1)}, bf16[512,2048]{1,0:T(8,128)(2,1)S(1)}, u32[]{:S(2)}, u32[]{:S(2)}) %collective-permute-start) | collective-permute-done | bytes 2097184 | tf_op jit(solution)/shard_map/ppermute | solution.py:18
  60.4 1.3 collective-permute-done.1
  61.7 5.4 %pad_maximum_fusion = bf16[1536,2048]{1,0:T(8,128)(2,1)} fusion(bf16[512,2048]{1,0:T(8,128)(2,1)} %collective-permute-done.1, bf16[512,2048]{1,0:T(8,128)(2,1)} %param.6, bf16[512,2048]{1,0:T(8,128)(2,1)S(1)} %collective-permute-done), kind=kLoop, calls=%fused_computation.4 | loop fusion | flops 18874368 | bytes 12582912 | tf_op jit(solution)/shard_map/concatenate | solution.py:22
  67.1 7.4 %gather_fusion = bf16[8,256,2048]{2,1,0:T(8,128)(2,1)} fusion(bf16[6,256,2048]{2,1,0:T(8,128)(2,1)} %bitcast.23, s32[1024]{0:T(1024)S(1)} %pad_clamp_fusion), kind=kCustom, calls=%fused_computation | custom fusion | bytes 16777248 | tf_op jit(solution)/shard_map/gather | solution.py:49
  74.5 14.5 %fusion = bf16[4,2048,2,256]{1,3,0,2:T(8,128)(2,1)} fusion(f32[2048,2]{0,1:T(2,128)S(1)} %mul.33, bf16[2,4,256,2048,1]{3,2,1,4,0:T(8,128)(2,1)} %bitcast.26, bf16[4,2,4,256,256]{4,3,2,1,0:T(8,128)(2,1)} %param.4), kind=kOutput, calls=%fused_computation.2 | convolution fusion | flops 8598323200 | bytes 20987904 | tf_op jit(solution)/shard_map/prkml,rklj->pjrm/dot_general | solution.py:50
  89.0 8.3 %copy.17 = bf16[4,2048,2,256]{1,3,2,0:T(8,128)(2,1)} copy(bf16[4,2048,2,256]{1,3,0,2:T(8,128)(2,1)} %fusion) | data formatting | bytes 16777216 | tf_op jit(solution)/shard_map/convert_element_type | solution.py:57
  97.3 1.9 constant_dynamic-slice_fusion.2
  99.2 0.2 copy.26
  99.4 0.2 copy.28
  99.6 6.4 %collective-permute-start.3 = (bf16[4,64,512]{2,1,0:T(8,128)(2,1)S(1)}, bf16[4,64,512]{2,1,0:T(8,128)(2,1)S(1)}, u32[]{:S(2)}, u32[]{:S(2)}) collective-permute-start(bf16[4,64,512]{2,1,0:T(8,128)(2,1)S(1)} %copy.28), channel_id=1, source_target_pairs={{1,0},{2,1},{3,2},{4,3},{5,4},{6,5},{7,6},{8,7},{9,8},{10,9},{11,1... | collective-permute-start | bytes 786440 | tf_op jit(solution)/shard_map/ppermute | solution.py:10
  106.0 1.9 collective-permute-start.2
  107.9 0.2 copy.27
  108.1 2.5 %collective-permute-done.3 = bf16[4,64,512]{2,1,0:T(8,128)(2,1)S(1)} collective-permute-done((bf16[4,64,512]{2,1,0:T(8,128)(2,1)S(1)}, bf16[4,64,512]{2,1,0:T(8,128)(2,1)S(1)}, u32[]{:S(2)}, u32[]{:S(2)}) %collective-permute-start.3) | collective-permute-done | bytes 262176 | tf_op jit(solution)/shard_map/ppermute | solution.py:10
  110.6 6.2 %collective-permute-done.2 = bf16[4,64,512]{2,1,0:T(8,128)(2,1)S(1)} collective-permute-done((bf16[4,64,512]{2,1,0:T(8,128)(2,1)S(1)}, bf16[4,64,512]{2,1,0:T(8,128)(2,1)S(1)}, u32[]{:S(2)}, u32[]{:S(2)}) %collective-permute-start.2) | collective-permute-done | bytes 262176 | tf_op jit(solution)/shard_map/ppermute | solution.py:10
  116.9 1.4 bitcast_multiply_fusion.1
  118.3 0.4 fusion.9
  118.7 0.4 pad_slice_fusion.1
  119.2 0.4 pad_slice_fusion
  119.6 1.9 collective-permute-start.5
  121.5 6.0 %collective-permute-start.4 = (f32[512,1536]{1,0:T(8,128)S(1)}, f32[512,1536]{1,0:T(8,128)S(1)}, u32[]{:S(2)}, u32[]{:S(2)}) collective-permute-start(f32[512,1536]{1,0:T(8,128)S(1)} %pad_slice_fusion.1), channel_id=1, source_target_pairs={{1,0},{2,1},{3,2},{4,3},{5,4},{6,5},{7,6},{8,7},{9,8},{10,9},{11,1... | collective-permute-start | bytes 9437192 | tf_op jit(solution)/shard_map/ppermute | solution.py:10
  127.5 63.8 %collective-permute-done.5 = f32[512,1536]{1,0:T(8,128)S(1)} collective-permute-done((f32[512,1536]{1,0:T(8,128)S(1)}, f32[512,1536]{1,0:T(8,128)S(1)}, u32[]{:S(2)}, u32[]{:S(2)}) %collective-permute-start.5) | collective-permute-done | bytes 3145760 | tf_op jit(solution)/shard_map/ppermute | solution.py:10
  191.3 1.2 collective-permute-done.4
  192.5 1.0 fusion.2
  193.5 2.3 copy.24
  195.9 38.5 %reduce-scatter.4.cloned.1.call-done = f32[192,512]{1,0:T(8,128)} async-done(((f32[1536,512]{1,0:T(8,128)}), f32[192,512]{1,0:T(8,128)}) %reduce-scatter.4.cloned.1.call-update) | async-done | bytes 393232
  (4 shorter events, 0.1 us)
Async XLA Ops:
  6.5 227.8 %reduce-scatter.4.cloned.1.call-start = ((), (), s32[]{:S(2)}) async-start(), calls=%async_computation.1 | async-start | bytes 3538944
  6.5 53.9 %collective-permute-start = (bf16[512,2048]{1,0:T(8,128)(2,1)}, bf16[512,2048]{1,0:T(8,128)(2,1)S(1)}, u32[]{:S(2)}, u32[]{:S(2)}) collective-permute-start(bf16[512,2048]{1,0:T(8,128)(2,1)} %param.6), channel_id=1, source_target_pairs={{0,1},{1,2},{2,3},{3,4},{4,5},{5,6},{6,7},{7,8},{8,9},{9,10},{10,1... | collective-permute-start | bytes 6291464 | tf_op jit(solution)/shard_map/ppermute | solution.py:18
  10.4 51.3 %collective-permute-start.1 = (bf16[512,2048]{1,0:T(8,128)(2,1)}, bf16[512,2048]{1,0:T(8,128)(2,1)}, u32[]{:S(2)}, u32[]{:S(2)}) collective-permute-start(bf16[512,2048]{1,0:T(8,128)(2,1)} %param.6), channel_id=1, source_target_pairs={{1,0},{2,1},{3,2},{4,3},{5,4},{6,5},{7,6},{8,7},{9,8},{10,9},{11,1... | collective-permute-start | bytes 6291464 | tf_op jit(solution)/shard_map/ppermute | solution.py:21
  99.6 11.0 %collective-permute-start.3 = (bf16[4,64,512]{2,1,0:T(8,128)(2,1)S(1)}, bf16[4,64,512]{2,1,0:T(8,128)(2,1)S(1)}, u32[]{:S(2)}, u32[]{:S(2)}) collective-permute-start(bf16[4,64,512]{2,1,0:T(8,128)(2,1)S(1)} %copy.28), channel_id=1, source_target_pairs={{1,0},{2,1},{3,2},{4,3},{5,4},{6,5},{7,6},{8,7},{9,8},{10,9},{11,1... | collective-permute-start | bytes 786440 | tf_op jit(solution)/shard_map/ppermute | solution.py:10
  106.0 10.9 %collective-permute-start.2 = (bf16[4,64,512]{2,1,0:T(8,128)(2,1)S(1)}, bf16[4,64,512]{2,1,0:T(8,128)(2,1)S(1)}, u32[]{:S(2)}, u32[]{:S(2)}) collective-permute-start(bf16[4,64,512]{2,1,0:T(8,128)(2,1)S(1)} %copy.26), channel_id=1, source_target_pairs={{0,1},{1,2},{2,3},{3,4},{4,5},{5,6},{6,7},{7,8},{8,9},{9,10},{10,1... | collective-permute-start | bytes 786440 | tf_op jit(solution)/shard_map/ppermute | solution.py:10
  119.6 71.8 %collective-permute-start.5 = (f32[512,1536]{1,0:T(8,128)S(1)}, f32[512,1536]{1,0:T(8,128)S(1)}, u32[]{:S(2)}, u32[]{:S(2)}) collective-permute-start(f32[512,1536]{1,0:T(8,128)S(1)} %pad_slice_fusion), channel_id=1, source_target_pairs={{0,1},{1,2},{2,3},{3,4},{4,5},{5,6},{6,7},{7,8},{8,9},{9,10},{10,1... | collective-permute-start | bytes 9437192 | tf_op jit(solution)/shard_map/ppermute | solution.py:10
  121.5 71.0 %collective-permute-start.4 = (f32[512,1536]{1,0:T(8,128)S(1)}, f32[512,1536]{1,0:T(8,128)S(1)}, u32[]{:S(2)}, u32[]{:S(2)}) collective-permute-start(f32[512,1536]{1,0:T(8,128)S(1)} %pad_slice_fusion.1), channel_id=1, source_target_pairs={{1,0},{2,1},{3,2},{4,3},{5,4},{6,5},{7,6},{8,7},{9,8},{10,9},{11,1... | collective-permute-start | bytes 9437192 | tf_op jit(solution)/shard_map/ppermute | solution.py:10
Sparse Core Ops, SparseCore 0:
  196.0 38.3 reduce-scatter.3
where the time goes:
time: 242 us; the launch traced here: 241 us
  waiting for transfers between devices  156 us (64%)
  starting transfers between devices  26.2 us (11%)
  local copies, waits for them, and re-layouts  22.1 us (9%)
  matrix products  15.9 us (7%)
  between operations  13.5 us (6%)
  other arithmetic  7.9 us (3%)
    ppermute x4, waiting for transfers between devices, passed_along(): return lax.ppermute(block, axis, route)  73.7 us
    ppermute x1, waiting for transfers between devices, padded_2(): lax.ppermute(lax.slice_in_dim(block, block.shape[dim] - width, None, axis...  42 us
    unnamed x2, waiting for transfers between devices  38.5 us
    ppermute x4, starting transfers between devices, passed_along(): return lax.ppermute(block, axis, route)  16.2 us
    dot_general x1, matrix products, on_device(): jnp.einsum('prkml,rklj->pjrm', integrals, gathered, preferred_element_typ...  14.5 us
    convert_element_type x1, local copies, waits for them, and re-layouts, on_device(): masked = (product * factor[None, :, :, None]).astype(jnp.bfloat16).reshap...  8.28 us
    gather x1, local copies, waits for them, and re-layouts, on_device(): gathered = ext_blocks[local_columns]  7.4 us
    ppermute x1, starting transfers between devices, padded_2(): lax.ppermute(lax.slice_in_dim(block, 0, width, axis=dim), axis, backward)  6.13 us
  transfers between devices with their start and end apart: 7, of which 7 were waited for; matrix products, arithmetic and copies ran while one was open for 1% of the time, Pallas kernels for 0%

commit v1 on v0

v1 whole, which is shorter than its diff:
```python
import jax
import jax.numpy as jnp
from jax import lax
from jax.experimental import pallas as pl
from jax.experimental.pallas import tpu as pltpu
from jax.sharding import PartitionSpec as P

BS = 256
OB = 64
ROWS = 512
BF16 = jnp.bfloat16
F32 = jnp.float32
PARTS = (((0, 192), (384, 512)), ((0, 128), (320, 512)))
RESTS = ((192, 384), (128, 320))
OWN = (((0, 64), (256, 448)), ((64, 256), (448, 512)))
VMEM = pl.BlockSpec(memory_space=pltpu.VMEM)
SMEM = pl.BlockSpec(memory_space=pltpu.SMEM)


def pair_up(left, right):
    return jnp.concatenate([left[:, OB:], right[:, :OB]], axis=1)


def prep_kernel(orb_ref, own_ref, send_ref, buf, sems):
    d = lax.axis_index("row")
    core = lax.axis_index("aux") % 2
    odd = d % 2
    base = (d - 2 - odd) // 2
    last = orb_ref.shape[1] // 128 - 1
    copies = []
    for j in range(3):
        group = jnp.clip(base + j, 0, last)
        copies.append(
            pltpu.make_async_copy(
                orb_ref.at[:, pl.ds(pl.multiple_of(group * 128, 128), 128)],
                buf.at[j],
                sems.at[j],
            )
        )
    for copy in copies:
        copy.start()
    for copy in copies:
        copy.wait()
    b = [buf[j] for j in range(3)]
    line = [b[0], pair_up(b[0], b[1]), b[1], pair_up(b[1], b[2]), b[2]]
    pairs = [jnp.where(odd == 1, line[j + 1], line[j]) for j in range(4)]
    own_ref[:, :128] = pairs[1]
    own_ref[:, 128:] = pairs[2]
    send_ref[:, :128] = jnp.where(core == 0, pairs[2], pairs[0])
    send_ref[:, 128:] = jnp.where(core == 0, pairs[3], pairs[1])


def prep(orbitals):
    rows = orbitals.shape[0]
    return pl.pallas_call(
        prep_kernel,
        name="prep",
        out_shape=[jax.ShapeDtypeStruct((rows, 256), BF16)] * 2,
        in_specs=[pl.BlockSpec(memory_space=pl.ANY)],
        out_specs=[VMEM, VMEM],
        scratch_shapes=[pltpu.VMEM((3, rows, 128), BF16), pltpu.SemaphoreType.DMA((3,))],
    )(orbitals)


def half_kernel(
    cols_ref, mask_ref, int_ref, own_ref, got_ref, swp_ref,
    x_ref, xb_ref, q1_ref, q2_ref, q3_ref, q4_ref, rhs,
):
    p, r = pl.program_id(0), pl.program_id(1)
    d = lax.axis_index("row")
    core = lax.axis_index("aux") % 2

    @pl.when((p == 0) & (r == 0))
    def _():
        for c in range(2):
            first, second = (slice(0, 128), slice(128, 256))
            if c:
                first, second = second, first
            sources = (got_ref, own_ref, swp_ref) if c == 0 else (swp_ref, own_ref, got_ref)

            @pl.when(core == c)
            def _():
                for j, source in enumerate(sources):
                    for h in range(2):
                        rows = slice(h * BS, (h + 1) * BS)
                        rhs[2 * j + h, :, :128] = source[rows, first]
                        rhs[2 * j + h, :, 128:] = source[rows, second]

    acc = jnp.zeros((BS, 256), F32)
    for k in range(4):
        index = cols_ref[r, k] - 2 * (d - 1)
        acc = acc + jnp.dot(int_ref[0, 0, k], rhs[index], preferred_element_type=F32)
    count = mask_ref.shape[0]
    lane = lax.broadcasted_iota(jnp.int32, (1, 256), 1)
    factors = []
    for j in range(3):
        s = d - 1 + j
        inside = (s >= 0) & (s < count)
        value = mask_ref[jnp.clip(s, 0, count - 1), 2 * d + r]
        factors.append(jnp.where(inside, value, 0).astype(F32))
    low, mid, high = factors
    quarter = lane // OB
    f0 = jnp.where(core == 0, low, mid)
    f1 = jnp.where(core == 0, mid, high)
    f2 = jnp.where(core == 0, mid, low)
    f3 = jnp.where(core == 0, high, mid)
    factor = jnp.where(
        quarter == 0, f0, jnp.where(quarter == 1, f1, jnp.where(quarter == 2, f2, f3))
    )
    out = (acc * factor).astype(BF16)
    rows = pl.ds(pl.multiple_of(r * BS, BS), BS)
    lanes = pl.ds(pl.multiple_of(p * 128, 128), 128)
    x_ref[rows, lanes] = out[:, :128]
    xb_ref[rows, lanes] = out[:, 128:]

    @pl.when((p == pl.num_programs(0) - 1) & (r == pl.num_programs(1) - 1))
    def _():
        for c in range(2):

            @pl.when(core == c)
            def _():
                at = 0
                for start, end in PARTS[c]:
                    q1_ref[at : at + end - start] = xb_ref[start:end]
                    at += end - start
                at = 0
                for start, end in PARTS[1 - c]:
                    q3_ref[at : at + end - start] = x_ref[start:end]
                    at += end - start
                start, end = RESTS[1 - c]
                q2_ref[...] = x_ref[start:end]
                start, end = RESTS[c]
                q4_ref[...] = xb_ref[start:end]


def half_transform(block_columns, occ_mask, integrals, own, got, swapped):
    aux, rb, kept, bs, _ = integrals.shape
    whole = lambda p, r: (0, 0)
    lanes = aux * 128
    shapes = [(rb * bs, lanes)] * 2 + [(320, lanes), (192, lanes), (320, lanes), (192, lanes)]
    halo = pl.BlockSpec((rb * bs, 256), whole)
    return pl.pallas_call(
        half_kernel,
        name="half",
        out_shape=[jax.ShapeDtypeStruct(s, BF16) for s in shapes],
        grid=(aux, rb),
        in_specs=[
            SMEM,
            SMEM,
            pl.BlockSpec((1, 1, kept, bs, bs), lambda p, r: (p, r, 0, 0, 0)),
            halo,
            halo,
            halo,
        ],
        out_specs=[pl.BlockSpec(s, whole) for s in shapes],
        scratch_shapes=[pltpu.VMEM((3 * rb, bs, 256), BF16)],
    )(block_columns, occ_mask, integrals, own, got, swapped)


def nt(a, b):
    return lax.dot_general(a, b, (((1,), (1,)), ((), ())), preferred_element_type=F32)


def own_kernel(x_ref, xb_ref, xs_ref, xbs_ref, o_ref):
    core = lax.axis_index("aux") % 2
    lane = lax.broadcasted_iota(jnp.int32, (256, x_ref.shape[1]), 1)
    keep = ((lane // OB) % 2 == 1) == (core == 0)

    def picked(ref):
        both = [jnp.concatenate([ref[s:e] for s, e in OWN[c]], axis=0) for c in range(2)]
        return jnp.where(core == 0, both[0], both[1])

    total = None
    for ref, masked in ((x_ref, False), (xb_ref, True), (xs_ref, False), (xbs_ref, True)):
        rows = picked(ref)
        if masked:
            rows = jnp.where(keep, rows, jnp.zeros_like(rows))
        part = nt(rows, ref[...])
        total = part if total is None else total + part
    o_ref[...] = total


def own_part(x, xb, xs, xbs):
    return pl.pallas_call(
        own_kernel,
        name="own",
        out_shape=jax.ShapeDtypeStruct((256, x.shape[0]), F32),
        in_specs=[VMEM] * 4,
        out_specs=VMEM,
    )(x, xb, xs, xbs)


def off_kernel(
    x_ref, xb_ref, xs_ref, xbs_ref, q1_ref, q2_ref, q3_ref, q4_ref, o_ref,
    keep_ref, s1_ref, s2_ref, s3_ref, chunks,
):
    a = lax.axis_index("aux")
    core, y = a % 2, a // 2
    t = nt(q1_ref[...], x_ref[...]) + nt(q3_ref[...], xs_ref[...])
    u = nt(q2_ref[...], xb_ref[...]) + nt(q4_ref[...], xbs_ref[...])

    @pl.when(core == 0)
    def _():
        chunks[0] = t[:192]
        chunks[1, :128] = t[192:]
        chunks[1, 128:] = o_ref[:64]
        chunks[2] = o_ref[64:]
        chunks[3] = u

    @pl.when(core == 1)
    def _():
        chunks[0] = u
        chunks[1] = o_ref[:192]
        chunks[2, :64] = o_ref[192:]
        chunks[2, 64:] = t[:128]
        chunks[3] = t[128:]

    keep_ref[...] = chunks[y]
    for step, ref in enumerate((s1_ref, s2_ref, s3_ref)):
        ref[...] = chunks[(y + step + 1) % 4].astype(BF16)


def off_part(x, xb, xs, xbs, q1, q2, q3, q4, own):
    shape = (192, x.shape[0])
    return pl.pallas_call(
        off_kernel,
        name="off",
        out_shape=[jax.ShapeDtypeStruct(shape, F32)] + [jax.ShapeDtypeStruct(shape, BF16)] * 3,
        in_specs=[VMEM] * 9,
        out_specs=[VMEM] * 4,
        scratch_shapes=[pltpu.VMEM((4,) + shape, F32)],
    )(x, xb, xs, xbs, q1, q2, q3, q4, own)


def row_moves(rows, chips, core_0_up, cross):
    pairs = []
    for d in range(rows):
        for y in range(chips):
            for core in range(2):
                step = 1 if (core == 0) == core_0_up else -1
                if 0 <= d + step < rows:
                    target = 1 - core if cross else core
                    pairs.append(((2 * y + core) * rows + d, (2 * y + target) * rows + d + step))
    return pairs


def on_device(integrals, block_columns, orbitals, occ_mask):
    aux_devices, rows = lax.axis_size("aux"), lax.axis_size("row")
    chips = aux_devices // 2
    scale = 1.0 / (integrals.shape[0] * aux_devices * OB) ** 0.5

    def move(value, core_0_up, cross):
        return lax.ppermute(value, ("aux", "row"), row_moves(rows, chips, core_0_up, cross))

    def swap(value):
        return lax.ppermute(value, "aux", [(i, i ^ 1) for i in range(aux_devices)])

    def along_y(value, step):
        route = [(i, (i + 2 * step) % aux_devices) for i in range(aux_devices)]
        return lax.ppermute(value, "aux", route)

    own, send = prep(orbitals)
    got = move(send, True, False)
    swapped = swap(got)
    x, xb, q1, q2, q3, q4 = half_transform(
        block_columns, occ_mask.T, integrals, own, got, swapped
    )
    r1 = move(q1, True, False)
    r3 = move(q3, False, True)
    xs = swap(xb)
    xbs = swap(x)
    r2 = move(q2, False, False)
    r4 = move(q4, True, True)
    o = own_part(x, xb, xs, xbs)
    kept, s1, s2, s3 = off_part(x, xb, xs, xbs, r1, r2, r3, r4, o)
    total = kept
    for step, sent in enumerate((s1, s2, s3)):
        total = total + along_y(sent, step + 1).astype(F32)
    return (total * scale).T


def solution(mesh):
    in_specs = (P("aux", "row", None, None, None), P("row", None), P("row", None), P())
    out_specs = P("row", "aux")
    return jax.shard_map(
        on_device, mesh=mesh, in_specs=in_specs, out_specs=out_specs, check_vma=False
    )
```

time: 242 us -> 65.2 us (0.27)
  waiting for transfers between devices: 156 us -> 19.4 us
  local copies, waits for them, and re-layouts: 22.1 us -> 3.01 us
  Pallas kernels: 0 us -> 16.7 us
  matrix products: 15.9 us -> 0 us
  between operations: 13.5 us -> 0.11 us
  other arithmetic: 7.9 us -> 1.86 us
  starting transfers between devices: 26.2 us -> 23.2 us
    ppermute x6 -> x11, waiting for transfers between devices: 117 us -> 19.4 us  [the longest x5 9.3 us: move(): lax.ppermute(value, ('aux', 'row'), row_moves(rows, chips, core_0_up, cro...]
    unnamed x2 -> x0, waiting for transfers between devices: 38.5 us -> none
    pallas_call x0 -> x4, Pallas kernels: none -> 16.7 us  [the longest x1 7.75 us: half_transform(): pl.pallas_call(half_kernel, name='half', out_shape=[jax.ShapeDtypeStruct(...]
    dot_general x2 -> x0, matrix products: 15.9 us -> none  [the longest x1 14.5 us: on_device(): jnp.einsum('prkml,rklj->pjrm', integrals, gathered, preferred_element_typ...]
    convert_element_type x2 -> x0, local copies, waits for them, and re-layouts: 8.35 us -> none  [the longest x1 8.28 us: on_device(): masked = (product * factor[None, :, :, None]).astype(jnp.bfloat16).reshap...]
    gather x1 -> x0, local copies, waits for them, and re-layouts: 7.4 us -> none  [on_device(): gathered = ext_blocks[local_columns]]
    concatenate x1 -> x0, other arithmetic: 5.42 us -> none  [padded_2(): block = jnp.concatenate([low, block, high], axis=dim)]
    ppermute x6 -> x11, starting transfers between devices: 26.2 us -> 23.2 us  [the longest x5 16.9 us: move(): lax.ppermute(value, ('aux', 'row'), row_moves(rows, chips, core_0_up, cro...]
  transfers between devices with their start and end apart: 7 -> 11, of which waited for: 7 -> 5; matrix products, arithmetic and copies ran while one was open for 1% -> 0% of each run, Pallas kernels for 0% -> 5%
where the time goes in v1:
time: 65.2 us; the launch traced here: 64.3 us
  starting transfers between devices  23.2 us (36%)
  waiting for transfers between devices  19.4 us (30%)
  Pallas kernels  16.7 us (26%)
  local copies, waits for them, and re-layouts  3.01 us (5%)
  other arithmetic  1.86 us (3%)
    ppermute x5, starting transfers between devices, move(): lax.ppermute(value, ('aux', 'row'), row_moves(rows, chips, core_0_up, cro...  16.9 us
    ppermute x5, waiting for transfers between devices, move(): lax.ppermute(value, ('aux', 'row'), row_moves(rows, chips, core_0_up, cro...  9.3 us
    ppermute x3, waiting for transfers between devices, along_y(): return lax.ppermute(value, 'aux', route)  8.51 us
    pallas_call x1, Pallas kernels, half_transform(): pl.pallas_call(half_kernel, name='half', out_shape=[jax.ShapeDtypeStruct(...  7.75 us
    ppermute x3, starting transfers between devices, along_y(): return lax.ppermute(value, 'aux', route)  5.82 us
    pallas_call x1, Pallas kernels, off_part(): pl.pallas_call(off_kernel, name='off', out_shape=[jax.ShapeDtypeStruct(sh...  3.89 us
    pallas_call x1, Pallas kernels, own_part(): pl.pallas_call(own_kernel, name='own', out_shape=jax.ShapeDtypeStruct((25...  3.04 us
    unnamed x16, local copies, waits for them, and re-layouts  3.01 us
  transfers between devices with their start and end apart: 11, of which 5 were waited for; matrix products, arithmetic and copies ran while one was open for 0% of the time, Pallas kernels for 5%

profile of v1, /device:TPU:6, one launch (start us, length us, event | category | flops | bytes accessed | tf_op | source)
XLA Modules:
  0.0 64.3 jit_solution(14342998667379594626)
XLA Ops:
  0.0 2.1 %prep.1 = (bf16[512,256]{1,0:T(8,128)(2,1)}, bf16[512,256]{1,0:T(8,128)(2,1)}) custom-call(bf16[512,2048]{1,0:T(8,128)(2,1)} %orb_ref.1), custom_call_target="tpu_custom_call" | custom-call | tf_op jit(solution)/shard_map/prep/pallas_call | solution.py:55
  2.1 3.8 %collective-permute-start = (bf16[512,256]{1,0:T(8,128)(2,1)}, bf16[512,256]{1,0:T(8,128)(2,1)S(1)}, u32[]{:S(2)}, u32[]{:S(2)}) collective-permute-start(bf16[512,256]{1,0:T(8,128)(2,1)} %get-tuple-element.18), channel_id=1, source_target_pairs={{0,1},{64,65},{128,129},{192,193},{1,2},{33,32},{65,66},{97,96},{1... | collective-permute-start | bytes 786440 | tf_op jit(solution)/shard_map/ppermute | solution.py:253
  5.9 8.8 %collective-permute-done.got_ref = bf16[512,256]{1,0:T(8,128)(2,1)S(1)} collective-permute-done((bf16[512,256]{1,0:T(8,128)(2,1)}, bf16[512,256]{1,0:T(8,128)(2,1)S(1)}, u32[]{:S(2)}, u32[]{:S(2)}) %collective-permute-start) | collective-permute-done | bytes 262176 | tf_op jit(solution)/shard_map/ppermute | solution.py:253
  14.7 0.0 collective-permute-start.1
  14.7 1.5 %collective-permute-done.1.swp_ref = bf16[512,256]{1,0:T(8,128)(2,1)S(1)} collective-permute-done((bf16[512,256]{1,0:T(8,128)(2,1)S(1)}, bf16[512,256]{1,0:T(8,128)(2,1)S(1)}, u32[]{:S(2)}, u32[]{:S(2)}) %collective-permute-start.1) | collective-permute-done | bytes 262176 | tf_op jit(solution)/shard_map/ppermute | solution.py:256
  16.2 0.7 %copy-done.5 = bf16[512,256]{1,0:T(8,128)(2,1)} copy-done((bf16[512,256]{1,0:T(8,128)(2,1)}, bf16[512,256]{1,0:T(8,128)(2,1)S(1)}, u32[]{:S(2)}) %copy-start.5) | copy-done | bytes 262168
  16.9 7.7 %half.1 = (bf16[512,512]{1,0:T(8,128)(2,1)}, bf16[512,512]{1,0:T(8,128)(2,1)}, bf16[320,512]{1,0:T(8,128)(2,1)}, bf16[192,512]{1,0:T(8,128)(2,1)}, bf16[320,512]{1,0:T(8,128)(2,1)}, /*index=5*/bf16[192,512]{1,0:T(8,128)(2,1)}) custom-call(s32[2,4]{1,0:T(2,128)} %cols_ref.1, s32[32,64]{1,0:T(8,128)} %bitcast.3, bf16[4,2,4,256,256]{4,3,2,1,0:T(8,128)(2,1)} %int_ref.1, ...), custom_call_target="tpu_custom_call" | custom-call | tf_op jit(solution)/shard_map/half/pallas_call | solution.py:142
  24.6 0.2 collective-permute-start.3
  24.8 0.3 collective-permute-start.2
  25.1 1.9 %collective-permute-start.4 = (bf16[320,512]{1,0:T(8,128)(2,1)}, bf16[320,512]{1,0:T(8,128)(2,1)S(1)}, u32[]{:S(2)}, u32[]{:S(2)}) collective-permute-start(bf16[320,512]{1,0:T(8,128)(2,1)} %get-tuple-element.21), channel_id=1, source_target_pairs={{0,1},{64,65},{128,129},{192,193},{1,2},{33,32},{65,66},{97,96},{1... | collective-permute-start | bytes 983048 | tf_op jit(solution)/shard_map/ppermute | solution.py:253
  27.1 4.5 %collective-permute-start.6 = (bf16[320,512]{1,0:T(8,128)(2,1)}, bf16[320,512]{1,0:T(8,128)(2,1)S(1)}, u32[]{:S(2)}, u32[]{:S(2)}) collective-permute-start(bf16[320,512]{1,0:T(8,128)(2,1)} %get-tuple-element.23), channel_id=1, source_target_pairs={{32,1},{96,65},{160,129},{224,193},{1,32},{33,2},{65,96},{97,66},{... | collective-permute-start | bytes 983048 | tf_op jit(solution)/shard_map/ppermute | solution.py:253
  31.5 3.5 %collective-permute-start.5 = (bf16[192,512]{1,0:T(8,128)(2,1)}, bf16[192,512]{1,0:T(8,128)(2,1)S(1)}, u32[]{:S(2)}, u32[]{:S(2)}) collective-permute-start(bf16[192,512]{1,0:T(8,128)(2,1)} %get-tuple-element.22), channel_id=1, source_target_pairs={{32,33},{96,97},{160,161},{224,225},{1,0},{33,34},{65,64},{97,98},... | collective-permute-start | bytes 589832 | tf_op jit(solution)/shard_map/ppermute | solution.py:253
  35.0 0.0 collective-permute-done.3.xbs_ref
  35.0 3.2 %collective-permute-start.7 = (bf16[192,512]{1,0:T(8,128)(2,1)}, bf16[192,512]{1,0:T(8,128)(2,1)S(1)}, u32[]{:S(2)}, u32[]{:S(2)}) collective-permute-start(bf16[192,512]{1,0:T(8,128)(2,1)} %get-tuple-element.24), channel_id=1, source_target_pairs={{0,33},{64,97},{128,161},{192,225},{1,34},{33,0},{65,98},{97,64},{... | collective-permute-start | bytes 589832 | tf_op jit(solution)/shard_map/ppermute | solution.py:253
  38.2 0.0 collective-permute-done.2.xs_ref
  38.3 0.8 %copy-done.1 = bf16[512,512]{1,0:T(8,128)(2,1)} copy-done((bf16[512,512]{1,0:T(8,128)(2,1)}, bf16[512,512]{1,0:T(8,128)(2,1)S(1)}, u32[]{:S(2)}) %copy-start.1) | copy-done | bytes 524312
  39.1 3.0 %own.1.o_ref = f32[256,512]{1,0:T(8,128)} custom-call(bf16[512,512]{1,0:T(8,128)(2,1)} %get-tuple-element.19.x_ref, bf16[512,512]{1,0:T(8,128)(2,1)} %get-tuple-element.20.xb_ref, bf16[512,512]{1,0:T(8,128)(2,1)} %copy-done.1, bf16[512,512]{1,0:T(8,128)(2,1)} %copy-done), custom_call_target="tpu_custom_call" | custom-call | tf_op jit(solution)/shard_map/own/pallas_call | solution.py:184
  42.1 0.0 collective-permute-done.5.q2_ref
  42.1 0.5 collective-permute-done.7.q4_ref
  42.7 0.0 collective-permute-done.4.q1_ref
  42.7 0.0 collective-permute-done.6.q3_ref
  42.7 0.1 copy-done.6
  42.8 0.5 copy-done.7
  43.3 0.1 copy-done.2
  43.4 0.7 %copy-done.3 = bf16[320,512]{1,0:T(8,128)(2,1)} copy-done((bf16[320,512]{1,0:T(8,128)(2,1)}, bf16[320,512]{1,0:T(8,128)(2,1)S(1)}, u32[]{:S(2)}) %copy-start.3) | copy-done | bytes 327704
  44.2 3.9 %off.1 = (f32[192,512]{1,0:T(8,128)}, bf16[192,512]{1,0:T(8,128)(2,1)}, bf16[192,512]{1,0:T(8,128)(2,1)}, bf16[192,512]{1,0:T(8,128)(2,1)}) custom-call(bf16[512,512]{1,0:T(8,128)(2,1)} %get-tuple-element.19.x_ref, bf16[512,512]{1,0:T(8,128)(2,1)} %get-tuple-element.20.xb_ref, bf16[512,512]{1,0:T(8,128)(2,1)} %copy-done.1, bf16[512,512]{1,0:T(8,128)(2,1)} %copy-done, ...), custom_call_target="tpu_custom_call" | custom-call | tf_op jit(solution)/shard_map/off/pallas_call | solution.py:225
  48.1 1.6 %collective-permute-start.8 = (bf16[192,512]{1,0:T(8,128)(2,1)}, bf16[192,512]{1,0:T(8,128)(2,1)S(1)}, u32[]{:S(2)}, u32[]{:S(2)}) collective-permute-start(bf16[192,512]{1,0:T(8,128)(2,1)} %get-tuple-element.26), channel_id=1, source_target_pairs={{0,64},{32,96},{64,128},{96,160},{128,192},{160,224},{192,0},{224,... | collective-permute-start | bytes 589832 | tf_op jit(solution)/shard_map/ppermute | solution.py:260
  49.7 2.9 %collective-permute-start.9 = (bf16[192,512]{1,0:T(8,128)(2,1)}, bf16[192,512]{1,0:T(8,128)(2,1)S(1)}, u32[]{:S(2)}, u32[]{:S(2)}) collective-permute-start(bf16[192,512]{1,0:T(8,128)(2,1)} %get-tuple-element.27), channel_id=1, source_target_pairs={{0,128},{32,160},{64,192},{96,224},{128,0},{160,32},{192,64},{224,... | collective-permute-start | bytes 589832 | tf_op jit(solution)/shard_map/ppermute | solution.py:260
  52.6 1.3 %collective-permute-start.10 = (bf16[192,512]{1,0:T(8,128)(2,1)}, bf16[192,512]{1,0:T(8,128)(2,1)S(1)}, u32[]{:S(2)}, u32[]{:S(2)}) collective-permute-start(bf16[192,512]{1,0:T(8,128)(2,1)} %get-tuple-element.28), channel_id=1, source_target_pairs={{0,192},{32,224},{64,0},{96,32},{128,64},{160,96},{192,128},{224,1... | collective-permute-start | bytes 589832 | tf_op jit(solution)/shard_map/ppermute | solution.py:260
  53.9 3.0 %collective-permute-done.8 = bf16[192,512]{1,0:T(8,128)(2,1)S(1)} collective-permute-done((bf16[192,512]{1,0:T(8,128)(2,1)}, bf16[192,512]{1,0:T(8,128)(2,1)S(1)}, u32[]{:S(2)}, u32[]{:S(2)}) %collective-permute-start.8) | collective-permute-done | bytes 196640 | tf_op jit(solution)/shard_map/ppermute | solution.py:260
  56.9 5.5 %collective-permute-done.9 = bf16[192,512]{1,0:T(8,128)(2,1)S(1)} collective-permute-done((bf16[192,512]{1,0:T(8,128)(2,1)}, bf16[192,512]{1,0:T(8,128)(2,1)S(1)}, u32[]{:S(2)}, u32[]{:S(2)}) %collective-permute-start.9) | collective-permute-done | bytes 196640 | tf_op jit(solution)/shard_map/ppermute | solution.py:260
  62.4 1.9 %multiply_bitcast_fusion = f32[512,192]{0,1:T(8,128)} fusion(bf16[192,512]{1,0:T(8,128)(2,1)S(1)} %collective-permute-done.10, bf16[192,512]{1,0:T(8,128)(2,1)S(1)} %collective-permute-done.9, f32[192,512]{1,0:T(8,128)} %get-tuple-element.25, bf16[192,512]{1,0:T(8,128)(2,1)S(1)} %collective-permute-done.8), kind=kLoop, calls=%fused_computation | loop fusion | flops 688128 | bytes 1376256 | tf_op jit(solution)/shard_map/transpose | solution.py:279
  (11 shorter events, 0.0 us)
Async XLA Ops:
  2.1 12.6 %collective-permute-start = (bf16[512,256]{1,0:T(8,128)(2,1)}, bf16[512,256]{1,0:T(8,128)(2,1)S(1)}, u32[]{:S(2)}, u32[]{:S(2)}) collective-permute-start(bf16[512,256]{1,0:T(8,128)(2,1)} %get-tuple-element.18), channel_id=1, source_target_pairs={{0,1},{64,65},{128,129},{192,193},{1,2},{33,32},{65,66},{97,96},{1... | collective-permute-start | bytes 786440 | tf_op jit(solution)/shard_map/ppermute | solution.py:253
  14.7 1.5 %copy-start.4 = (bf16[512,256]{1,0:T(8,128)(2,1)}, bf16[512,256]{1,0:T(8,128)(2,1)S(1)}, u32[]{:S(2)}) copy-start(bf16[512,256]{1,0:T(8,128)(2,1)S(1)} %collective-permute-done.got_ref) | copy-start | bytes 786436
  14.7 1.5 %collective-permute-start.1 = (bf16[512,256]{1,0:T(8,128)(2,1)S(1)}, bf16[512,256]{1,0:T(8,128)(2,1)S(1)}, u32[]{:S(2)}, u32[]{:S(2)}) collective-permute-start(bf16[512,256]{1,0:T(8,128)(2,1)S(1)} %collective-permute-done.got_ref), channel_id=1, source_target_pairs={{0,32},{32,0},{64,96},{96,64},{128,160},{160,128},{192,224},{224,1... | collective-permute-start | bytes 786440 | tf_op jit(solution)/shard_map/ppermute | solution.py:256
  16.2 0.7 %copy-start.5 = (bf16[512,256]{1,0:T(8,128)(2,1)}, bf16[512,256]{1,0:T(8,128)(2,1)S(1)}, u32[]{:S(2)}) copy-start(bf16[512,256]{1,0:T(8,128)(2,1)S(1)} %collective-permute-done.1.swp_ref) | copy-start | bytes 786436
  24.6 10.4 %collective-permute-start.3 = (bf16[512,512]{1,0:T(8,128)(2,1)}, bf16[512,512]{1,0:T(8,128)(2,1)S(1)}, u32[]{:S(2)}, u32[]{:S(2)}) collective-permute-start(bf16[512,512]{1,0:T(8,128)(2,1)} %get-tuple-element.19.x_ref), channel_id=1, source_target_pairs={{0,32},{32,0},{64,96},{96,64},{128,160},{160,128},{192,224},{224,1... | collective-permute-start | bytes 1572872 | tf_op jit(solution)/shard_map/ppermute | solution.py:256
  24.8 13.4 %collective-permute-start.2 = (bf16[512,512]{1,0:T(8,128)(2,1)}, bf16[512,512]{1,0:T(8,128)(2,1)S(1)}, u32[]{:S(2)}, u32[]{:S(2)}) collective-permute-start(bf16[512,512]{1,0:T(8,128)(2,1)} %get-tuple-element.20.xb_ref), channel_id=1, source_target_pairs={{0,32},{32,0},{64,96},{96,64},{128,160},{160,128},{192,224},{224,1... | collective-permute-start | bytes 1572872 | tf_op jit(solution)/shard_map/ppermute | solution.py:256
  25.1 17.5 %collective-permute-start.4 = (bf16[320,512]{1,0:T(8,128)(2,1)}, bf16[320,512]{1,0:T(8,128)(2,1)S(1)}, u32[]{:S(2)}, u32[]{:S(2)}) collective-permute-start(bf16[320,512]{1,0:T(8,128)(2,1)} %get-tuple-element.21), channel_id=1, source_target_pairs={{0,1},{64,65},{128,129},{192,193},{1,2},{33,32},{65,66},{97,96},{1... | collective-permute-start | bytes 983048 | tf_op jit(solution)/shard_map/ppermute | solution.py:253
  27.1 15.6 %collective-permute-start.6 = (bf16[320,512]{1,0:T(8,128)(2,1)}, bf16[320,512]{1,0:T(8,128)(2,1)S(1)}, u32[]{:S(2)}, u32[]{:S(2)}) collective-permute-start(bf16[320,512]{1,0:T(8,128)(2,1)} %get-tuple-element.23), channel_id=1, source_target_pairs={{32,1},{96,65},{160,129},{224,193},{1,32},{33,2},{65,96},{97,66},{... | collective-permute-start | bytes 983048 | tf_op jit(solution)/shard_map/ppermute | solution.py:253
  31.5 10.6 %collective-permute-start.5 = (bf16[192,512]{1,0:T(8,128)(2,1)}, bf16[192,512]{1,0:T(8,128)(2,1)S(1)}, u32[]{:S(2)}, u32[]{:S(2)}) collective-permute-start(bf16[192,512]{1,0:T(8,128)(2,1)} %get-tuple-element.22), channel_id=1, source_target_pairs={{32,33},{96,97},{160,161},{224,225},{1,0},{33,34},{65,64},{97,98},... | collective-permute-start | bytes 589832 | tf_op jit(solution)/shard_map/ppermute | solution.py:253
  35.0 3.2 %copy-start = (bf16[512,512]{1,0:T(8,128)(2,1)}, bf16[512,512]{1,0:T(8,128)(2,1)S(1)}, u32[]{:S(2)}) copy-start(bf16[512,512]{1,0:T(8,128)(2,1)S(1)} %collective-permute-done.3.xbs_ref) | copy-start | bytes 1572868
  35.0 7.6 %collective-permute-start.7 = (bf16[192,512]{1,0:T(8,128)(2,1)}, bf16[192,512]{1,0:T(8,128)(2,1)S(1)}, u32[]{:S(2)}, u32[]{:S(2)}) collective-permute-start(bf16[192,512]{1,0:T(8,128)(2,1)} %get-tuple-element.24), channel_id=1, source_target_pairs={{0,33},{64,97},{128,161},{192,225},{1,34},{33,0},{65,98},{97,64},{... | collective-permute-start | bytes 589832 | tf_op jit(solution)/shard_map/ppermute | solution.py:253
  38.3 0.8 %copy-start.1 = (bf16[512,512]{1,0:T(8,128)(2,1)}, bf16[512,512]{1,0:T(8,128)(2,1)S(1)}, u32[]{:S(2)}) copy-start(bf16[512,512]{1,0:T(8,128)(2,1)S(1)} %collective-permute-done.2.xs_ref) | copy-start | bytes 1572868
  42.1 0.7 %copy-start.6 = (bf16[192,512]{1,0:T(8,128)(2,1)}, bf16[192,512]{1,0:T(8,128)(2,1)S(1)}, u32[]{:S(2)}) copy-start(bf16[192,512]{1,0:T(8,128)(2,1)S(1)} %collective-permute-done.5.q2_ref) | copy-start | bytes 589828
  42.7 0.7 %copy-start.7 = (bf16[192,512]{1,0:T(8,128)(2,1)}, bf16[192,512]{1,0:T(8,128)(2,1)S(1)}, u32[]{:S(2)}) copy-start(bf16[192,512]{1,0:T(8,128)(2,1)S(1)} %collective-permute-done.7.q4_ref) | copy-start | bytes 589828
  42.7 0.8 %copy-start.2 = (bf16[320,512]{1,0:T(8,128)(2,1)}, bf16[320,512]{1,0:T(8,128)(2,1)S(1)}, u32[]{:S(2)}) copy-start(bf16[320,512]{1,0:T(8,128)(2,1)S(1)} %collective-permute-done.4.q1_ref) | copy-start | bytes 983044
  43.4 0.7 %copy-start.3 = (bf16[320,512]{1,0:T(8,128)(2,1)}, bf16[320,512]{1,0:T(8,128)(2,1)S(1)}, u32[]{:S(2)}) copy-start(bf16[320,512]{1,0:T(8,128)(2,1)S(1)} %collective-permute-done.6.q3_ref) | copy-start | bytes 983044
  48.1 8.8 %collective-permute-start.8 = (bf16[192,512]{1,0:T(8,128)(2,1)}, bf16[192,512]{1,0:T(8,128)(2,1)S(1)}, u32[]{:S(2)}, u32[]{:S(2)}) collective-permute-start(bf16[192,512]{1,0:T(8,128)(2,1)} %get-tuple-element.26), channel_id=1, source_target_pairs={{0,64},{32,96},{64,128},{96,160},{128,192},{160,224},{192,0},{224,... | collective-permute-start | bytes 589832 | tf_op jit(solution)/shard_map/ppermute | solution.py:260
  49.7 12.8 %collective-permute-start.9 = (bf16[192,512]{1,0:T(8,128)(2,1)}, bf16[192,512]{1,0:T(8,128)(2,1)S(1)}, u32[]{:S(2)}, u32[]{:S(2)}) collective-permute-start(bf16[192,512]{1,0:T(8,128)(2,1)} %get-tuple-element.27), channel_id=1, source_target_pairs={{0,128},{32,160},{64,192},{96,224},{128,0},{160,32},{192,64},{224,... | collective-permute-start | bytes 589832 | tf_op jit(solution)/shard_map/ppermute | solution.py:260
  52.6 9.9 %collective-permute-start.10 = (bf16[192,512]{1,0:T(8,128)(2,1)}, bf16[192,512]{1,0:T(8,128)(2,1)S(1)}, u32[]{:S(2)}, u32[]{:S(2)}) collective-permute-start(bf16[192,512]{1,0:T(8,128)(2,1)} %get-tuple-element.28), channel_id=1, source_target_pairs={{0,192},{32,224},{64,0},{96,32},{128,64},{160,96},{192,128},{224,1... | collective-permute-start | bytes 589832 | tf_op jit(solution)/shard_map/ppermute | solution.py:260

commit v2 on v1

v2 whole, which is shorter than its diff:
```python
import jax
import jax.numpy as jnp
from jax import lax
from jax.experimental import pallas as pl
from jax.experimental.pallas import tpu as pltpu
from jax.sharding import PartitionSpec as P

BS = 256
OB = 64
BF16 = jnp.bfloat16
F32 = jnp.float32
PARTS = (((0, 192), (384, 512)), ((0, 128), (320, 512)))
RESTS = ((192, 384), (128, 320))
OWN = (((0, 64), (256, 448)), ((64, 256), (448, 512)))
VMEM = pl.BlockSpec(memory_space=pltpu.VMEM)
SMEM = pl.BlockSpec(memory_space=pltpu.SMEM)
ANY = pl.BlockSpec(memory_space=pl.ANY)


def on_chip(*values):
    return [pltpu.with_memory_space_constraint(v, pltpu.VMEM) for v in values]


def in_hbm(value):
    return pltpu.with_memory_space_constraint(value, pltpu.HBM)


def room(megabytes):
    return pltpu.CompilerParams(vmem_limit_bytes=megabytes * 2**20)


def cost(macs, sent):
    return pl.CostEstimate(flops=2 * macs, transcendentals=0, bytes_accessed=sent)


def pair_up(left, right):
    return jnp.concatenate([left[:, OB:], right[:, :OB]], axis=1)


def slice_pairs(orb_ref, buf, sems, others=()):
    d = lax.axis_index("row")
    odd = d % 2
    base = (d - 2 - odd) // 2
    last = orb_ref.shape[1] // 128 - 1
    copies = []
    for j in range(3):
        group = jnp.clip(base + j, 0, last)
        lanes = pl.ds(pl.multiple_of(group * 128, 128), 128)
        copies.append(pltpu.make_async_copy(orb_ref.at[:, lanes], buf.at[j], sems.at[j]))
    copies += others
    for copy in copies:
        copy.start()
    for copy in copies:
        copy.wait()
    b = [buf[j] for j in range(3)]
    line = [b[0], pair_up(b[0], b[1]), b[1], pair_up(b[1], b[2]), b[2]]
    return [jnp.where(odd == 1, line[j + 1], line[j]) for j in range(4)]


def send_kernel(orb_ref, send_ref, buf, sems):
    core = lax.axis_index("aux") % 2
    pairs = slice_pairs(orb_ref, buf, sems)
    send_ref[:, :128] = jnp.where(core == 0, pairs[2], pairs[0])
    send_ref[:, 128:] = jnp.where(core == 0, pairs[3], pairs[1])


def halo_to_send(orbitals):
    rows = orbitals.shape[0]
    return pl.pallas_call(
        send_kernel,
        name="send",
        cost_estimate=cost(512 * 1024, 2**20),
        compiler_params=room(4),
        out_shape=pltpu.VMEM((rows, 256), BF16),
        in_specs=[ANY],
        out_specs=VMEM,
        scratch_shapes=[pltpu.VMEM((3, rows, 128), BF16), pltpu.SemaphoreType.DMA((3,))],
    )(in_hbm(orbitals))


def stage_kernel(orb_ref, int_ref, own_ref, near_ref, buf, sems, int_sems):
    aux, rb = int_ref.shape[:2]
    loads = [
        pltpu.make_async_copy(int_ref.at[p, r], near_ref.at[p, r], int_sems.at[p, r])
        for p in range(aux)
        for r in range(rb)
    ]
    pairs = slice_pairs(orb_ref, buf, sems, loads)
    own_ref[:, :128] = pairs[1]
    own_ref[:, 128:] = pairs[2]


def stage(orbitals, integrals):
    rows = orbitals.shape[0]
    return pl.pallas_call(
        stage_kernel,
        name="stage",
        cost_estimate=cost(512 * 1024, 9 * 2**20),
        compiler_params=room(4),
        out_shape=[pltpu.VMEM((rows, 256), BF16), pltpu.VMEM(integrals.shape, BF16)],
        in_specs=[ANY, ANY],
        out_specs=[VMEM, VMEM],
        scratch_shapes=[
            pltpu.VMEM((3, rows, 128), BF16),
            pltpu.SemaphoreType.DMA((3,)),
            pltpu.SemaphoreType.DMA(integrals.shape[:2]),
        ],
    )(in_hbm(orbitals), in_hbm(integrals))


def half_kernel(
    cols_ref, mask_ref, int_ref, own_ref, got_ref, swp_ref,
    x_ref, xb_ref, q1_ref, q2_ref, q3_ref, q4_ref, rhs,
):
    d = lax.axis_index("row")
    core = lax.axis_index("aux") % 2
    aux, rb, kept = int_ref.shape[:3]

    for c in range(2):
        first, second = (slice(0, 128), slice(128, 256))
        if c:
            first, second = second, first
        sources = (got_ref, own_ref, swp_ref) if c == 0 else (swp_ref, own_ref, got_ref)

        @pl.when(core == c)
        def _():
            for j, source in enumerate(sources):
                for h in range(2):
                    rows = slice(h * BS, (h + 1) * BS)
                    rhs[2 * j + h, :, :128] = source[rows, first]
                    rhs[2 * j + h, :, 128:] = source[rows, second]

    count = mask_ref.shape[0]
    quarter = lax.broadcasted_iota(jnp.int32, (1, 256), 1) // OB
    for r in range(rb):
        factors = []
        for j in range(3):
            s = d - 1 + j
            inside = (s >= 0) & (s < count)
            value = mask_ref[jnp.clip(s, 0, count - 1), rb * d + r]
            factors.append(jnp.where(inside, value, 0).astype(F32))
        low, mid, high = factors
        f0 = jnp.where(core == 0, low, mid)
        f1 = jnp.where(core == 0, mid, high)
        f2 = jnp.where(core == 0, mid, low)
        f3 = jnp.where(core == 0, high, mid)
        factor = jnp.where(
            quarter == 0, f0, jnp.where(quarter == 1, f1, jnp.where(quarter == 2, f2, f3))
        )
        weights = jnp.concatenate([rhs[cols_ref[r, k] - rb * (d - 1)] for k in range(kept)], axis=0)
        for p in range(aux):
            left = jnp.concatenate([int_ref[p, r, k] for k in range(kept)], axis=1)
            acc = jnp.dot(left, weights, preferred_element_type=F32)
            out = (acc * factor).astype(BF16)
            x_ref[r * BS : (r + 1) * BS, p * 128 : (p + 1) * 128] = out[:, :128]
            xb_ref[r * BS : (r + 1) * BS, p * 128 : (p + 1) * 128] = out[:, 128:]

    for c in range(2):

        @pl.when(core == c)
        def _():
            at = 0
            for start, end in PARTS[c]:
                q1_ref[at : at + end - start] = xb_ref[start:end]
                at += end - start
            at = 0
            for start, end in PARTS[1 - c]:
                q3_ref[at : at + end - start] = x_ref[start:end]
                at += end - start
            start, end = RESTS[1 - c]
            q2_ref[...] = x_ref[start:end]
            start, end = RESTS[c]
            q4_ref[...] = xb_ref[start:end]


def half_transform(block_columns, occ_mask, integrals, own, got, swapped):
    aux, rb, kept, bs, _ = integrals.shape
    lanes = aux * 128
    shapes = [(rb * bs, lanes)] * 2 + [(320, lanes), (192, lanes), (320, lanes), (192, lanes)]
    return pl.pallas_call(
        half_kernel,
        name="half",
        cost_estimate=cost(512 * 1024 * 1024, 8 * 2**20),
        compiler_params=room(8),
        out_shape=[pltpu.VMEM(s, BF16) for s in shapes],
        in_specs=[SMEM, SMEM] + [VMEM] * 4,
        out_specs=[VMEM] * 6,
        scratch_shapes=[pltpu.VMEM((3 * rb, bs, 256), BF16)],
    )(block_columns, occ_mask, *on_chip(integrals, own, got, swapped))


def nt(a, b):
    return lax.dot_general(a, b, (((1,), (1,)), ((), ())), preferred_element_type=F32)


def own_kernel(x_ref, xb_ref, xs_ref, xbs_ref, o_ref):
    core = lax.axis_index("aux") % 2
    lane = lax.broadcasted_iota(jnp.int32, (256, x_ref.shape[1]), 1)
    keep = ((lane // OB) % 2 == 1) == (core == 0)

    def picked(ref):
        both = [jnp.concatenate([ref[s:e] for s, e in OWN[c]], axis=0) for c in range(2)]
        return jnp.where(core == 0, both[0], both[1])

    total = None
    for ref, masked in ((x_ref, False), (xb_ref, True), (xs_ref, False), (xbs_ref, True)):
        rows = picked(ref)
        if masked:
            rows = jnp.where(keep, rows, jnp.zeros_like(rows))
        part = nt(rows, ref[...])
        total = part if total is None else total + part
    o_ref[...] = total


def own_part(x, xb, xs, xbs):
    return pl.pallas_call(
        own_kernel,
        name="own",
        cost_estimate=cost(256 * 512 * 2048, 3 * 2**20),
        compiler_params=room(4),
        out_shape=pltpu.VMEM((256, x.shape[0]), F32),
        in_specs=[VMEM] * 4,
        out_specs=VMEM,
    )(*on_chip(x, xb, xs, xbs))


def off_kernel(
    x_ref, xb_ref, xs_ref, xbs_ref, q1_ref, q2_ref, q3_ref, q4_ref, o_ref,
    keep_ref, s1_ref, s2_ref, s3_ref, chunks,
):
    a = lax.axis_index("aux")
    core, y = a % 2, a // 2
    t = nt(q1_ref[...], x_ref[...]) + nt(q3_ref[...], xs_ref[...])
    u = nt(q2_ref[...], xb_ref[...]) + nt(q4_ref[...], xbs_ref[...])

    @pl.when(core == 0)
    def _():
        chunks[0] = t[:192]
        chunks[1, :128] = t[192:]
        chunks[1, 128:] = o_ref[:64]
        chunks[2] = o_ref[64:]
        chunks[3] = u

    @pl.when(core == 1)
    def _():
        chunks[0] = u
        chunks[1] = o_ref[:192]
        chunks[2, :64] = o_ref[192:]
        chunks[2, 64:] = t[:128]
        chunks[3] = t[128:]

    keep_ref[...] = chunks[y]
    for step, ref in enumerate((s1_ref, s2_ref, s3_ref)):
        ref[...] = chunks[(y + step + 1) % 4].astype(BF16)


def off_part(x, xb, xs, xbs, q1, q2, q3, q4, own):
    shape = (192, x.shape[0])
    return pl.pallas_call(
        off_kernel,
        name="off",
        cost_estimate=cost(512 * 512 * 1024, 6 * 2**20),
        compiler_params=room(8),
        out_shape=[pltpu.VMEM(shape, F32)] + [pltpu.VMEM(shape, BF16)] * 3,
        in_specs=[VMEM] * 9,
        out_specs=[VMEM] * 4,
        scratch_shapes=[pltpu.VMEM((4,) + shape, F32)],
    )(*on_chip(x, xb, xs, xbs, q1, q2, q3, q4, own))


def sum_kernel(scale, *refs):
    total = refs[0][...]
    for ref in refs[1:-1]:
        total = total + ref[...].astype(F32)
    refs[-1][...] = total * scale


def sum_parts(scale, parts):
    return pl.pallas_call(
        lambda *refs: sum_kernel(scale, *refs),
        name="sum",
        cost_estimate=cost(192 * 512, 2**20),
        compiler_params=room(4),
        out_shape=jax.ShapeDtypeStruct(parts[0].shape, F32),
        in_specs=[VMEM] * 4,
        out_specs=VMEM,
    )(*on_chip(*parts))


def row_moves(rows, chips, core_0_up, cross):
    pairs = []
    for d in range(rows):
        for y in range(chips):
            for core in range(2):
                step = 1 if (core == 0) == core_0_up else -1
                target = 1 - core if cross else core
                end = (2 * y + target) * rows + (d + step) % rows
                pairs.append(((2 * y + core) * rows + d, end))
    return pairs


def on_device(integrals, block_columns, orbitals, occ_mask):
    aux_devices, rows = lax.axis_size("aux"), lax.axis_size("row")
    chips = aux_devices // 2
    scale = 1.0 / (integrals.shape[0] * aux_devices * OB) ** 0.5

    def move(value, core_0_up, cross):
        return lax.ppermute(value, ("aux", "row"), row_moves(rows, chips, core_0_up, cross))

    def swap(value):
        return lax.ppermute(value, "aux", [(i, i ^ 1) for i in range(aux_devices)])

    def along_y(value, step):
        route = [(i, (i + 2 * step) % aux_devices) for i in range(aux_devices)]
        return lax.ppermute(value, "aux", route)

    send = halo_to_send(orbitals)
    got = move(send, True, False)
    own, near = stage(orbitals, integrals)
    got, own, near = lax.optimization_barrier((got, own, near))
    swapped = swap(got)
    x, xb, q1, q2, q3, q4 = half_transform(block_columns, occ_mask.T, near, own, got, swapped)
    r1 = move(q1, True, False)
    r3 = move(q3, False, True)
    xs = swap(xb)
    xbs = swap(x)
    r2 = move(q2, False, False)
    r4 = move(q4, True, True)
    o = own_part(x, xb, xs, xbs)
    kept, *sent = off_part(x, xb, xs, xbs, r1, r2, r3, r4, o)
    parts = [kept] + [along_y(value, step + 1) for step, value in enumerate(sent)]
    return sum_parts(scale, parts).T


def solution(mesh):
    in_specs = (P("aux", "row", None, None, None), P("row", None), P("row", None), P())
    out_specs = P("row", "aux")
    return jax.shard_map(
        on_device, mesh=mesh, in_specs=in_specs, out_specs=out_specs, check_vma=False
    )
```

time: 65.2 us -> 50.9 us (0.78)
  the two profiles are of different devices: /device:TPU:6 before, /device:TPU:1 now
where the time goes in v2:
time: 50.9 us; the launch traced here: 50.8 us
  starting transfers between devices  22 us (43%)
  waiting for transfers between devices  20 us (39%)
  Pallas kernels  8.69 us (17%)
    ppermute x5, starting transfers between devices, move(): lax.ppermute(value, ('aux', 'row'), row_moves(rows, chips, core_0_up, cro...  14.4 us
    ppermute x5, waiting for transfers between devices, move(): lax.ppermute(value, ('aux', 'row'), row_moves(rows, chips, core_0_up, cro...  11.5 us
    ppermute x3, waiting for transfers between devices, along_y(): return lax.ppermute(value, 'aux', route)  7.31 us
    ppermute x3, starting transfers between devices, along_y(): return lax.ppermute(value, 'aux', route)  5.07 us
    ppermute x3, starting transfers between devices, swap(): return lax.ppermute(value, 'aux', [(i, i ^ 1) for i in range(aux_devices)])  2.59 us
    pallas_call x1, Pallas kernels, stage(): pl.pallas_call(stage_kernel, name='stage', cost_estimate=cost(512 * 1024,...  2.53 us
    pallas_call x1, Pallas kernels, half_transform(): pl.pallas_call(half_kernel, name='half', cost_estimate=cost(512 * 1024 *...  2.29 us
    pallas_call x1, Pallas kernels, halo_to_send(): pl.pallas_call(send_kernel, name='send', cost_estimate=cost(512 * 1024, 2...  1.28 us
  transfers between devices with their start and end apart: 11, of which 6 were waited for; matrix products, arithmetic and copies ran while one was open for 0% of the time, Pallas kernels for 6%

profile of v2, /device:TPU:1, one launch (start us, length us, event | category | flops | bytes accessed | tf_op | source)
XLA Modules:
  0.0 50.8 jit_solution(3205676770351378913)
XLA Ops:
  0.0 0.0 copy-start
  0.0 0.0 copy-start.1
  0.0 1.3 %send.1 = bf16[512,256]{1,0:T(8,128)(2,1)S(1)} custom-call(bf16[512,2048]{1,0:T(8,128)(2,1)} %orb_ref.3), custom_call_target="tpu_custom_call" | custom-call | flops 1048576 | bytes 1048576 | tf_op jit(solution)/shard_map/send/pallas_call | solution.py:69
  1.3 8.7 %collective-permute-start = (bf16[512,256]{1,0:T(8,128)(2,1)S(1)}, bf16[512,256]{1,0:T(8,128)(2,1)S(1)}, u32[]{:S(2)}, u32[]{:S(2)}) collective-permute-start(bf16[512,256]{1,0:T(8,128)(2,1)S(1)} %send.1), channel_id=1, source_target_pairs={{0,1},{32,63},{64,65},{96,127},{128,129},{160,191},{192,193},{224,... | collective-permute-start | bytes 786440 | tf_op jit(solution)/shard_map/ppermute | solution.py:308
  10.0 2.5 %stage.1 = (bf16[512,256]{1,0:T(8,128)(2,1)S(1)}, bf16[4,2,4,256,256]{4,3,2,1,0:T(8,128)(2,1)S(1)}) custom-call(bf16[512,2048]{1,0:T(8,128)(2,1)} %orb_ref.3, bf16[4,2,4,256,256]{4,3,2,1,0:T(8,128)(2,1)} %int_ref.1), custom_call_target="tpu_custom_call" | custom-call | flops 1048576 | bytes 9437184 | tf_op jit(solution)/shard_map/stage/pallas_call | solution.py:95
  12.5 0.8 %collective-permute-done.got_ref = bf16[512,256]{1,0:T(8,128)(2,1)S(1)} collective-permute-done((bf16[512,256]{1,0:T(8,128)(2,1)S(1)}, bf16[512,256]{1,0:T(8,128)(2,1)S(1)}, u32[]{:S(2)}, u32[]{:S(2)}) %collective-permute-start) | collective-permute-done | bytes 262176 | tf_op jit(solution)/shard_map/ppermute | solution.py:308
  13.3 2.0 %collective-permute-start.1 = (bf16[512,256]{1,0:T(8,128)(2,1)S(1)}, bf16[512,256]{1,0:T(8,128)(2,1)S(1)}, u32[]{:S(2)}, u32[]{:S(2)}) collective-permute-start(bf16[512,256]{1,0:T(8,128)(2,1)S(1)} %collective-permute-done.got_ref), channel_id=1, source_target_pairs={{0,32},{32,0},{64,96},{96,64},{128,160},{160,128},{192,224},{224,1... | collective-permute-start | bytes 786440 | tf_op jit(solution)/shard_map/ppermute | solution.py:311
  15.3 1.2 %collective-permute-done.1.swp_ref = bf16[512,256]{1,0:T(8,128)(2,1)S(1)} collective-permute-done((bf16[512,256]{1,0:T(8,128)(2,1)S(1)}, bf16[512,256]{1,0:T(8,128)(2,1)S(1)}, u32[]{:S(2)}, u32[]{:S(2)}) %collective-permute-start.1) | collective-permute-done | bytes 262176 | tf_op jit(solution)/shard_map/ppermute | solution.py:311
  16.4 0.0 copy-done
  16.4 0.0 copy-done.1
  16.4 2.3 %half.1 = (bf16[512,512]{1,0:T(8,128)(2,1)S(1)}, bf16[512,512]{1,0:T(8,128)(2,1)S(1)}, bf16[320,512]{1,0:T(8,128)(2,1)S(1)}, bf16[192,512]{1,0:T(8,128)(2,1)S(1)...) custom-call(s32[2,4]{1,0:T(2,128)S(1)} %copy-done.1, s32[32,64]{1,0:T(8,128)S(1)} %bitcast.2, ...), custom_call_target="tpu_custom_call" | custom-call | flops 1073741824 | bytes 8388608 | tf_op jit(solution)/shard_map/half/pallas_call | solution.py:180
  18.7 0.4 collective-permute-start.3
  19.1 0.2 collective-permute-start.2
  19.3 3.6 %collective-permute-start.4 = (bf16[320,512]{1,0:T(8,128)(2,1)S(1)}, bf16[320,512]{1,0:T(8,128)(2,1)S(1)}, u32[]{:S(2)}, u32[]{:S(2)}) collective-permute-start(bf16[320,512]{1,0:T(8,128)(2,1)S(1)} %get-tuple-element.27), channel_id=1, source_target_pairs={{0,1},{32,63},{64,65},{96,127},{128,129},{160,191},{192,193},{224,... | collective-permute-start | bytes 983048 | tf_op jit(solution)/shard_map/ppermute | solution.py:308
  22.9 0.0 collective-permute-start.6
  23.0 0.0 collective-permute-start.5
  23.0 0.0 collective-permute-done.3.xbs_ref
  23.0 2.1 %collective-permute-start.7 = (bf16[192,512]{1,0:T(8,128)(2,1)S(1)}, bf16[192,512]{1,0:T(8,128)(2,1)S(1)}, u32[]{:S(2)}, u32[]{:S(2)}) collective-permute-start(bf16[192,512]{1,0:T(8,128)(2,1)S(1)} %get-tuple-element.30), channel_id=1, source_target_pairs={{0,33},{32,31},{64,97},{96,95},{128,161},{160,159},{192,225},{224,... | collective-permute-start | bytes 589832 | tf_op jit(solution)/shard_map/ppermute | solution.py:308
  25.0 0.0 collective-permute-done.2.xs_ref
  25.0 0.7 %own.1.o_ref = f32[256,512]{1,0:T(8,128)S(1)} custom-call(bf16[512,512]{1,0:T(8,128)(2,1)S(1)} %get-tuple-element.25.x_ref, bf16[512,512]{1,0:T(8,128)(2,1)S(1)} %get-tuple-element.26.xb_ref, bf16[512,512]{1,0:T(8,128)(2,1)S(1)} %collective-permute-done.2.xs_ref, bf16[512,512]{1,0:T(8,128)(2,1)S(1)} %collective-permute-done.3.xbs_ref), custom_call_target="tpu_custom_call" | custom-call | flops 536870912 | bytes 3145728 | tf_op jit(solution)/shard_map/own/pallas_call | solution.py:216
  25.8 10.3 %collective-permute-done.5.q2_ref = bf16[192,512]{1,0:T(8,128)(2,1)S(1)} collective-permute-done((bf16[192,512]{1,0:T(8,128)(2,1)S(1)}, bf16[192,512]{1,0:T(8,128)(2,1)S(1)}, u32[]{:S(2)}, u32[]{:S(2)}) %collective-permute-start.5) | collective-permute-done | bytes 196640 | tf_op jit(solution)/shard_map/ppermute | solution.py:308
  36.0 0.5 collective-permute-done.7.q4_ref
  36.5 0.0 collective-permute-done.4.q1_ref
  36.5 0.0 collective-permute-done.6.q3_ref
  36.5 1.0 %off.1 = (f32[192,512]{1,0:T(8,128)S(1)}, bf16[192,512]{1,0:T(8,128)(2,1)S(1)}, bf16[192,512]{1,0:T(8,128)(2,1)S(1)}, bf16[192,512]{1,0:T(8,128)(2,1)S(1)}) custom-call(bf16[512,512]{1,0:T(8,128)(2,1)S(1)} %get-tuple-element.25.x_ref, bf16[512,512]{1,0:T(8,128)(2,1)S(1)} %get-tuple-element.26.xb_ref, bf16[512,512]{1,0:T(8,128)(2,1)S(1)} %collective-permute-done.2.xs_ref, ...), custom_call_target="tpu_custom_call" | custom-call | flops 536870912 | bytes 6291456 | tf_op jit(solution)/shard_map/off/pallas_call | solution.py:259
  37.6 1.4 %collective-permute-start.8 = (bf16[192,512]{1,0:T(8,128)(2,1)S(1)}, bf16[192,512]{1,0:T(8,128)(2,1)S(1)}, u32[]{:S(2)}, u32[]{:S(2)}) collective-permute-start(bf16[192,512]{1,0:T(8,128)(2,1)S(1)} %get-tuple-element.32), channel_id=1, source_target_pairs={{0,64},{32,96},{64,128},{96,160},{128,192},{160,224},{192,0},{224,... | collective-permute-start | bytes 589832 | tf_op jit(solution)/shard_map/ppermute | solution.py:315
  38.9 2.6 %collective-permute-start.9 = (bf16[192,512]{1,0:T(8,128)(2,1)S(1)}, bf16[192,512]{1,0:T(8,128)(2,1)S(1)}, u32[]{:S(2)}, u32[]{:S(2)}) collective-permute-start(bf16[192,512]{1,0:T(8,128)(2,1)S(1)} %get-tuple-element.33), channel_id=1, source_target_pairs={{0,128},{32,160},{64,192},{96,224},{128,0},{160,32},{192,64},{224,... | collective-permute-start | bytes 589832 | tf_op jit(solution)/shard_map/ppermute | solution.py:315
  41.6 1.1 %collective-permute-start.10 = (bf16[192,512]{1,0:T(8,128)(2,1)S(1)}, bf16[192,512]{1,0:T(8,128)(2,1)S(1)}, u32[]{:S(2)}, u32[]{:S(2)}) collective-permute-start(bf16[192,512]{1,0:T(8,128)(2,1)S(1)} %get-tuple-element.34), channel_id=1, source_target_pairs={{0,192},{32,224},{64,0},{96,32},{128,64},{160,96},{192,128},{224,1... | collective-permute-start | bytes 589832 | tf_op jit(solution)/shard_map/ppermute | solution.py:315
  42.6 1.9 %collective-permute-done.8.refs_1_ = bf16[192,512]{1,0:T(8,128)(2,1)S(1)} collective-permute-done((bf16[192,512]{1,0:T(8,128)(2,1)S(1)}, bf16[192,512]{1,0:T(8,128)(2,1)S(1)}, u32[]{:S(2)}, u32[]{:S(2)}) %collective-permute-start.8) | collective-permute-done | bytes 196640 | tf_op jit(solution)/shard_map/ppermute | solution.py:315
  44.5 5.5 %collective-permute-done.9.refs_2_ = bf16[192,512]{1,0:T(8,128)(2,1)S(1)} collective-permute-done((bf16[192,512]{1,0:T(8,128)(2,1)S(1)}, bf16[192,512]{1,0:T(8,128)(2,1)S(1)}, u32[]{:S(2)}, u32[]{:S(2)}) %collective-permute-start.9) | collective-permute-done | bytes 196640 | tf_op jit(solution)/shard_map/ppermute | solution.py:315
  49.9 0.0 collective-permute-done.10.refs_3_
  49.9 0.8 %sum.1 = f32[192,512]{1,0:T(8,128)} custom-call(f32[192,512]{1,0:T(8,128)S(1)} %get-tuple-element.31.refs_0_, bf16[192,512]{1,0:T(8,128)(2,1)S(1)} %collective-permute-done.8.refs_1_, bf16[192,512]{1,0:T(8,128)(2,1)S(1)} %collective-permute-done.9.refs_2_, bf16[192,512]{1,0:T(8,128)(2,1)S(1)} %collective-permute-done.10.refs_3_), custom_call_target="tpu_custom_call" | custom-call | flops 196608 | bytes 1048576 | tf_op jit(solution)/shard_map/sum/pallas_call | solution.py:279
Async XLA Ops:
  0.0 16.4 %copy-start = (s32[64,32]{0,1:T(8,128)S(1)}, s32[64,32]{0,1:T(8,128)}, u32[]{:S(2)}) copy-start(s32[64,32]{0,1:T(8,128)} %param.7) | copy-start | bytes 24580
  0.0 16.4 %copy-start.1 = (s32[2,4]{1,0:T(2,128)S(1)}, s32[2,4]{1,0:T(2,128)}, u32[]{:S(2)}) copy-start(s32[2,4]{1,0:T(2,128)} %cols_ref.1) | copy-start | bytes 100
  1.3 12.0 %collective-permute-start = (bf16[512,256]{1,0:T(8,128)(2,1)S(1)}, bf16[512,256]{1,0:T(8,128)(2,1)S(1)}, u32[]{:S(2)}, u32[]{:S(2)}) collective-permute-start(bf16[512,256]{1,0:T(8,128)(2,1)S(1)} %send.1), channel_id=1, source_target_pairs={{0,1},{32,63},{64,65},{96,127},{128,129},{160,191},{192,193},{224,... | collective-permute-start | bytes 786440 | tf_op jit(solution)/shard_map/ppermute | solution.py:308
  13.3 3.2 %collective-permute-start.1 = (bf16[512,256]{1,0:T(8,128)(2,1)S(1)}, bf16[512,256]{1,0:T(8,128)(2,1)S(1)}, u32[]{:S(2)}, u32[]{:S(2)}) collective-permute-start(bf16[512,256]{1,0:T(8,128)(2,1)S(1)} %collective-permute-done.got_ref), channel_id=1, source_target_pairs={{0,32},{32,0},{64,96},{96,64},{128,160},{160,128},{192,224},{224,1... | collective-permute-start | bytes 786440 | tf_op jit(solution)/shard_map/ppermute | solution.py:311
  18.7 4.2 %collective-permute-start.3 = (bf16[512,512]{1,0:T(8,128)(2,1)S(1)}, bf16[512,512]{1,0:T(8,128)(2,1)S(1)}, u32[]{:S(2)}, u32[]{:S(2)}) collective-permute-start(bf16[512,512]{1,0:T(8,128)(2,1)S(1)} %get-tuple-element.25.x_ref), channel_id=1, source_target_pairs={{0,32},{32,0},{64,96},{96,64},{128,160},{160,128},{192,224},{224,1... | collective-permute-start | bytes 1572872 | tf_op jit(solution)/shard_map/ppermute | solution.py:311
  19.1 5.9 %collective-permute-start.2 = (bf16[512,512]{1,0:T(8,128)(2,1)S(1)}, bf16[512,512]{1,0:T(8,128)(2,1)S(1)}, u32[]{:S(2)}, u32[]{:S(2)}) collective-permute-start(bf16[512,512]{1,0:T(8,128)(2,1)S(1)} %get-tuple-element.26.xb_ref), channel_id=1, source_target_pairs={{0,32},{32,0},{64,96},{96,64},{128,160},{160,128},{192,224},{224,1... | collective-permute-start | bytes 1572872 | tf_op jit(solution)/shard_map/ppermute | solution.py:311
  19.3 17.2 %collective-permute-start.4 = (bf16[320,512]{1,0:T(8,128)(2,1)S(1)}, bf16[320,512]{1,0:T(8,128)(2,1)S(1)}, u32[]{:S(2)}, u32[]{:S(2)}) collective-permute-start(bf16[320,512]{1,0:T(8,128)(2,1)S(1)} %get-tuple-element.27), channel_id=1, source_target_pairs={{0,1},{32,63},{64,65},{96,127},{128,129},{160,191},{192,193},{224,... | collective-permute-start | bytes 983048 | tf_op jit(solution)/shard_map/ppermute | solution.py:308
  22.9 13.6 %collective-permute-start.6 = (bf16[320,512]{1,0:T(8,128)(2,1)S(1)}, bf16[320,512]{1,0:T(8,128)(2,1)S(1)}, u32[]{:S(2)}, u32[]{:S(2)}) collective-permute-start(bf16[320,512]{1,0:T(8,128)(2,1)S(1)} %get-tuple-element.29), channel_id=1, source_target_pairs={{0,63},{32,1},{64,127},{96,65},{128,191},{160,129},{192,255},{224,... | collective-permute-start | bytes 983048 | tf_op jit(solution)/shard_map/ppermute | solution.py:308
  23.0 13.1 %collective-permute-start.5 = (bf16[192,512]{1,0:T(8,128)(2,1)S(1)}, bf16[192,512]{1,0:T(8,128)(2,1)S(1)}, u32[]{:S(2)}, u32[]{:S(2)}) collective-permute-start(bf16[192,512]{1,0:T(8,128)(2,1)S(1)} %get-tuple-element.28), channel_id=1, source_target_pairs={{0,31},{32,33},{64,95},{96,97},{128,159},{160,161},{192,223},{224,... | collective-permute-start | bytes 589832 | tf_op jit(solution)/shard_map/ppermute | solution.py:308
  23.0 13.6 %collective-permute-start.7 = (bf16[192,512]{1,0:T(8,128)(2,1)S(1)}, bf16[192,512]{1,0:T(8,128)(2,1)S(1)}, u32[]{:S(2)}, u32[]{:S(2)}) collective-permute-start(bf16[192,512]{1,0:T(8,128)(2,1)S(1)} %get-tuple-element.30), channel_id=1, source_target_pairs={{0,33},{32,31},{64,97},{96,95},{128,161},{160,159},{192,225},{224,... | collective-permute-start | bytes 589832 | tf_op jit(solution)/shard_map/ppermute | solution.py:308
  37.6 6.9 %collective-permute-start.8 = (bf16[192,512]{1,0:T(8,128)(2,1)S(1)}, bf16[192,512]{1,0:T(8,128)(2,1)S(1)}, u32[]{:S(2)}, u32[]{:S(2)}) collective-permute-start(bf16[192,512]{1,0:T(8,128)(2,1)S(1)} %get-tuple-element.32), channel_id=1, source_target_pairs={{0,64},{32,96},{64,128},{96,160},{128,192},{160,224},{192,0},{224,... | collective-permute-start | bytes 589832 | tf_op jit(solution)/shard_map/ppermute | solution.py:315
  38.9 11.0 %collective-permute-start.9 = (bf16[192,512]{1,0:T(8,128)(2,1)S(1)}, bf16[192,512]{1,0:T(8,128)(2,1)S(1)}, u32[]{:S(2)}, u32[]{:S(2)}) collective-permute-start(bf16[192,512]{1,0:T(8,128)(2,1)S(1)} %get-tuple-element.33), channel_id=1, source_target_pairs={{0,128},{32,160},{64,192},{96,224},{128,0},{160,32},{192,64},{224,... | collective-permute-start | bytes 589832 | tf_op jit(solution)/shard_map/ppermute | solution.py:315
  41.6 8.4 %collective-permute-start.10 = (bf16[192,512]{1,0:T(8,128)(2,1)S(1)}, bf16[192,512]{1,0:T(8,128)(2,1)S(1)}, u32[]{:S(2)}, u32[]{:S(2)}) collective-permute-start(bf16[192,512]{1,0:T(8,128)(2,1)S(1)} %get-tuple-element.34), channel_id=1, source_target_pairs={{0,192},{32,224},{64,0},{96,32},{128,64},{160,96},{192,128},{224,1... | collective-permute-start | bytes 589832 | tf_op jit(solution)/shard_map/ppermute | solution.py:315

commit v3 on v2

--- a/solution.py
+++ b/solution.py
@@ -1,3 +1,5 @@
+import functools
+
 import jax
 import jax.numpy as jnp
 from jax import lax
@@ -225,13 +227,16 @@
 
 
 def off_kernel(
-    x_ref, xb_ref, xs_ref, xbs_ref, q1_ref, q2_ref, q3_ref, q4_ref, o_ref,
+    last, x_ref, xb_ref, xs_ref, xbs_ref, q1_ref, q2_ref, q3_ref, q4_ref, o_ref,
     keep_ref, s1_ref, s2_ref, s3_ref, chunks,
 ):
     a = lax.axis_index("aux")
     core, y = a % 2, a // 2
+    d = lax.axis_index("row")
     t = nt(q1_ref[...], x_ref[...]) + nt(q3_ref[...], xs_ref[...])
     u = nt(q2_ref[...], xb_ref[...]) + nt(q4_ref[...], xbs_ref[...])
+    t = jnp.where(d == jnp.where(core == 0, 0, last), 0.0, t)
+    u = jnp.where(d == jnp.where(core == 0, last, 0), 0.0, u)
 
     @pl.when(core == 0)
     def _():
@@ -254,10 +259,10 @@
         ref[...] = chunks[(y + step + 1) % 4].astype(BF16)
 
 
-def off_part(x, xb, xs, xbs, q1, q2, q3, q4, own):
+def off_part(last, x, xb, xs, xbs, q1, q2, q3, q4, own):
     shape = (192, x.shape[0])
     return pl.pallas_call(
-        off_kernel,
+        functools.partial(off_kernel, last),
         name="off",
         cost_estimate=cost(512 * 512 * 1024, 6 * 2**20),
         compiler_params=room(8),
@@ -293,9 +298,11 @@
         for y in range(chips):
             for core in range(2):
                 step = 1 if (core == 0) == core_0_up else -1
-                target = 1 - core if cross else core
-                end = (2 * y + target) * rows + (d + step) % rows
-                pairs.append(((2 * y + core) * rows + d, end))
+                inside = 0 <= d + step < rows
+                target = 1 - core if cross == inside else core
+                end = d + step if inside else d
+                chip = (y + 1) % chips if cross and not inside else y
+                pairs.append(((2 * y + core) * rows + d, (2 * chip + target) * rows + end))
     return pairs
 
 
@@ -327,8 +334,8 @@
     r2 = move(q2, False, False)
     r4 = move(q4, True, True)
     o = own_part(x, xb, xs, xbs)
-    kept, *sent = off_part(x, xb, xs, xbs, r1, r2, r3, r4, o)
-    parts = [kept] + [along_y(value, step + 1) for step, value in enumerate(sent)]
+    kept, *sent = off_part(rows - 1, x, xb, xs, xbs, r1, r2, r3, r4, o)
+    parts = [kept] + [along_y(sent[step - 1], step) for step in (2, 1, 3)]
     return sum_parts(scale, parts).T
 
 

time: 50.9 us -> 46.3 us (0.910)
  the two profiles are of different devices: /device:TPU:1 before, /device:TPU:6 now
where the time goes in v3:
time: 46.3 us; the launch traced here: 45.7 us
  waiting for transfers between devices  22.5 us (49%)
  starting transfers between devices  14.5 us (31%)
  Pallas kernels  8.58 us (19%)
    ppermute x5, waiting for transfers between devices, move(): lax.ppermute(value, ('aux', 'row'), row_moves(rows, chips, core_0_up, cro...  14.1 us
    ppermute x5, starting transfers between devices, move(): lax.ppermute(value, ('aux', 'row'), row_moves(rows, chips, core_0_up, cro...  7.42 us
    ppermute x3, waiting for transfers between devices, along_y(): return lax.ppermute(value, 'aux', route)  6.87 us
    ppermute x3, starting transfers between devices, along_y(): return lax.ppermute(value, 'aux', route)  6.51 us
    pallas_call x1, Pallas kernels, stage(): pl.pallas_call(stage_kernel, name='stage', cost_estimate=cost(512 * 1024,...  2.53 us
    pallas_call x1, Pallas kernels, half_transform(): pl.pallas_call(half_kernel, name='half', cost_estimate=cost(512 * 1024 *...  2.2 us
    ppermute x3, waiting for transfers between devices, swap(): return lax.ppermute(value, 'aux', [(i, i ^ 1) for i in range(aux_devices)])  1.54 us
    pallas_call x1, Pallas kernels, halo_to_send(): pl.pallas_call(send_kernel, name='send', cost_estimate=cost(512 * 1024, 2...  1.28 us
  transfers between devices with their start and end apart: 11, of which 5 were waited for; matrix products, arithmetic and copies ran while one was open for 0% of the time, Pallas kernels for 7%

profile of v3, /device:TPU:6, one launch (start us, length us, event | category | flops | bytes accessed | tf_op | source)
XLA Modules:
  0.0 45.7 jit_solution(5361842710335741760)
XLA Ops:
  0.0 0.0 copy-start
  0.0 0.0 copy-start.1
  0.0 1.3 %send.1 = bf16[512,256]{1,0:T(8,128)(2,1)S(1)} custom-call(bf16[512,2048]{1,0:T(8,128)(2,1)} %orb_ref.3), custom_call_target="tpu_custom_call" | custom-call | flops 1048576 | bytes 1048576 | tf_op jit(solution)/shard_map/send/pallas_call | solution.py:71
  1.3 2.0 %collective-permute-start = (bf16[512,256]{1,0:T(8,128)(2,1)S(1)}, bf16[512,256]{1,0:T(8,128)(2,1)S(1)}, u32[]{:S(2)}, u32[]{:S(2)}) collective-permute-start(bf16[512,256]{1,0:T(8,128)(2,1)S(1)} %send.1), channel_id=1, source_target_pairs={{0,1},{32,0},{64,65},{96,64},{128,129},{160,128},{192,193},{224,19... | collective-permute-start | bytes 786440 | tf_op jit(solution)/shard_map/ppermute | solution.py:315
  3.3 2.5 %stage.1 = (bf16[512,256]{1,0:T(8,128)(2,1)S(1)}, bf16[4,2,4,256,256]{4,3,2,1,0:T(8,128)(2,1)S(1)}) custom-call(bf16[512,2048]{1,0:T(8,128)(2,1)} %orb_ref.3, bf16[4,2,4,256,256]{4,3,2,1,0:T(8,128)(2,1)} %int_ref.1), custom_call_target="tpu_custom_call" | custom-call | flops 1048576 | bytes 9437184 | tf_op jit(solution)/shard_map/stage/pallas_call | solution.py:97
  5.8 6.0 %collective-permute-done.got_ref = bf16[512,256]{1,0:T(8,128)(2,1)S(1)} collective-permute-done((bf16[512,256]{1,0:T(8,128)(2,1)S(1)}, bf16[512,256]{1,0:T(8,128)(2,1)S(1)}, u32[]{:S(2)}, u32[]{:S(2)}) %collective-permute-start) | collective-permute-done | bytes 262176 | tf_op jit(solution)/shard_map/ppermute | solution.py:315
  11.9 0.0 collective-permute-start.1
  11.9 1.5 %collective-permute-done.1.swp_ref = bf16[512,256]{1,0:T(8,128)(2,1)S(1)} collective-permute-done((bf16[512,256]{1,0:T(8,128)(2,1)S(1)}, bf16[512,256]{1,0:T(8,128)(2,1)S(1)}, u32[]{:S(2)}, u32[]{:S(2)}) %collective-permute-start.1) | collective-permute-done | bytes 262176 | tf_op jit(solution)/shard_map/ppermute | solution.py:318
  13.4 0.0 copy-done
  13.4 0.0 copy-done.1
  13.4 2.2 %half.1 = (bf16[512,512]{1,0:T(8,128)(2,1)S(1)}, bf16[512,512]{1,0:T(8,128)(2,1)S(1)}, bf16[320,512]{1,0:T(8,128)(2,1)S(1)}, bf16[192,512]{1,0:T(8,128)(2,1)S(1)...) custom-call(s32[2,4]{1,0:T(2,128)S(1)} %copy-done.1, s32[32,64]{1,0:T(8,128)S(1)} %bitcast.2, ...), custom_call_target="tpu_custom_call" | custom-call | flops 1073741824 | bytes 8388608 | tf_op jit(solution)/shard_map/half/pallas_call | solution.py:182
  15.6 0.3 collective-permute-start.3
  15.9 0.3 collective-permute-start.2
  16.2 0.0 collective-permute-start.4
  16.2 2.6 %collective-permute-start.6 = (bf16[320,512]{1,0:T(8,128)(2,1)S(1)}, bf16[320,512]{1,0:T(8,128)(2,1)S(1)}, u32[]{:S(2)}, u32[]{:S(2)}) collective-permute-start(bf16[320,512]{1,0:T(8,128)(2,1)S(1)} %get-tuple-element.29), channel_id=1, source_target_pairs={{0,64},{32,1},{64,128},{96,65},{128,192},{160,129},{192,0},{224,19... | collective-permute-start | bytes 983048 | tf_op jit(solution)/shard_map/ppermute | solution.py:315
  18.8 1.6 %collective-permute-start.5 = (bf16[192,512]{1,0:T(8,128)(2,1)S(1)}, bf16[192,512]{1,0:T(8,128)(2,1)S(1)}, u32[]{:S(2)}, u32[]{:S(2)}) collective-permute-start(bf16[192,512]{1,0:T(8,128)(2,1)S(1)} %get-tuple-element.28), channel_id=1, source_target_pairs={{0,32},{32,33},{64,96},{96,97},{128,160},{160,161},{192,224},{224,... | collective-permute-start | bytes 589832 | tf_op jit(solution)/shard_map/ppermute | solution.py:315
  20.3 0.0 collective-permute-done.3.xbs_ref
  20.3 1.3 %collective-permute-start.7 = (bf16[192,512]{1,0:T(8,128)(2,1)S(1)}, bf16[192,512]{1,0:T(8,128)(2,1)S(1)}, u32[]{:S(2)}, u32[]{:S(2)}) collective-permute-start(bf16[192,512]{1,0:T(8,128)(2,1)S(1)} %get-tuple-element.30), channel_id=1, source_target_pairs={{0,33},{32,96},{64,97},{96,160},{128,161},{160,224},{192,225},{224... | collective-permute-start | bytes 589832 | tf_op jit(solution)/shard_map/ppermute | solution.py:315
  21.6 0.0 collective-permute-done.2.xs_ref
  21.6 0.7 %own.1.o_ref = f32[256,512]{1,0:T(8,128)S(1)} custom-call(bf16[512,512]{1,0:T(8,128)(2,1)S(1)} %get-tuple-element.25.x_ref, bf16[512,512]{1,0:T(8,128)(2,1)S(1)} %get-tuple-element.26.xb_ref, bf16[512,512]{1,0:T(8,128)(2,1)S(1)} %collective-permute-done.2.xs_ref, bf16[512,512]{1,0:T(8,128)(2,1)S(1)} %collective-permute-done.3.xbs_ref), custom_call_target="tpu_custom_call" | custom-call | flops 536870912 | bytes 3145728 | tf_op jit(solution)/shard_map/own/pallas_call | solution.py:218
  22.4 8.1 %collective-permute-done.5.q2_ref = bf16[192,512]{1,0:T(8,128)(2,1)S(1)} collective-permute-done((bf16[192,512]{1,0:T(8,128)(2,1)S(1)}, bf16[192,512]{1,0:T(8,128)(2,1)S(1)}, u32[]{:S(2)}, u32[]{:S(2)}) %collective-permute-start.5) | collective-permute-done | bytes 196640 | tf_op jit(solution)/shard_map/ppermute | solution.py:315
  30.4 0.0 collective-permute-done.7.q4_ref
  30.5 0.0 collective-permute-done.4.q1_ref
  30.5 0.0 collective-permute-done.6.q3_ref
  30.5 1.0 %off.1 = (f32[192,512]{1,0:T(8,128)S(1)}, bf16[192,512]{1,0:T(8,128)(2,1)S(1)}, bf16[192,512]{1,0:T(8,128)(2,1)S(1)}, bf16[192,512]{1,0:T(8,128)(2,1)S(1)}) custom-call(bf16[512,512]{1,0:T(8,128)(2,1)S(1)} %get-tuple-element.25.x_ref, bf16[512,512]{1,0:T(8,128)(2,1)S(1)} %get-tuple-element.26.xb_ref, bf16[512,512]{1,0:T(8,128)(2,1)S(1)} %collective-permute-done.2.xs_ref, ...), custom_call_target="tpu_custom_call" | custom-call | flops 536870912 | bytes 6291456 | tf_op jit(solution)/shard_map/off/pallas_call | solution.py:264
  31.5 3.3 %collective-permute-start.8 = (bf16[192,512]{1,0:T(8,128)(2,1)S(1)}, bf16[192,512]{1,0:T(8,128)(2,1)S(1)}, u32[]{:S(2)}, u32[]{:S(2)}) collective-permute-start(bf16[192,512]{1,0:T(8,128)(2,1)S(1)} %get-tuple-element.32), channel_id=1, source_target_pairs={{0,128},{32,160},{64,192},{96,224},{128,0},{160,32},{192,64},{224,... | collective-permute-start | bytes 589832 | tf_op jit(solution)/shard_map/ppermute | solution.py:322
  34.7 0.7 %collective-permute-start.9 = (bf16[192,512]{1,0:T(8,128)(2,1)S(1)}, bf16[192,512]{1,0:T(8,128)(2,1)S(1)}, u32[]{:S(2)}, u32[]{:S(2)}) collective-permute-start(bf16[192,512]{1,0:T(8,128)(2,1)S(1)} %get-tuple-element.33), channel_id=1, source_target_pairs={{0,64},{32,96},{64,128},{96,160},{128,192},{160,224},{192,0},{224,... | collective-permute-start | bytes 589832 | tf_op jit(solution)/shard_map/ppermute | solution.py:322
  35.4 2.6 %collective-permute-start.10 = (bf16[192,512]{1,0:T(8,128)(2,1)S(1)}, bf16[192,512]{1,0:T(8,128)(2,1)S(1)}, u32[]{:S(2)}, u32[]{:S(2)}) collective-permute-start(bf16[192,512]{1,0:T(8,128)(2,1)S(1)} %get-tuple-element.34), channel_id=1, source_target_pairs={{0,192},{32,224},{64,0},{96,32},{128,64},{160,96},{192,128},{224,1... | collective-permute-start | bytes 589832 | tf_op jit(solution)/shard_map/ppermute | solution.py:322
  38.0 1.9 %collective-permute-done.8.refs_1_ = bf16[192,512]{1,0:T(8,128)(2,1)S(1)} collective-permute-done((bf16[192,512]{1,0:T(8,128)(2,1)S(1)}, bf16[192,512]{1,0:T(8,128)(2,1)S(1)}, u32[]{:S(2)}, u32[]{:S(2)}) %collective-permute-start.8) | collective-permute-done | bytes 196640 | tf_op jit(solution)/shard_map/ppermute | solution.py:322
  39.9 5.0 %collective-permute-done.9.refs_2_ = bf16[192,512]{1,0:T(8,128)(2,1)S(1)} collective-permute-done((bf16[192,512]{1,0:T(8,128)(2,1)S(1)}, bf16[192,512]{1,0:T(8,128)(2,1)S(1)}, u32[]{:S(2)}, u32[]{:S(2)}) %collective-permute-start.9) | collective-permute-done | bytes 196640 | tf_op jit(solution)/shard_map/ppermute | solution.py:322
  44.8 0.0 collective-permute-done.10.refs_3_
  44.8 0.8 %sum.1 = f32[192,512]{1,0:T(8,128)} custom-call(f32[192,512]{1,0:T(8,128)S(1)} %get-tuple-element.31.refs_0_, bf16[192,512]{1,0:T(8,128)(2,1)S(1)} %collective-permute-done.8.refs_1_, bf16[192,512]{1,0:T(8,128)(2,1)S(1)} %collective-permute-done.9.refs_2_, bf16[192,512]{1,0:T(8,128)(2,1)S(1)} %collective-permute-done.10.refs_3_), custom_call_target="tpu_custom_call" | custom-call | flops 196608 | bytes 1048576 | tf_op jit(solution)/shard_map/sum/pallas_call | solution.py:284
Async XLA Ops:
  0.0 13.4 %copy-start = (s32[64,32]{0,1:T(8,128)S(1)}, s32[64,32]{0,1:T(8,128)}, u32[]{:S(2)}) copy-start(s32[64,32]{0,1:T(8,128)} %param.7) | copy-start | bytes 24580
  0.0 13.4 %copy-start.1 = (s32[2,4]{1,0:T(2,128)S(1)}, s32[2,4]{1,0:T(2,128)}, u32[]{:S(2)}) copy-start(s32[2,4]{1,0:T(2,128)} %cols_ref.1) | copy-start | bytes 100
  1.3 10.6 %collective-permute-start = (bf16[512,256]{1,0:T(8,128)(2,1)S(1)}, bf16[512,256]{1,0:T(8,128)(2,1)S(1)}, u32[]{:S(2)}, u32[]{:S(2)}) collective-permute-start(bf16[512,256]{1,0:T(8,128)(2,1)S(1)} %send.1), channel_id=1, source_target_pairs={{0,1},{32,0},{64,65},{96,64},{128,129},{160,128},{192,193},{224,19... | collective-permute-start | bytes 786440 | tf_op jit(solution)/shard_map/ppermute | solution.py:315
  11.9 1.5 %collective-permute-start.1 = (bf16[512,256]{1,0:T(8,128)(2,1)S(1)}, bf16[512,256]{1,0:T(8,128)(2,1)S(1)}, u32[]{:S(2)}, u32[]{:S(2)}) collective-permute-start(bf16[512,256]{1,0:T(8,128)(2,1)S(1)} %collective-permute-done.got_ref), channel_id=1, source_target_pairs={{0,32},{32,0},{64,96},{96,64},{128,160},{160,128},{192,224},{224,1... | collective-permute-start | bytes 786440 | tf_op jit(solution)/shard_map/ppermute | solution.py:318
  15.6 4.7 %collective-permute-start.3 = (bf16[512,512]{1,0:T(8,128)(2,1)S(1)}, bf16[512,512]{1,0:T(8,128)(2,1)S(1)}, u32[]{:S(2)}, u32[]{:S(2)}) collective-permute-start(bf16[512,512]{1,0:T(8,128)(2,1)S(1)} %get-tuple-element.25.x_ref), channel_id=1, source_target_pairs={{0,32},{32,0},{64,96},{96,64},{128,160},{160,128},{192,224},{224,1... | collective-permute-start | bytes 1572872 | tf_op jit(solution)/shard_map/ppermute | solution.py:318
  15.9 5.7 %collective-permute-start.2 = (bf16[512,512]{1,0:T(8,128)(2,1)S(1)}, bf16[512,512]{1,0:T(8,128)(2,1)S(1)}, u32[]{:S(2)}, u32[]{:S(2)}) collective-permute-start(bf16[512,512]{1,0:T(8,128)(2,1)S(1)} %get-tuple-element.26.xb_ref), channel_id=1, source_target_pairs={{0,32},{32,0},{64,96},{96,64},{128,160},{160,128},{192,224},{224,1... | collective-permute-start | bytes 1572872 | tf_op jit(solution)/shard_map/ppermute | solution.py:318
  16.2 14.3 %collective-permute-start.4 = (bf16[320,512]{1,0:T(8,128)(2,1)S(1)}, bf16[320,512]{1,0:T(8,128)(2,1)S(1)}, u32[]{:S(2)}, u32[]{:S(2)}) collective-permute-start(bf16[320,512]{1,0:T(8,128)(2,1)S(1)} %get-tuple-element.27), channel_id=1, source_target_pairs={{0,1},{32,0},{64,65},{96,64},{128,129},{160,128},{192,193},{224,19... | collective-permute-start | bytes 983048 | tf_op jit(solution)/shard_map/ppermute | solution.py:315
  16.2 14.3 %collective-permute-start.6 = (bf16[320,512]{1,0:T(8,128)(2,1)S(1)}, bf16[320,512]{1,0:T(8,128)(2,1)S(1)}, u32[]{:S(2)}, u32[]{:S(2)}) collective-permute-start(bf16[320,512]{1,0:T(8,128)(2,1)S(1)} %get-tuple-element.29), channel_id=1, source_target_pairs={{0,64},{32,1},{64,128},{96,65},{128,192},{160,129},{192,0},{224,19... | collective-permute-start | bytes 983048 | tf_op jit(solution)/shard_map/ppermute | solution.py:315
  18.8 11.7 %collective-permute-start.5 = (bf16[192,512]{1,0:T(8,128)(2,1)S(1)}, bf16[192,512]{1,0:T(8,128)(2,1)S(1)}, u32[]{:S(2)}, u32[]{:S(2)}) collective-permute-start(bf16[192,512]{1,0:T(8,128)(2,1)S(1)} %get-tuple-element.28), channel_id=1, source_target_pairs={{0,32},{32,33},{64,96},{96,97},{128,160},{160,161},{192,224},{224,... | collective-permute-start | bytes 589832 | tf_op jit(solution)/shard_map/ppermute | solution.py:315
  20.3 10.1 %collective-permute-start.7 = (bf16[192,512]{1,0:T(8,128)(2,1)S(1)}, bf16[192,512]{1,0:T(8,128)(2,1)S(1)}, u32[]{:S(2)}, u32[]{:S(2)}) collective-permute-start(bf16[192,512]{1,0:T(8,128)(2,1)S(1)} %get-tuple-element.30), channel_id=1, source_target_pairs={{0,33},{32,96},{64,97},{96,160},{128,161},{160,224},{192,225},{224... | collective-permute-start | bytes 589832 | tf_op jit(solution)/shard_map/ppermute | solution.py:315
  31.5 8.4 %collective-permute-start.8 = (bf16[192,512]{1,0:T(8,128)(2,1)S(1)}, bf16[192,512]{1,0:T(8,128)(2,1)S(1)}, u32[]{:S(2)}, u32[]{:S(2)}) collective-permute-start(bf16[192,512]{1,0:T(8,128)(2,1)S(1)} %get-tuple-element.32), channel_id=1, source_target_pairs={{0,128},{32,160},{64,192},{96,224},{128,0},{160,32},{192,64},{224,... | collective-permute-start | bytes 589832 | tf_op jit(solution)/shard_map/ppermute | solution.py:322
  34.7 10.1 %collective-permute-start.9 = (bf16[192,512]{1,0:T(8,128)(2,1)S(1)}, bf16[192,512]{1,0:T(8,128)(2,1)S(1)}, u32[]{:S(2)}, u32[]{:S(2)}) collective-permute-start(bf16[192,512]{1,0:T(8,128)(2,1)S(1)} %get-tuple-element.33), channel_id=1, source_target_pairs={{0,64},{32,96},{64,128},{96,160},{128,192},{160,224},{192,0},{224,... | collective-permute-start | bytes 589832 | tf_op jit(solution)/shard_map/ppermute | solution.py:322
  35.4 9.4 %collective-permute-start.10 = (bf16[192,512]{1,0:T(8,128)(2,1)S(1)}, bf16[192,512]{1,0:T(8,128)(2,1)S(1)}, u32[]{:S(2)}, u32[]{:S(2)}) collective-permute-start(bf16[192,512]{1,0:T(8,128)(2,1)S(1)} %get-tuple-element.34), channel_id=1, source_target_pairs={{0,192},{32,224},{64,0},{96,32},{128,64},{160,96},{192,128},{224,1... | collective-permute-start | bytes 589832 | tf_op jit(solution)/shard_map/ppermute | solution.py:322

commit v4 on v3

v4 whole, which is shorter than its diff:
```python
import functools

import jax
import jax.numpy as jnp
from jax import lax
from jax.experimental import pallas as pl
from jax.experimental.pallas import tpu as pltpu
from jax.sharding import PartitionSpec as P

BS = 256
OB = 64
GROUP = 2
BF16 = jnp.bfloat16
F32 = jnp.float32
PARTS = (((0, 192), (384, 512)), ((0, 128), (320, 512)))
RESTS = ((192, 384), (128, 320))
OWN = (((0, 64), (256, 448)), ((64, 256), (448, 512)))
VMEM = pl.BlockSpec(memory_space=pltpu.VMEM)
SMEM = pl.BlockSpec(memory_space=pltpu.SMEM)
ANY = pl.BlockSpec(memory_space=pl.ANY)


def on_chip(*values):
    return [pltpu.with_memory_space_constraint(v, pltpu.VMEM) for v in values]


def in_hbm(value):
    return pltpu.with_memory_space_constraint(value, pltpu.HBM)


def room(megabytes):
    return pltpu.CompilerParams(vmem_limit_bytes=megabytes * 2**20)


def cost(macs, sent):
    return pl.CostEstimate(flops=2 * macs, transcendentals=0, bytes_accessed=sent)


def pair_up(left, right):
    return jnp.concatenate([left[:, OB:], right[:, :OB]], axis=1)


def load_groups(orb_ref, first, buf, sems):
    last = orb_ref.shape[1] // 128 - 1
    copies = []
    for j in range(buf.shape[0]):
        group = jnp.clip(first + j, 0, last)
        lanes = pl.ds(pl.multiple_of(group * 128, 128), 128)
        copies.append(pltpu.make_async_copy(orb_ref.at[:, lanes], buf.at[j], sems.at[j]))
    return copies


def send_kernel(orb_ref, send_ref, buf, sems):
    d = lax.axis_index("row")
    core = lax.axis_index("aux") % 2
    odd = d % 2
    copies = load_groups(orb_ref, (d - 2 - odd) // 2 + 1 - core, buf, sems)
    for copy in copies:
        copy.start()
    for copy in copies:
        copy.wait()
    rows = buf.shape[1]
    half = rows // 2

    @pl.when(odd == 0)
    def _():
        send_ref[:rows] = buf[0]
        send_ref[rows:] = jnp.concatenate([buf[1, :half, :OB], buf[1, half:, :OB]], axis=1)

    @pl.when(odd == 1)
    def _():
        send_ref[:rows] = pair_up(buf[0], buf[1])
        send_ref[rows:] = jnp.concatenate([buf[1, :half, OB:], buf[1, half:, OB:]], axis=1)


def halo_to_send(orbitals):
    rows = orbitals.shape[0]
    return pl.pallas_call(
        send_kernel,
        name="send",
        cost_estimate=cost(512 * 1024, 2**20),
        compiler_params=room(4),
        out_shape=pltpu.VMEM((rows + rows // 2, 128), BF16),
        in_specs=[ANY],
        out_specs=VMEM,
        scratch_shapes=[pltpu.VMEM((2, rows, 128), BF16), pltpu.SemaphoreType.DMA((2,))],
    )(in_hbm(orbitals))


def stage_kernel(
    cols_hbm, mask_hbm, orb_ref, int_ref, own_ref, near_ref, factor_ref, local_ref,
    cols_ref, mask_ref, buf, sems, int_sems, table_sems,
):
    aux, rb, kept = int_ref.shape[:3]
    loads = [
        pltpu.make_async_copy(int_ref.at[p, r], near_ref.at[p, r], int_sems.at[p, r])
        for p in range(aux)
        for r in range(rb)
    ]
    d = lax.axis_index("row")
    odd = d % 2
    copies = load_groups(orb_ref, (d - 2 - odd) // 2, buf, sems) + loads
    tables = [
        pltpu.make_async_copy(cols_hbm, cols_ref, table_sems.at[0]),
        pltpu.make_async_copy(mask_hbm, mask_ref, table_sems.at[1]),
    ]
    for copy in tables + copies:
        copy.start()
    for copy in tables:
        copy.wait()
    core = lax.axis_index("aux") % 2
    count = mask_ref.shape[0]
    quarter = lax.broadcasted_iota(jnp.int32, (1, 256), 1) // OB
    for r in range(rb):
        factors = []
        for j in range(3):
            s = d - 1 + j
            inside = (s >= 0) & (s < count)
            value = mask_ref[jnp.clip(s, 0, count - 1), rb * d + r]
            factors.append(jnp.where(inside, value, 0).astype(F32))
        low, mid, high = factors
        f0 = jnp.where(core == 0, low, mid)
        f1 = jnp.where(core == 0, mid, high)
        f2 = jnp.where(core == 0, mid, low)
        f3 = jnp.where(core == 0, high, mid)
        factor = jnp.where(
            quarter == 0, f0, jnp.where(quarter == 1, f1, jnp.where(quarter == 2, f2, f3))
        )
        factor_ref[r : r + 1] = factor
        for k in range(kept):
            local_ref[r, k] = cols_ref[r, k] - rb * (d - 1)
    for copy in copies:
        copy.wait()

    @pl.when(odd == 0)
    def _():
        own_ref[:, :128] = pair_up(buf[0], buf[1])
        own_ref[:, 128:] = buf[1]

    @pl.when(odd == 1)
    def _():
        own_ref[:, :128] = buf[1]
        own_ref[:, 128:] = pair_up(buf[1], buf[2])


def stage(block_columns, occ_mask, orbitals, integrals):
    rows, rb = orbitals.shape[0], integrals.shape[1]
    return pl.pallas_call(
        stage_kernel,
        name="stage",
        cost_estimate=cost(512 * 1024, 9 * 2**20),
        compiler_params=room(4),
        out_shape=[
            pltpu.VMEM((rows, 256), BF16),
            pltpu.VMEM(integrals.shape, BF16),
            pltpu.VMEM((rb, 256), F32),
            pltpu.SMEM(block_columns.shape, jnp.int32),
        ],
        in_specs=[ANY] * 4,
        out_specs=[VMEM, VMEM, VMEM, SMEM],
        scratch_shapes=[
            pltpu.SMEM(block_columns.shape, jnp.int32),
            pltpu.SMEM(occ_mask.shape, jnp.int32),
            pltpu.VMEM((3, rows, 128), BF16),
            pltpu.SemaphoreType.DMA((3,)),
            pltpu.SemaphoreType.DMA(integrals.shape[:2]),
            pltpu.SemaphoreType.DMA((2,)),
        ],
    )(*[in_hbm(v) for v in (block_columns, occ_mask, orbitals, integrals)])


def half_kernel(
    cols_ref, factor_ref, int_ref, own_ref, got_ref, swp_ref,
    x_ref, q1_ref, q2_ref, q3_ref, q4_ref, rhs,
):
    core = lax.axis_index("aux") % 2
    aux, rb, kept = int_ref.shape[:3]

    for c in range(2):
        first, second = (slice(0, 128), slice(128, 256))
        if c:
            first, second = second, first

        @pl.when(core == c)
        def _():
            for h in range(rb):
                rows = slice(h * BS, (h + 1) * BS)
                rhs[rb + h, :, :128] = own_ref[rows, first]
                rhs[rb + h, :, 128:] = own_ref[rows, second]
            for j, source in ((0, got_ref if c == 0 else swp_ref), (2, swp_ref if c == 0 else got_ref)):
                for h in range(rb):
                    pair = source[h * BS : (h + 1) * BS]
                    third = source[rb * BS :, h * OB : (h + 1) * OB]
                    rhs[rb * j + h, :, first] = pair
                    rhs[rb * j + h, :, second] = jnp.concatenate([pair[:, OB:], third], axis=1)

    for r in range(rb):
        factor = factor_ref[r : r + 1]
        weights = jnp.concatenate([rhs[cols_ref[r, k]] for k in range(kept)], axis=0)
        for start in range(0, aux, GROUP):
            left = jnp.concatenate(
                [int_ref[start : start + GROUP, r, k].reshape(GROUP * BS, BS) for k in range(kept)], axis=1
            )
            acc = jnp.dot(left, weights, preferred_element_type=F32)
            out = (acc * factor).astype(BF16)
            for j in range(GROUP):
                lanes = slice((start + j) * 128, (start + j + 1) * 128)
                x_ref[0, r * BS : (r + 1) * BS, lanes] = out[j * BS : (j + 1) * BS, :128]
                x_ref[1, r * BS : (r + 1) * BS, lanes] = out[j * BS : (j + 1) * BS, 128:]

    for c in range(2):

        @pl.when(core == c)
        def _():
            at = 0
            for start, end in PARTS[c]:
                q1_ref[at : at + end - start] = x_ref[1, start:end]
                at += end - start
            at = 0
            for start, end in PARTS[1 - c]:
                q3_ref[at : at + end - start] = x_ref[0, start:end]
                at += end - start
            start, end = RESTS[1 - c]
            q2_ref[...] = x_ref[0, start:end]
            start, end = RESTS[c]
            q4_ref[...] = x_ref[1, start:end]


def half_transform(columns, factors, integrals, own, got, swapped):
    aux, rb, kept, bs, _ = integrals.shape
    lanes = aux * 128
    shapes = [(2, rb * bs, lanes)] + [(320, lanes), (192, lanes), (320, lanes), (192, lanes)]
    return pl.pallas_call(
        half_kernel,
        name="half",
        cost_estimate=cost(512 * 1024 * 1024, 8 * 2**20),
        compiler_params=room(8),
        out_shape=[pltpu.VMEM(s, BF16) for s in shapes],
        in_specs=[SMEM] + [VMEM] * 5,
        out_specs=[VMEM] * 5,
        scratch_shapes=[pltpu.VMEM((3 * rb, bs, 256), BF16)],
    )(pltpu.with_memory_space_constraint(columns, pltpu.SMEM), *on_chip(factors, integrals, own, got, swapped))


def nt(a, b):
    return lax.dot_general(a, b, (((1,), (1,)), ((), ())), preferred_element_type=F32)


def own_kernel(x_ref, s_ref, o_ref):
    core = lax.axis_index("aux") % 2
    lane = lax.broadcasted_iota(jnp.int32, (256, x_ref.shape[2]), 1)
    keep = ((lane // OB) % 2 == 1) == (core == 0)

    def picked(ref):
        both = [jnp.concatenate([ref[s:e] for s, e in OWN[c]], axis=0) for c in range(2)]
        return jnp.where(core == 0, both[0], both[1])

    total = None
    for ref, masked in (
        (x_ref.at[0], False), (x_ref.at[1], True), (s_ref.at[1], False), (s_ref.at[0], True),
    ):
        rows = picked(ref)
        if masked:
            rows = jnp.where(keep, rows, jnp.zeros_like(rows))
        part = nt(rows, ref[...])
        total = part if total is None else total + part
    o_ref[...] = total


def own_part(x, s):
    return pl.pallas_call(
        own_kernel,
        name="own",
        cost_estimate=cost(256 * 512 * 2048, 3 * 2**20),
        compiler_params=room(4),
        out_shape=pltpu.VMEM((256, x.shape[1]), F32),
        in_specs=[VMEM] * 2,
        out_specs=VMEM,
    )(*on_chip(x, s))


def near_kernel(last, x_ref, s_ref, q1_ref, q3_ref, t_ref):
    d, core = lax.axis_index("row"), lax.axis_index("aux") % 2
    t = nt(q1_ref[...], x_ref[0]) + nt(q3_ref[...], s_ref[1])
    t_ref[...] = jnp.where(d == jnp.where(core == 0, 0, last), 0.0, t)


def near_part(last, x, s, q1, q3):
    return pl.pallas_call(
        functools.partial(near_kernel, last),
        name="near",
        cost_estimate=cost(320 * 512 * 1024, 2 * 2**20),
        compiler_params=room(4),
        out_shape=pltpu.VMEM((320, x.shape[1]), F32),
        in_specs=[VMEM] * 4,
        out_specs=VMEM,
    )(*on_chip(x, s, q1, q3))


def off_kernel(
    last, x_ref, s_ref, q2_ref, q4_ref, o_ref, t_ref, keep_ref, s1_ref, s2_ref, s3_ref, chunks,
):
    a = lax.axis_index("aux")
    core, y = a % 2, a // 2
    d = lax.axis_index("row")
    u = nt(q2_ref[...], x_ref[1]) + nt(q4_ref[...], s_ref[0])
    u = jnp.where(d == jnp.where(core == 0, last, 0), 0.0, u)

    @pl.when(core == 0)
    def _():
        chunks[0] = t_ref[:192]
        chunks[1, :128] = t_ref[192:]
        chunks[1, 128:] = o_ref[:64]
        chunks[2] = o_ref[64:]
        chunks[3] = u

    @pl.when(core == 1)
    def _():
        chunks[0] = u
        chunks[1] = o_ref[:192]
        chunks[2, :64] = o_ref[192:]
        chunks[2, 64:] = t_ref[:128]
        chunks[3] = t_ref[128:]

    keep_ref[...] = chunks[y]
    for step, ref in enumerate((s1_ref, s2_ref, s3_ref)):
        ref[...] = chunks[(y + step + 1) % 4].astype(BF16)


def off_part(last, x, s, q2, q4, own, near):
    shape = (192, x.shape[1])
    return pl.pallas_call(
        functools.partial(off_kernel, last),
        name="off",
        cost_estimate=cost(192 * 512 * 1024, 4 * 2**20),
        compiler_params=room(8),
        out_shape=[pltpu.VMEM(shape, F32)] + [pltpu.VMEM(shape, BF16)] * 3,
        in_specs=[VMEM] * 6,
        out_specs=[VMEM] * 4,
        scratch_shapes=[pltpu.VMEM((4,) + shape, F32)],
    )(*on_chip(x, s, q2, q4, own, near))


def sum_kernel(scale, *refs):
    rows = refs[-1].shape[0]
    at = pl.ds(pl.multiple_of(pl.program_id(0) * rows, rows), rows)
    total = refs[0][at]
    for ref in refs[1:-1]:
        total = total + ref[at].astype(F32)
    refs[-1][...] = total * scale


def sum_parts(scale, parts):
    rows, columns = parts[0].shape
    steps = 1
    return pl.pallas_call(
        functools.partial(sum_kernel, scale),
        name="sum",
        cost_estimate=cost(192 * 512, 2**20),
        compiler_params=room(4),
        grid=(steps,),
        out_shape=jax.ShapeDtypeStruct((rows, columns), F32),
        in_specs=[VMEM] * 4,
        out_specs=pl.BlockSpec((rows // steps, columns), lambda i: (i, 0)),
    )(*on_chip(*parts))


def row_moves(rows, chips, core_0_up, cross):
    pairs = []
    for d in range(rows):
        for y in range(chips):
            for core in range(2):
                step = 1 if (core == 0) == core_0_up else -1
                inside = 0 <= d + step < rows
                target = 1 - core if cross == inside else core
                end = d + step if inside else d
                chip = (y + 1) % chips if cross and not inside else y
                pairs.append(((2 * y + core) * rows + d, (2 * chip + target) * rows + end))
    return pairs


def on_device(integrals, block_columns, orbitals, occ_mask):
    aux_devices, rows = lax.axis_size("aux"), lax.axis_size("row")
    chips = aux_devices // 2
    scale = 1.0 / (integrals.shape[0] * aux_devices * OB) ** 0.5

    def move(value, core_0_up, cross):
        return lax.ppermute(value, ("aux", "row"), row_moves(rows, chips, core_0_up, cross))

    def swap(value):
        return lax.ppermute(value, "aux", [(i, i ^ 1) for i in range(aux_devices)])

    def along_y(value, step):
        route = [(i, (i + 2 * step) % aux_devices) for i in range(aux_devices)]
        return lax.ppermute(value, "aux", route)

    send = halo_to_send(orbitals)
    got = move(send, True, False)
    own, near, factors, columns = stage(block_columns, occ_mask.T, orbitals, integrals)
    got, own, near, factors, columns = lax.optimization_barrier((got, own, near, factors, columns))
    swapped = swap(got)
    x, q1, q2, q3, q4 = half_transform(columns, factors, near, own, got, swapped)
    r1 = move(q1, True, False)
    r3 = move(q3, False, True)
    others = swap(x)
    r2 = move(q2, False, False)
    r4 = move(q4, True, True)
    o = own_part(x, others)
    t = near_part(rows - 1, x, others, r1, r3)
    kept, *sent = off_part(rows - 1, x, others, r2, r4, o, t)
    parts = [kept] + [along_y(sent[step - 1], step) for step in (2, 1, 3)]
    return sum_parts(scale, parts).T


def solution(mesh):
    in_specs = (P("aux", "row", None, None, None), P("row", None), P("row", None), P())
    out_specs = P("row", "aux")
    return jax.shard_map(
        on_device, mesh=mesh, in_specs=in_specs, out_specs=out_specs, check_vma=False
    )
```

time: 46.3 us -> 43.9 us (0.948)
  waiting for transfers between devices: 22.5 us -> 21.1 us
  Pallas kernels: 8.58 us -> 7.87 us
    ppermute x5, waiting for transfers between devices: 14.1 us -> 12.9 us  [move(): lax.ppermute(value, ('aux', 'row'), row_moves(rows, chips, core_0_up, cro...]
    pallas_call x1, Pallas kernels: 2.2 us -> 1.51 us  [half_transform(): pl.pallas_call(half_kernel, name='half', cost_estimate=cost(512 * 1024 *...]
    pallas_call x1 -> x2, Pallas kernels: 0.84 us -> 1.37 us  [the longest x1 0.84 us: sum_parts(): pl.pallas_call(functools.partial(sum_kernel, scale), name='sum', cost_est...]
    ppermute x3 -> x2, waiting for transfers between devices: 1.54 us -> 1.44 us  [swap(): return lax.ppermute(value, 'aux', [(i, i ^ 1) for i in range(aux_devices)])]
  transfers between devices with their start and end apart: 11 -> 10, of which waited for: 5 -> 6; matrix products, arithmetic and copies ran while one was open for 0% -> 0% of each run, Pallas kernels for 7% -> 9%
where the time goes in v4:
time: 43.9 us; the launch traced here: 43.2 us
  waiting for transfers between devices  21.1 us (48%)
  starting transfers between devices  14.2 us (32%)
  Pallas kernels  7.87 us (18%)
    ppermute x5, waiting for transfers between devices, move(): lax.ppermute(value, ('aux', 'row'), row_moves(rows, chips, core_0_up, cro...  12.9 us
    ppermute x5, starting transfers between devices, move(): lax.ppermute(value, ('aux', 'row'), row_moves(rows, chips, core_0_up, cro...  7.42 us
    ppermute x3, waiting for transfers between devices, along_y(): return lax.ppermute(value, 'aux', route)  6.82 us
    ppermute x3, starting transfers between devices, along_y(): return lax.ppermute(value, 'aux', route)  6.52 us
    pallas_call x1, Pallas kernels, stage(): pl.pallas_call(stage_kernel, name='stage', cost_estimate=cost(512 * 1024,...  2.51 us
    pallas_call x1, Pallas kernels, half_transform(): pl.pallas_call(half_kernel, name='half', cost_estimate=cost(512 * 1024 *...  1.51 us
    ppermute x2, waiting for transfers between devices, swap(): return lax.ppermute(value, 'aux', [(i, i ^ 1) for i in range(aux_devices)])  1.44 us
    pallas_call x1, Pallas kernels, halo_to_send(): pl.pallas_call(send_kernel, name='send', cost_estimate=cost(512 * 1024, 2...  1.07 us
  transfers between devices with their start and end apart: 10, of which 6 were waited for; matrix products, arithmetic and copies ran while one was open for 0% of the time, Pallas kernels for 9%

profile of v4, /device:TPU:6, one launch (start us, length us, event | category | flops | bytes accessed | tf_op | source)
XLA Modules:
  0.0 43.2 jit_solution(848234446898140535)
XLA Ops:
  0.0 1.1 %send.1 = bf16[768,128]{1,0:T(8,128)(2,1)S(1)} custom-call(bf16[512,2048]{1,0:T(8,128)(2,1)} %orb_ref.3), custom_call_target="tpu_custom_call" | custom-call | flops 1048576 | bytes 1048576 | tf_op jit(solution)/shard_map/send/pallas_call | solution.py:78
  1.1 2.1 %collective-permute-start = (bf16[768,128]{1,0:T(8,128)(2,1)S(1)}, bf16[768,128]{1,0:T(8,128)(2,1)S(1)}, u32[]{:S(2)}, u32[]{:S(2)}) collective-permute-start(bf16[768,128]{1,0:T(8,128)(2,1)S(1)} %send.1), channel_id=1, source_target_pairs={{0,1},{32,0},{64,65},{96,64},{128,129},{160,128},{192,193},{224,19... | collective-permute-start | bytes 589832 | tf_op jit(solution)/shard_map/ppermute | solution.py:388
  3.1 2.5 %stage.1 = (bf16[512,256]{1,0:T(8,128)(2,1)S(1)}, bf16[4,2,4,256,256]{4,3,2,1,0:T(8,128)(2,1)S(1)}, f32[2,256]{1,0:T(2,128)S(1)}, s32[2,4]{1,0:T(2,128)S(4)}) custom-call(s32[2,4]{1,0:T(2,128)} %cols_hbm.1, s32[32,64]{1,0:T(8,128)} %bitcast.2, bf16[512,2048]{1,0:T(8,128)(2,1)} %orb_ref.3, bf16[4,2,4,256,256]{4,3,2,1,0:T(8,128)(2,1)} %int_ref.1), custom_call_target="tpu_custom_call" | custom-call | flops 1048576 | bytes 9437184 | tf_op jit(solution)/shard_map/stage/pallas_call | solution.py:148
  5.7 5.3 %collective-permute-done.got_ref = bf16[768,128]{1,0:T(8,128)(2,1)S(1)} collective-permute-done((bf16[768,128]{1,0:T(8,128)(2,1)S(1)}, bf16[768,128]{1,0:T(8,128)(2,1)S(1)}, u32[]{:S(2)}, u32[]{:S(2)}) %collective-permute-start) | collective-permute-done | bytes 196640 | tf_op jit(solution)/shard_map/ppermute | solution.py:388
  11.0 0.0 collective-permute-start.1
  11.0 1.4 %collective-permute-done.1.swp_ref = bf16[768,128]{1,0:T(8,128)(2,1)S(1)} collective-permute-done((bf16[768,128]{1,0:T(8,128)(2,1)S(1)}, bf16[768,128]{1,0:T(8,128)(2,1)S(1)}, u32[]{:S(2)}, u32[]{:S(2)}) %collective-permute-start.1) | collective-permute-done | bytes 196640 | tf_op jit(solution)/shard_map/ppermute | solution.py:391
  12.4 1.5 %half.1 = (bf16[2,512,512]{2,1,0:T(8,128)(2,1)S(1)}, bf16[320,512]{1,0:T(8,128)(2,1)S(1)}, bf16[192,512]{1,0:T(8,128)(2,1)S(1)}, bf16[320,512]{1,0:T(8,128)(2,1)S(1)}, bf16[192,512]{1,0:T(8,128)(2,1)S(1)}) custom-call(s32[2,4]{1,0:T(2,128)S(4)} %get-tuple-element.27.cols_ref, f32[2,256]{1,0:T(2,128)S(1)} %get-tuple-element.28.factor_ref, ...), custom_call_target="tpu_custom_call" | custom-call | flops 1073741824 | bytes 8388608 | tf_op jit(solution)/shard_map/half/pallas_call | solution.py:233
  14.0 0.2 collective-permute-start.2
  14.2 0.0 collective-permute-start.5
  14.2 2.6 %collective-permute-start.6 = (bf16[320,512]{1,0:T(8,128)(2,1)S(1)}, bf16[320,512]{1,0:T(8,128)(2,1)S(1)}, u32[]{:S(2)}, u32[]{:S(2)}) collective-permute-start(bf16[320,512]{1,0:T(8,128)(2,1)S(1)} %get-tuple-element.36), channel_id=1, source_target_pairs={{0,64},{32,1},{64,128},{96,65},{128,192},{160,129},{192,0},{224,19... | collective-permute-start | bytes 983048 | tf_op jit(solution)/shard_map/ppermute | solution.py:388
  16.8 1.5 %collective-permute-start.3 = (bf16[192,512]{1,0:T(8,128)(2,1)S(1)}, bf16[192,512]{1,0:T(8,128)(2,1)S(1)}, u32[]{:S(2)}, u32[]{:S(2)}) collective-permute-start(bf16[192,512]{1,0:T(8,128)(2,1)S(1)} %get-tuple-element.33), channel_id=1, source_target_pairs={{0,32},{32,33},{64,96},{96,97},{128,160},{160,161},{192,224},{224,... | collective-permute-start | bytes 589832 | tf_op jit(solution)/shard_map/ppermute | solution.py:388
  18.3 1.2 %collective-permute-start.4 = (bf16[192,512]{1,0:T(8,128)(2,1)S(1)}, bf16[192,512]{1,0:T(8,128)(2,1)S(1)}, u32[]{:S(2)}, u32[]{:S(2)}) collective-permute-start(bf16[192,512]{1,0:T(8,128)(2,1)S(1)} %get-tuple-element.34), channel_id=1, source_target_pairs={{0,33},{32,96},{64,97},{96,160},{128,161},{160,224},{192,225},{224... | collective-permute-start | bytes 589832 | tf_op jit(solution)/shard_map/ppermute | solution.py:388
  19.5 7.3 %collective-permute-done.5.q1_ref = bf16[320,512]{1,0:T(8,128)(2,1)S(1)} collective-permute-done((bf16[320,512]{1,0:T(8,128)(2,1)S(1)}, bf16[320,512]{1,0:T(8,128)(2,1)S(1)}, u32[]{:S(2)}, u32[]{:S(2)}) %collective-permute-start.5) | collective-permute-done | bytes 327712 | tf_op jit(solution)/shard_map/ppermute | solution.py:388
  26.8 0.0 collective-permute-done.6.q3_ref
  26.8 0.0 collective-permute-done.2.s_ref
  26.8 0.5 %near.1.t_ref = f32[320,512]{1,0:T(8,128)S(1)} custom-call(bf16[2,512,512]{2,1,0:T(8,128)(2,1)S(1)} %get-tuple-element.32.x_ref, bf16[2,512,512]{2,1,0:T(8,128)(2,1)S(1)} %collective-permute-done.2.s_ref, bf16[320,512]{1,0:T(8,128)(2,1)S(1)} %collective-permute-done.5.q1_ref, bf16[320,512]{1,0:T(8,128)(2,1)S(1)} %collective-permute-done.6.q3_ref), custom_call_target="tpu_custom_call" | custom-call | flops 335544320 | bytes 2097152 | tf_op jit(solution)/shard_map/near/pallas_call | solution.py:289
  27.4 0.7 %own.1.o_ref = f32[256,512]{1,0:T(8,128)S(1)} custom-call(bf16[2,512,512]{2,1,0:T(8,128)(2,1)S(1)} %get-tuple-element.32.x_ref, bf16[2,512,512]{2,1,0:T(8,128)(2,1)S(1)} %collective-permute-done.2.s_ref), custom_call_target="tpu_custom_call" | custom-call | flops 536870912 | bytes 3145728 | tf_op jit(solution)/shard_map/own/pallas_call | solution.py:271
  28.1 0.3 collective-permute-done.3.q2_ref
  28.4 0.0 collective-permute-done.4.q4_ref
  28.4 0.7 %off.1 = (f32[192,512]{1,0:T(8,128)S(1)}, bf16[192,512]{1,0:T(8,128)(2,1)S(1)}, bf16[192,512]{1,0:T(8,128)(2,1)S(1)}, bf16[192,512]{1,0:T(8,128)(2,1)S(1)}) custom-call(bf16[2,512,512]{2,1,0:T(8,128)(2,1)S(1)} %get-tuple-element.32.x_ref, bf16[2,512,512]{2,1,0:T(8,128)(2,1)S(1)} %collective-permute-done.2.s_ref, ...), custom_call_target="tpu_custom_call" | custom-call | flops 201326592 | bytes 4194304 | tf_op jit(solution)/shard_map/off/pallas_call | solution.py:332
  29.1 3.3 %collective-permute-start.7 = (bf16[192,512]{1,0:T(8,128)(2,1)S(1)}, bf16[192,512]{1,0:T(8,128)(2,1)S(1)}, u32[]{:S(2)}, u32[]{:S(2)}) collective-permute-start(bf16[192,512]{1,0:T(8,128)(2,1)S(1)} %get-tuple-element.38), channel_id=1, source_target_pairs={{0,128},{32,160},{64,192},{96,224},{128,0},{160,32},{192,64},{224,... | collective-permute-start | bytes 589832 | tf_op jit(solution)/shard_map/ppermute | solution.py:395
  32.3 0.7 %collective-permute-start.8 = (bf16[192,512]{1,0:T(8,128)(2,1)S(1)}, bf16[192,512]{1,0:T(8,128)(2,1)S(1)}, u32[]{:S(2)}, u32[]{:S(2)}) collective-permute-start(bf16[192,512]{1,0:T(8,128)(2,1)S(1)} %get-tuple-element.39), channel_id=1, source_target_pairs={{0,64},{32,96},{64,128},{96,160},{128,192},{160,224},{192,0},{224,... | collective-permute-start | bytes 589832 | tf_op jit(solution)/shard_map/ppermute | solution.py:395
  33.0 2.6 %collective-permute-start.9 = (bf16[192,512]{1,0:T(8,128)(2,1)S(1)}, bf16[192,512]{1,0:T(8,128)(2,1)S(1)}, u32[]{:S(2)}, u32[]{:S(2)}) collective-permute-start(bf16[192,512]{1,0:T(8,128)(2,1)S(1)} %get-tuple-element.40), channel_id=1, source_target_pairs={{0,192},{32,224},{64,0},{96,32},{128,64},{160,96},{192,128},{224,1... | collective-permute-start | bytes 589832 | tf_op jit(solution)/shard_map/ppermute | solution.py:395
  35.6 1.8 %collective-permute-done.7.refs_1_ = bf16[192,512]{1,0:T(8,128)(2,1)S(1)} collective-permute-done((bf16[192,512]{1,0:T(8,128)(2,1)S(1)}, bf16[192,512]{1,0:T(8,128)(2,1)S(1)}, u32[]{:S(2)}, u32[]{:S(2)}) %collective-permute-start.7) | collective-permute-done | bytes 196640 | tf_op jit(solution)/shard_map/ppermute | solution.py:395
  37.4 5.0 %collective-permute-done.8.refs_2_ = bf16[192,512]{1,0:T(8,128)(2,1)S(1)} collective-permute-done((bf16[192,512]{1,0:T(8,128)(2,1)S(1)}, bf16[192,512]{1,0:T(8,128)(2,1)S(1)}, u32[]{:S(2)}, u32[]{:S(2)}) %collective-permute-start.8) | collective-permute-done | bytes 196640 | tf_op jit(solution)/shard_map/ppermute | solution.py:395
  42.4 0.0 collective-permute-done.9.refs_3_
  42.4 0.8 %sum.1 = f32[192,512]{1,0:T(8,128)} custom-call(f32[192,512]{1,0:T(8,128)S(1)} %get-tuple-element.37.refs_0_, bf16[192,512]{1,0:T(8,128)(2,1)S(1)} %collective-permute-done.7.refs_1_, bf16[192,512]{1,0:T(8,128)(2,1)S(1)} %collective-permute-done.8.refs_2_, bf16[192,512]{1,0:T(8,128)(2,1)S(1)} %collective-permute-done.9.refs_3_), custom_call_target="tpu_custom_call" | custom-call | flops 196608 | bytes 1048576 | tf_op jit(solution)/shard_map/sum/pallas_call | solution.py:356
Async XLA Ops:
  1.1 9.9 %collective-permute-start = (bf16[768,128]{1,0:T(8,128)(2,1)S(1)}, bf16[768,128]{1,0:T(8,128)(2,1)S(1)}, u32[]{:S(2)}, u32[]{:S(2)}) collective-permute-start(bf16[768,128]{1,0:T(8,128)(2,1)S(1)} %send.1), channel_id=1, source_target_pairs={{0,1},{32,0},{64,65},{96,64},{128,129},{160,128},{192,193},{224,19... | collective-permute-start | bytes 589832 | tf_op jit(solution)/shard_map/ppermute | solution.py:388
  11.0 1.4 %collective-permute-start.1 = (bf16[768,128]{1,0:T(8,128)(2,1)S(1)}, bf16[768,128]{1,0:T(8,128)(2,1)S(1)}, u32[]{:S(2)}, u32[]{:S(2)}) collective-permute-start(bf16[768,128]{1,0:T(8,128)(2,1)S(1)} %collective-permute-done.got_ref), channel_id=1, source_target_pairs={{0,32},{32,0},{64,96},{96,64},{128,160},{160,128},{192,224},{224,1... | collective-permute-start | bytes 589832 | tf_op jit(solution)/shard_map/ppermute | solution.py:391
  14.0 12.9 %collective-permute-start.2 = (bf16[2,512,512]{2,1,0:T(8,128)(2,1)S(1)}, bf16[2,512,512]{2,1,0:T(8,128)(2,1)S(1)}, u32[]{:S(2)}, u32[]{:S(2)}) collective-permute-start(bf16[2,512,512]{2,1,0:T(8,128)(2,1)S(1)} %get-tuple-element.32.x_ref), channel_id=1, source_target_pairs={{0,32},{32,0},{64,96},{96,64},{128,160},{160,128},{192,224},{224,1... | collective-permute-start | bytes 3145736 | tf_op jit(solution)/shard_map/ppermute | solution.py:391
  14.2 12.6 %collective-permute-start.5 = (bf16[320,512]{1,0:T(8,128)(2,1)S(1)}, bf16[320,512]{1,0:T(8,128)(2,1)S(1)}, u32[]{:S(2)}, u32[]{:S(2)}) collective-permute-start(bf16[320,512]{1,0:T(8,128)(2,1)S(1)} %get-tuple-element.35), channel_id=1, source_target_pairs={{0,1},{32,0},{64,65},{96,64},{128,129},{160,128},{192,193},{224,19... | collective-permute-start | bytes 983048 | tf_op jit(solution)/shard_map/ppermute | solution.py:388
  14.2 12.6 %collective-permute-start.6 = (bf16[320,512]{1,0:T(8,128)(2,1)S(1)}, bf16[320,512]{1,0:T(8,128)(2,1)S(1)}, u32[]{:S(2)}, u32[]{:S(2)}) collective-permute-start(bf16[320,512]{1,0:T(8,128)(2,1)S(1)} %get-tuple-element.36), channel_id=1, source_target_pairs={{0,64},{32,1},{64,128},{96,65},{128,192},{160,129},{192,0},{224,19... | collective-permute-start | bytes 983048 | tf_op jit(solution)/shard_map/ppermute | solution.py:388
  16.8 11.5 %collective-permute-start.3 = (bf16[192,512]{1,0:T(8,128)(2,1)S(1)}, bf16[192,512]{1,0:T(8,128)(2,1)S(1)}, u32[]{:S(2)}, u32[]{:S(2)}) collective-permute-start(bf16[192,512]{1,0:T(8,128)(2,1)S(1)} %get-tuple-element.33), channel_id=1, source_target_pairs={{0,32},{32,33},{64,96},{96,97},{128,160},{160,161},{192,224},{224,... | collective-permute-start | bytes 589832 | tf_op jit(solution)/shard_map/ppermute | solution.py:388
  18.3 10.1 %collective-permute-start.4 = (bf16[192,512]{1,0:T(8,128)(2,1)S(1)}, bf16[192,512]{1,0:T(8,128)(2,1)S(1)}, u32[]{:S(2)}, u32[]{:S(2)}) collective-permute-start(bf16[192,512]{1,0:T(8,128)(2,1)S(1)} %get-tuple-element.34), channel_id=1, source_target_pairs={{0,33},{32,96},{64,97},{96,160},{128,161},{160,224},{192,225},{224... | collective-permute-start | bytes 589832 | tf_op jit(solution)/shard_map/ppermute | solution.py:388
  29.1 8.3 %collective-permute-start.7 = (bf16[192,512]{1,0:T(8,128)(2,1)S(1)}, bf16[192,512]{1,0:T(8,128)(2,1)S(1)}, u32[]{:S(2)}, u32[]{:S(2)}) collective-permute-start(bf16[192,512]{1,0:T(8,128)(2,1)S(1)} %get-tuple-element.38), channel_id=1, source_target_pairs={{0,128},{32,160},{64,192},{96,224},{128,0},{160,32},{192,64},{224,... | collective-permute-start | bytes 589832 | tf_op jit(solution)/shard_map/ppermute | solution.py:395
  32.3 10.1 %collective-permute-start.8 = (bf16[192,512]{1,0:T(8,128)(2,1)S(1)}, bf16[192,512]{1,0:T(8,128)(2,1)S(1)}, u32[]{:S(2)}, u32[]{:S(2)}) collective-permute-start(bf16[192,512]{1,0:T(8,128)(2,1)S(1)} %get-tuple-element.39), channel_id=1, source_target_pairs={{0,64},{32,96},{64,128},{96,160},{128,192},{160,224},{192,0},{224,... | collective-permute-start | bytes 589832 | tf_op jit(solution)/shard_map/ppermute | solution.py:395
  33.0 9.4 %collective-permute-start.9 = (bf16[192,512]{1,0:T(8,128)(2,1)S(1)}, bf16[192,512]{1,0:T(8,128)(2,1)S(1)}, u32[]{:S(2)}, u32[]{:S(2)}) collective-permute-start(bf16[192,512]{1,0:T(8,128)(2,1)S(1)} %get-tuple-element.40), channel_id=1, source_target_pairs={{0,192},{32,224},{64,0},{96,32},{128,64},{160,96},{192,128},{224,1... | collective-permute-start | bytes 589832 | tf_op jit(solution)/shard_map/ppermute | solution.py:395

commit v5 on v4

--- a/solution.py
+++ b/solution.py
@@ -9,6 +9,7 @@
 
 BS = 256
 OB = 64
+SPLIT = 4
 GROUP = 2
 BF16 = jnp.bfloat16
 F32 = jnp.float32
@@ -40,13 +41,19 @@
     return jnp.concatenate([left[:, OB:], right[:, :OB]], axis=1)
 
 
-def load_groups(orb_ref, first, buf, sems):
+def load_groups(orb_ref, first, buf, sems, parts=1):
     last = orb_ref.shape[1] // 128 - 1
     copies = []
     for j in range(buf.shape[0]):
         group = jnp.clip(first + j, 0, last)
         lanes = pl.ds(pl.multiple_of(group * 128, 128), 128)
-        copies.append(pltpu.make_async_copy(orb_ref.at[:, lanes], buf.at[j], sems.at[j]))
+        for part in range(parts):
+            rows = pl.ds(part * (buf.shape[1] // parts), buf.shape[1] // parts)
+            copies.append(
+                pltpu.make_async_copy(
+                    orb_ref.at[rows, lanes], buf.at[j, rows], sems.at[j * parts + part]
+                )
+            )
     return copies
 
 
@@ -54,7 +61,7 @@
     d = lax.axis_index("row")
     core = lax.axis_index("aux") % 2
     odd = d % 2
-    copies = load_groups(orb_ref, (d - 2 - odd) // 2 + 1 - core, buf, sems)
+    copies = load_groups(orb_ref, (d - 2 - odd) // 2 + 1 - core, buf, sems, SPLIT)
     for copy in copies:
         copy.start()
     for copy in copies:
@@ -83,7 +90,7 @@
         out_shape=pltpu.VMEM((rows + rows // 2, 128), BF16),
         in_specs=[ANY],
         out_specs=VMEM,
-        scratch_shapes=[pltpu.VMEM((2, rows, 128), BF16), pltpu.SemaphoreType.DMA((2,))],
+        scratch_shapes=[pltpu.VMEM((2, rows, 128), BF16), pltpu.SemaphoreType.DMA((2 * SPLIT,))],
     )(in_hbm(orbitals))
 
 
@@ -279,90 +286,112 @@
     )(*on_chip(x, s))
 
 
-def near_kernel(last, x_ref, s_ref, q1_ref, q3_ref, t_ref):
-    d, core = lax.axis_index("row"), lax.axis_index("aux") % 2
+def place():
+    a = lax.axis_index("aux")
+    return a // 2, a % 2, jnp.where(a % 2 == 0, 3, 0)
+
+
+def near_kernel(last, x_ref, s_ref, q1_ref, q3_ref, o_ref, chunks, send_ref):
+    d = lax.axis_index("row")
+    y, core, _ = place()
     t = nt(q1_ref[...], x_ref[0]) + nt(q3_ref[...], s_ref[1])
-    t_ref[...] = jnp.where(d == jnp.where(core == 0, 0, last), 0.0, t)
-
-
-def near_part(last, x, s, q1, q3):
+    t = jnp.where(d == jnp.where(core == 0, 0, last), 0.0, t)
+
+    @pl.when(core == 0)
+    def _():
+        chunks[0] = t[:192]
+        chunks[1, :128] = t[192:]
+        chunks[1, 128:] = o_ref[:64]
+        chunks[2] = o_ref[64:]
+        chunks[3] = jnp.zeros(chunks.shape[1:], F32)
+
+    @pl.when(core == 1)
+    def _():
+        chunks[0] = jnp.zeros(chunks.shape[1:], F32)
+        chunks[1] = o_ref[:192]
+        chunks[2, :64] = o_ref[192:]
+        chunks[2, 64:] = t[:128]
+        chunks[3] = t[128:]
+
+    send_ref[...] = chunks[y ^ 2].astype(BF16)
+
+
+def near_part(last, x, s, q1, q3, own):
     return pl.pallas_call(
         functools.partial(near_kernel, last),
         name="near",
         cost_estimate=cost(320 * 512 * 1024, 2 * 2**20),
-        compiler_params=room(4),
-        out_shape=pltpu.VMEM((320, x.shape[1]), F32),
-        in_specs=[VMEM] * 4,
-        out_specs=VMEM,
-    )(*on_chip(x, s, q1, q3))
-
-
-def off_kernel(
-    last, x_ref, s_ref, q2_ref, q4_ref, o_ref, t_ref, keep_ref, s1_ref, s2_ref, s3_ref, chunks,
-):
-    a = lax.axis_index("aux")
-    core, y = a % 2, a // 2
+        compiler_params=room(6),
+        out_shape=[pltpu.VMEM((4, 192, x.shape[1]), F32), pltpu.VMEM((192, x.shape[1]), BF16)],
+        in_specs=[VMEM] * 5,
+        out_specs=[VMEM] * 2,
+    )(*on_chip(x, s, q1, q3, own))
+
+
+def off_kernel(last, x_ref, s_ref, q2_ref, q4_ref, chunks, keep_ref, s1_ref, s3_ref, far_ref):
     d = lax.axis_index("row")
+    y, core, far = place()
     u = nt(q2_ref[...], x_ref[1]) + nt(q4_ref[...], s_ref[0])
     u = jnp.where(d == jnp.where(core == 0, last, 0), 0.0, u)
-
-    @pl.when(core == 0)
-    def _():
-        chunks[0] = t_ref[:192]
-        chunks[1, :128] = t_ref[192:]
-        chunks[1, 128:] = o_ref[:64]
-        chunks[2] = o_ref[64:]
-        chunks[3] = u
-
-    @pl.when(core == 1)
-    def _():
-        chunks[0] = u
-        chunks[1] = o_ref[:192]
-        chunks[2, :64] = o_ref[192:]
-        chunks[2, 64:] = t_ref[:128]
-        chunks[3] = t_ref[128:]
-
-    keep_ref[...] = chunks[y]
-    for step, ref in enumerate((s1_ref, s2_ref, s3_ref)):
-        ref[...] = chunks[(y + step + 1) % 4].astype(BF16)
-
-
-def off_part(last, x, s, q2, q4, own, near):
+    keep_ref[...] = jnp.where(y == far, u, chunks[y])
+    s1_ref[...] = jnp.where(y ^ 1 == far, u, chunks[y ^ 1]).astype(BF16)
+    s3_ref[...] = jnp.where(y ^ 3 == far, u, chunks[y ^ 3]).astype(BF16)
+    far_ref[...] = u.astype(BF16)
+
+
+def off_part(last, x, s, q2, q4, near):
     shape = (192, x.shape[1])
     return pl.pallas_call(
         functools.partial(off_kernel, last),
         name="off",
         cost_estimate=cost(192 * 512 * 1024, 4 * 2**20),
-        compiler_params=room(8),
+        compiler_params=room(4),
         out_shape=[pltpu.VMEM(shape, F32)] + [pltpu.VMEM(shape, BF16)] * 3,
-        in_specs=[VMEM] * 6,
+        in_specs=[VMEM] * 5,
         out_specs=[VMEM] * 4,
-        scratch_shapes=[pltpu.VMEM((4,) + shape, F32)],
-    )(*on_chip(x, s, q2, q4, own, near))
-
-
-def sum_kernel(scale, *refs):
-    rows = refs[-1].shape[0]
-    at = pl.ds(pl.multiple_of(pl.program_id(0) * rows, rows), rows)
-    total = refs[0][at]
-    for ref in refs[1:-1]:
-        total = total + ref[at].astype(F32)
-    refs[-1][...] = total * scale
-
-
-def sum_parts(scale, parts):
-    rows, columns = parts[0].shape
-    steps = 1
+    )(*on_chip(x, s, q2, q4, near))
+
+
+def add_kernel(at_far, keep_ref, part_ref, out_ref):
+    y, _, far = place()
+    out_ref[...] = keep_ref[...] + jnp.where((y == far) == at_far, part_ref[...].astype(F32), 0.0)
+
+
+def add(name, at_far, kept, part):
+    return pl.pallas_call(
+        functools.partial(add_kernel, at_far),
+        name=name,
+        cost_estimate=cost(192 * 512, 2**20),
+        compiler_params=room(4),
+        out_shape=pltpu.VMEM(kept.shape, F32),
+        in_specs=[VMEM] * 2,
+        out_specs=VMEM,
+    )(*on_chip(kept, part))
+
+
+def sum_kernel(scale, keep_ref, s1_ref, s3_ref, out_ref):
+    total = keep_ref[...] + s1_ref[...].astype(F32) + s3_ref[...].astype(F32)
+    out_ref[...] = total * scale
+
+
+def sum_parts(scale, *parts):
     return pl.pallas_call(
         functools.partial(sum_kernel, scale),
         name="sum",
         cost_estimate=cost(192 * 512, 2**20),
         compiler_params=room(4),
-        grid=(steps,),
-        out_shape=jax.ShapeDtypeStruct((rows, columns), F32),
-        in_specs=[VMEM] * 4,
-        out_specs=pl.BlockSpec((rows // steps, columns), lambda i: (i, 0)),
+        out_shape=jax.ShapeDtypeStruct(parts[0].shape, F32),
+        in_specs=[VMEM] * len(parts),
+        out_specs=VMEM,
     )(*on_chip(*parts))
+
+
+ACROSS = {(y, c): (y ^ 2, c) for y in range(4) for c in range(2)}
+FIRST = {**ACROSS, (1, 0): (0, 1), (2, 1): (3, 0)}
+FINAL = {
+    (1, 0): (3, 0), (2, 1): (0, 1), (0, 0): (1, 1), (3, 1): (2, 0),
+    (0, 1): (0, 0), (1, 1): (1, 0), (2, 0): (2, 1), (3, 0): (3, 1),
+}
 
 
 def row_moves(rows, chips, core_0_up, cross):
@@ -390,26 +419,33 @@
     def swap(value):
         return lax.ppermute(value, "aux", [(i, i ^ 1) for i in range(aux_devices)])
 
-    def along_y(value, step):
-        route = [(i, (i + 2 * step) % aux_devices) for i in range(aux_devices)]
-        return lax.ppermute(value, "aux", route)
+    def along_y(value, route):
+        pairs = [(2 * y + c, 2 * end[0] + end[1]) for (y, c), end in sorted(route.items())]
+        return lax.ppermute(value, "aux", pairs)
+
+    def exchange(value, step):
+        return along_y(value, {(y, c): (y ^ step, c) for y in range(chips) for c in range(2)})
 
     send = halo_to_send(orbitals)
     got = move(send, True, False)
-    own, near, factors, columns = stage(block_columns, occ_mask.T, orbitals, integrals)
-    got, own, near, factors, columns = lax.optimization_barrier((got, own, near, factors, columns))
+    own, staged, factors, columns = stage(block_columns, occ_mask.T, orbitals, integrals)
+    got, own, staged, factors, columns = lax.optimization_barrier(
+        (got, own, staged, factors, columns)
+    )
     swapped = swap(got)
-    x, q1, q2, q3, q4 = half_transform(columns, factors, near, own, got, swapped)
+    x, q1, q2, q3, q4 = half_transform(columns, factors, staged, own, got, swapped)
     r1 = move(q1, True, False)
     r3 = move(q3, False, True)
     others = swap(x)
     r2 = move(q2, False, False)
     r4 = move(q4, True, True)
     o = own_part(x, others)
-    t = near_part(rows - 1, x, others, r1, r3)
-    kept, *sent = off_part(rows - 1, x, others, r2, r4, o, t)
-    parts = [kept] + [along_y(sent[step - 1], step) for step in (2, 1, 3)]
-    return sum_parts(scale, parts).T
+    near, first = near_part(rows - 1, x, others, r1, r3, o)
+    first = along_y(first, FIRST)
+    kept, s1, s3, far = off_part(rows - 1, x, others, r2, r4, near)
+    kept = add("first", False, kept, first)
+    kept = add("far", True, kept, along_y(far, FINAL))
+    return sum_parts(scale, kept, exchange(s1, 1), exchange(s3, 3)).T
 
 
 def solution(mesh):

time: 43.9 us -> 43.6 us (level); the launches traced: 43.2 us -> 43.5 us
    ppermute x5, waiting for transfers between devices: 12.9 us -> 11.9 us  [move(): lax.ppermute(value, ('aux', 'row'), row_moves(rows, chips, core_0_up, cro...]
    ppermute x3 -> x4, waiting for transfers between devices: 6.82 us -> 7.82 us  [along_y(): return lax.ppermute(value, 'aux', pairs)]
    ppermute x3 -> x4, starting transfers between devices: 6.52 us -> 6.74 us  [along_y(): return lax.ppermute(value, 'aux', pairs)]
  transfers between devices with their start and end apart: 10 -> 11, of which waited for: 6 -> 7; matrix products, arithmetic and copies ran while one was open for 0% -> 0% of each run, Pallas kernels for 9% -> 10%
where the time goes in v5:
time: 43.6 us; the launch traced here: 43.5 us
  waiting for transfers between devices  21.1 us (48%)
  starting transfers between devices  14.4 us (33%)
  Pallas kernels  7.87 us (18%)
    ppermute x5, waiting for transfers between devices, move(): lax.ppermute(value, ('aux', 'row'), row_moves(rows, chips, core_0_up, cro...  11.9 us
    ppermute x4, waiting for transfers between devices, along_y(): return lax.ppermute(value, 'aux', pairs)  7.82 us
    ppermute x5, starting transfers between devices, move(): lax.ppermute(value, ('aux', 'row'), row_moves(rows, chips, core_0_up, cro...  7.42 us
    ppermute x4, starting transfers between devices, along_y(): return lax.ppermute(value, 'aux', pairs)  6.74 us
    pallas_call x1, Pallas kernels, stage(): pl.pallas_call(stage_kernel, name='stage', cost_estimate=cost(512 * 1024,...  2.51 us
    pallas_call x1, Pallas kernels, half_transform(): pl.pallas_call(half_kernel, name='half', cost_estimate=cost(512 * 1024 *...  1.51 us
    ppermute x2, waiting for transfers between devices, swap(): return lax.ppermute(value, 'aux', [(i, i ^ 1) for i in range(aux_devices)])  1.44 us
    pallas_call x1, Pallas kernels, halo_to_send(): pl.pallas_call(send_kernel, name='send', cost_estimate=cost(512 * 1024, 2...  1.03 us
  transfers between devices with their start and end apart: 11, of which 7 were waited for; matrix products, arithmetic and copies ran while one was open for 0% of the time, Pallas kernels for 10%

profile of v5, /device:TPU:6, one launch (start us, length us, event | category | flops | bytes accessed | tf_op | source)
XLA Modules:
  0.0 43.5 jit_solution(11905707223105963424)
XLA Ops:
  0.0 1.0 %send.1 = bf16[768,128]{1,0:T(8,128)(2,1)S(1)} custom-call(bf16[512,2048]{1,0:T(8,128)(2,1)} %orb_ref.3), custom_call_target="tpu_custom_call" | custom-call | flops 1048576 | bytes 1048576 | tf_op jit(solution)/shard_map/send/pallas_call | solution.py:85
  1.0 2.1 %collective-permute-start = (bf16[768,128]{1,0:T(8,128)(2,1)S(1)}, bf16[768,128]{1,0:T(8,128)(2,1)S(1)}, u32[]{:S(2)}, u32[]{:S(2)}) collective-permute-start(bf16[768,128]{1,0:T(8,128)(2,1)S(1)} %send.1), channel_id=1, source_target_pairs={{0,1},{32,0},{64,65},{96,64},{128,129},{160,128},{192,193},{224,19... | collective-permute-start | bytes 589832 | tf_op jit(solution)/shard_map/ppermute | solution.py:417
  3.1 2.5 %stage.1 = (bf16[512,256]{1,0:T(8,128)(2,1)S(1)}, bf16[4,2,4,256,256]{4,3,2,1,0:T(8,128)(2,1)S(1)}, f32[2,256]{1,0:T(2,128)S(1)}, s32[2,4]{1,0:T(2,128)S(4)}) custom-call(s32[2,4]{1,0:T(2,128)} %cols_hbm.1, s32[32,64]{1,0:T(8,128)} %bitcast.2, bf16[512,2048]{1,0:T(8,128)(2,1)} %orb_ref.3, bf16[4,2,4,256,256]{4,3,2,1,0:T(8,128)(2,1)} %int_ref.1), custom_call_target="tpu_custom_call" | custom-call | flops 1048576 | bytes 9437184 | tf_op jit(solution)/shard_map/stage/pallas_call | solution.py:155
  5.6 5.3 %collective-permute-done.got_ref = bf16[768,128]{1,0:T(8,128)(2,1)S(1)} collective-permute-done((bf16[768,128]{1,0:T(8,128)(2,1)S(1)}, bf16[768,128]{1,0:T(8,128)(2,1)S(1)}, u32[]{:S(2)}, u32[]{:S(2)}) %collective-permute-start) | collective-permute-done | bytes 196640 | tf_op jit(solution)/shard_map/ppermute | solution.py:417
  11.0 0.0 collective-permute-start.1
  11.0 1.4 %collective-permute-done.1.swp_ref = bf16[768,128]{1,0:T(8,128)(2,1)S(1)} collective-permute-done((bf16[768,128]{1,0:T(8,128)(2,1)S(1)}, bf16[768,128]{1,0:T(8,128)(2,1)S(1)}, u32[]{:S(2)}, u32[]{:S(2)}) %collective-permute-start.1) | collective-permute-done | bytes 196640 | tf_op jit(solution)/shard_map/ppermute | solution.py:420
  12.4 1.5 %half.1 = (bf16[2,512,512]{2,1,0:T(8,128)(2,1)S(1)}, bf16[320,512]{1,0:T(8,128)(2,1)S(1)}, bf16[192,512]{1,0:T(8,128)(2,1)S(1)}, bf16[320,512]{1,0:T(8,128)(2,1)S(1)}, bf16[192,512]{1,0:T(8,128)(2,1)S(1)}) custom-call(s32[2,4]{1,0:T(2,128)S(4)} %get-tuple-element.29.cols_ref, f32[2,256]{1,0:T(2,128)S(1)} %get-tuple-element.30.factor_ref, ...), custom_call_target="tpu_custom_call" | custom-call | flops 1073741824 | bytes 8388608 | tf_op jit(solution)/shard_map/half/pallas_call | solution.py:240
  13.9 0.2 collective-permute-start.2
  14.1 0.0 collective-permute-start.5
  14.1 2.6 %collective-permute-start.6 = (bf16[320,512]{1,0:T(8,128)(2,1)S(1)}, bf16[320,512]{1,0:T(8,128)(2,1)S(1)}, u32[]{:S(2)}, u32[]{:S(2)}) collective-permute-start(bf16[320,512]{1,0:T(8,128)(2,1)S(1)} %get-tuple-element.38), channel_id=1, source_target_pairs={{0,64},{32,1},{64,128},{96,65},{128,192},{160,129},{192,0},{224,19... | collective-permute-start | bytes 983048 | tf_op jit(solution)/shard_map/ppermute | solution.py:417
  16.8 1.5 %collective-permute-start.3 = (bf16[192,512]{1,0:T(8,128)(2,1)S(1)}, bf16[192,512]{1,0:T(8,128)(2,1)S(1)}, u32[]{:S(2)}, u32[]{:S(2)}) collective-permute-start(bf16[192,512]{1,0:T(8,128)(2,1)S(1)} %get-tuple-element.35), channel_id=1, source_target_pairs={{0,32},{32,33},{64,96},{96,97},{128,160},{160,161},{192,224},{224,... | collective-permute-start | bytes 589832 | tf_op jit(solution)/shard_map/ppermute | solution.py:417
  18.3 1.2 %collective-permute-start.4 = (bf16[192,512]{1,0:T(8,128)(2,1)S(1)}, bf16[192,512]{1,0:T(8,128)(2,1)S(1)}, u32[]{:S(2)}, u32[]{:S(2)}) collective-permute-start(bf16[192,512]{1,0:T(8,128)(2,1)S(1)} %get-tuple-element.36), channel_id=1, source_target_pairs={{0,33},{32,96},{64,97},{96,160},{128,161},{160,224},{192,225},{224... | collective-permute-start | bytes 589832 | tf_op jit(solution)/shard_map/ppermute | solution.py:417
  19.5 0.0 collective-permute-done.2.s_ref
  19.5 0.7 %own.1.o_ref = f32[256,512]{1,0:T(8,128)S(1)} custom-call(bf16[2,512,512]{2,1,0:T(8,128)(2,1)S(1)} %get-tuple-element.34.x_ref, bf16[2,512,512]{2,1,0:T(8,128)(2,1)S(1)} %collective-permute-done.2.s_ref), custom_call_target="tpu_custom_call" | custom-call | flops 536870912 | bytes 3145728 | tf_op jit(solution)/shard_map/own/pallas_call | solution.py:278
  20.2 6.5 %collective-permute-done.5.q1_ref = bf16[320,512]{1,0:T(8,128)(2,1)S(1)} collective-permute-done((bf16[320,512]{1,0:T(8,128)(2,1)S(1)}, bf16[320,512]{1,0:T(8,128)(2,1)S(1)}, u32[]{:S(2)}, u32[]{:S(2)}) %collective-permute-start.5) | collective-permute-done | bytes 327712 | tf_op jit(solution)/shard_map/ppermute | solution.py:417
  26.8 0.0 collective-permute-done.6.q3_ref
  26.8 0.7 %near.1 = (f32[4,192,512]{2,1,0:T(8,128)S(1)}, bf16[192,512]{1,0:T(8,128)(2,1)S(1)}) custom-call(bf16[2,512,512]{2,1,0:T(8,128)(2,1)S(1)} %get-tuple-element.34.x_ref, bf16[2,512,512]{2,1,0:T(8,128)(2,1)S(1)} %collective-permute-done.2.s_ref, bf16[320,512]{1,0:T(8,128)(2,1)S(1)} %collective-permute-done.5.q1_ref, ...), custom_call_target="tpu_custom_call" | custom-call | flops 335544320 | bytes 2097152 | tf_op jit(solution)/shard_map/near/pallas_call | solution.py:320
  27.4 3.3 %collective-permute-start.7 = (bf16[192,512]{1,0:T(8,128)(2,1)S(1)}, bf16[192,512]{1,0:T(8,128)(2,1)S(1)}, u32[]{:S(2)}, u32[]{:S(2)}) collective-permute-start(bf16[192,512]{1,0:T(8,128)(2,1)S(1)} %get-tuple-element.41), channel_id=1, source_target_pairs={{0,128},{32,160},{64,32},{96,224},{128,0},{160,192},{192,64},{224,... | collective-permute-start | bytes 589832 | tf_op jit(solution)/shard_map/ppermute | solution.py:424
  30.7 0.0 collective-permute-done.3.q2_ref
  30.7 0.0 collective-permute-done.4.q4_ref
  30.7 0.5 %off.1 = (f32[192,512]{1,0:T(8,128)S(1)}, bf16[192,512]{1,0:T(8,128)(2,1)S(1)}, bf16[192,512]{1,0:T(8,128)(2,1)S(1)}, bf16[192,512]{1,0:T(8,128)(2,1)S(1)}) custom-call(bf16[2,512,512]{2,1,0:T(8,128)(2,1)S(1)} %get-tuple-element.34.x_ref, bf16[2,512,512]{2,1,0:T(8,128)(2,1)S(1)} %collective-permute-done.2.s_ref, ...), custom_call_target="tpu_custom_call" | custom-call | flops 201326592 | bytes 4194304 | tf_op jit(solution)/shard_map/off/pallas_call | solution.py:344
  31.2 0.9 %collective-permute-start.8 = (bf16[192,512]{1,0:T(8,128)(2,1)S(1)}, bf16[192,512]{1,0:T(8,128)(2,1)S(1)}, u32[]{:S(2)}, u32[]{:S(2)}) collective-permute-start(bf16[192,512]{1,0:T(8,128)(2,1)S(1)} %get-tuple-element.42), channel_id=1, source_target_pairs={{0,96},{32,0},{64,192},{96,64},{128,160},{160,32},{192,224},{224,1... | collective-permute-start | bytes 589832 | tf_op jit(solution)/shard_map/ppermute | solution.py:424
  32.1 1.1 %collective-permute-start.9 = (bf16[192,512]{1,0:T(8,128)(2,1)S(1)}, bf16[192,512]{1,0:T(8,128)(2,1)S(1)}, u32[]{:S(2)}, u32[]{:S(2)}) collective-permute-start(bf16[192,512]{1,0:T(8,128)(2,1)S(1)} %get-tuple-element.43), channel_id=1, source_target_pairs={{0,64},{32,96},{64,0},{96,32},{128,192},{160,224},{192,128},{224,1... | collective-permute-start | bytes 589832 | tf_op jit(solution)/shard_map/ppermute | solution.py:424
  33.2 1.5 %collective-permute-start.10 = (bf16[192,512]{1,0:T(8,128)(2,1)S(1)}, bf16[192,512]{1,0:T(8,128)(2,1)S(1)}, u32[]{:S(2)}, u32[]{:S(2)}) collective-permute-start(bf16[192,512]{1,0:T(8,128)(2,1)S(1)} %get-tuple-element.44), channel_id=1, source_target_pairs={{0,192},{32,224},{64,128},{96,160},{128,64},{160,96},{192,0},{224,... | collective-permute-start | bytes 589832 | tf_op jit(solution)/shard_map/ppermute | solution.py:424
  34.7 1.8 %collective-permute-done.7.part_ref = bf16[192,512]{1,0:T(8,128)(2,1)S(1)} collective-permute-done((bf16[192,512]{1,0:T(8,128)(2,1)S(1)}, bf16[192,512]{1,0:T(8,128)(2,1)S(1)}, u32[]{:S(2)}, u32[]{:S(2)}) %collective-permute-start.7) | collective-permute-done | bytes 196640 | tf_op jit(solution)/shard_map/ppermute | solution.py:424
  36.5 0.1 first.1.keep_ref
  36.6 2.3 %collective-permute-done.8.part_ref = bf16[192,512]{1,0:T(8,128)(2,1)S(1)} collective-permute-done((bf16[192,512]{1,0:T(8,128)(2,1)S(1)}, bf16[192,512]{1,0:T(8,128)(2,1)S(1)}, u32[]{:S(2)}, u32[]{:S(2)}) %collective-permute-start.8) | collective-permute-done | bytes 196640 | tf_op jit(solution)/shard_map/ppermute | solution.py:424
  38.8 0.1 far.1.keep_ref
  38.9 2.3 %collective-permute-done.9.s1_ref = bf16[192,512]{1,0:T(8,128)(2,1)S(1)} collective-permute-done((bf16[192,512]{1,0:T(8,128)(2,1)S(1)}, bf16[192,512]{1,0:T(8,128)(2,1)S(1)}, u32[]{:S(2)}, u32[]{:S(2)}) %collective-permute-start.9) | collective-permute-done | bytes 196640 | tf_op jit(solution)/shard_map/ppermute | solution.py:424
  41.2 1.5 %collective-permute-done.10.s3_ref = bf16[192,512]{1,0:T(8,128)(2,1)S(1)} collective-permute-done((bf16[192,512]{1,0:T(8,128)(2,1)S(1)}, bf16[192,512]{1,0:T(8,128)(2,1)S(1)}, u32[]{:S(2)}, u32[]{:S(2)}) %collective-permute-start.10) | collective-permute-done | bytes 196640 | tf_op jit(solution)/shard_map/ppermute | solution.py:424
  42.7 0.8 %sum.1 = f32[192,512]{1,0:T(8,128)} custom-call(f32[192,512]{1,0:T(8,128)S(1)} %far.1.keep_ref, bf16[192,512]{1,0:T(8,128)(2,1)S(1)} %collective-permute-done.9.s1_ref, bf16[192,512]{1,0:T(8,128)(2,1)S(1)} %collective-permute-done.10.s3_ref), custom_call_target="tpu_custom_call" | custom-call | flops 196608 | bytes 1048576 | tf_op jit(solution)/shard_map/sum/pallas_call | solution.py:378
Async XLA Ops:
  1.0 9.9 %collective-permute-start = (bf16[768,128]{1,0:T(8,128)(2,1)S(1)}, bf16[768,128]{1,0:T(8,128)(2,1)S(1)}, u32[]{:S(2)}, u32[]{:S(2)}) collective-permute-start(bf16[768,128]{1,0:T(8,128)(2,1)S(1)} %send.1), channel_id=1, source_target_pairs={{0,1},{32,0},{64,65},{96,64},{128,129},{160,128},{192,193},{224,19... | collective-permute-start | bytes 589832 | tf_op jit(solution)/shard_map/ppermute | solution.py:417
  11.0 1.4 %collective-permute-start.1 = (bf16[768,128]{1,0:T(8,128)(2,1)S(1)}, bf16[768,128]{1,0:T(8,128)(2,1)S(1)}, u32[]{:S(2)}, u32[]{:S(2)}) collective-permute-start(bf16[768,128]{1,0:T(8,128)(2,1)S(1)} %collective-permute-done.got_ref), channel_id=1, source_target_pairs={{0,32},{32,0},{64,96},{96,64},{128,160},{160,128},{192,224},{224,1... | collective-permute-start | bytes 589832 | tf_op jit(solution)/shard_map/ppermute | solution.py:420
  13.9 5.6 %collective-permute-start.2 = (bf16[2,512,512]{2,1,0:T(8,128)(2,1)S(1)}, bf16[2,512,512]{2,1,0:T(8,128)(2,1)S(1)}, u32[]{:S(2)}, u32[]{:S(2)}) collective-permute-start(bf16[2,512,512]{2,1,0:T(8,128)(2,1)S(1)} %get-tuple-element.34.x_ref), channel_id=1, source_target_pairs={{0,32},{32,0},{64,96},{96,64},{128,160},{160,128},{192,224},{224,1... | collective-permute-start | bytes 3145736 | tf_op jit(solution)/shard_map/ppermute | solution.py:420
  14.1 12.6 %collective-permute-start.5 = (bf16[320,512]{1,0:T(8,128)(2,1)S(1)}, bf16[320,512]{1,0:T(8,128)(2,1)S(1)}, u32[]{:S(2)}, u32[]{:S(2)}) collective-permute-start(bf16[320,512]{1,0:T(8,128)(2,1)S(1)} %get-tuple-element.37), channel_id=1, source_target_pairs={{0,1},{32,0},{64,65},{96,64},{128,129},{160,128},{192,193},{224,19... | collective-permute-start | bytes 983048 | tf_op jit(solution)/shard_map/ppermute | solution.py:417
  14.1 12.6 %collective-permute-start.6 = (bf16[320,512]{1,0:T(8,128)(2,1)S(1)}, bf16[320,512]{1,0:T(8,128)(2,1)S(1)}, u32[]{:S(2)}, u32[]{:S(2)}) collective-permute-start(bf16[320,512]{1,0:T(8,128)(2,1)S(1)} %get-tuple-element.38), channel_id=1, source_target_pairs={{0,64},{32,1},{64,128},{96,65},{128,192},{160,129},{192,0},{224,19... | collective-permute-start | bytes 983048 | tf_op jit(solution)/shard_map/ppermute | solution.py:417
  16.8 13.9 %collective-permute-start.3 = (bf16[192,512]{1,0:T(8,128)(2,1)S(1)}, bf16[192,512]{1,0:T(8,128)(2,1)S(1)}, u32[]{:S(2)}, u32[]{:S(2)}) collective-permute-start(bf16[192,512]{1,0:T(8,128)(2,1)S(1)} %get-tuple-element.35), channel_id=1, source_target_pairs={{0,32},{32,33},{64,96},{96,97},{128,160},{160,161},{192,224},{224,... | collective-permute-start | bytes 589832 | tf_op jit(solution)/shard_map/ppermute | solution.py:417
  18.3 12.4 %collective-permute-start.4 = (bf16[192,512]{1,0:T(8,128)(2,1)S(1)}, bf16[192,512]{1,0:T(8,128)(2,1)S(1)}, u32[]{:S(2)}, u32[]{:S(2)}) collective-permute-start(bf16[192,512]{1,0:T(8,128)(2,1)S(1)} %get-tuple-element.36), channel_id=1, source_target_pairs={{0,33},{32,96},{64,97},{96,160},{128,161},{160,224},{192,225},{224... | collective-permute-start | bytes 589832 | tf_op jit(solution)/shard_map/ppermute | solution.py:417
  27.4 9.1 %collective-permute-start.7 = (bf16[192,512]{1,0:T(8,128)(2,1)S(1)}, bf16[192,512]{1,0:T(8,128)(2,1)S(1)}, u32[]{:S(2)}, u32[]{:S(2)}) collective-permute-start(bf16[192,512]{1,0:T(8,128)(2,1)S(1)} %get-tuple-element.41), channel_id=1, source_target_pairs={{0,128},{32,160},{64,32},{96,224},{128,0},{160,192},{192,64},{224,... | collective-permute-start | bytes 589832 | tf_op jit(solution)/shard_map/ppermute | solution.py:424
  31.2 7.6 %collective-permute-start.8 = (bf16[192,512]{1,0:T(8,128)(2,1)S(1)}, bf16[192,512]{1,0:T(8,128)(2,1)S(1)}, u32[]{:S(2)}, u32[]{:S(2)}) collective-permute-start(bf16[192,512]{1,0:T(8,128)(2,1)S(1)} %get-tuple-element.42), channel_id=1, source_target_pairs={{0,96},{32,0},{64,192},{96,64},{128,160},{160,32},{192,224},{224,1... | collective-permute-start | bytes 589832 | tf_op jit(solution)/shard_map/ppermute | solution.py:424
  32.1 9.0 %collective-permute-start.9 = (bf16[192,512]{1,0:T(8,128)(2,1)S(1)}, bf16[192,512]{1,0:T(8,128)(2,1)S(1)}, u32[]{:S(2)}, u32[]{:S(2)}) collective-permute-start(bf16[192,512]{1,0:T(8,128)(2,1)S(1)} %get-tuple-element.43), channel_id=1, source_target_pairs={{0,64},{32,96},{64,0},{96,32},{128,192},{160,224},{192,128},{224,1... | collective-permute-start | bytes 589832 | tf_op jit(solution)/shard_map/ppermute | solution.py:424
  33.2 9.4 %collective-permute-start.10 = (bf16[192,512]{1,0:T(8,128)(2,1)S(1)}, bf16[192,512]{1,0:T(8,128)(2,1)S(1)}, u32[]{:S(2)}, u32[]{:S(2)}) collective-permute-start(bf16[192,512]{1,0:T(8,128)(2,1)S(1)} %get-tuple-element.44), channel_id=1, source_target_pairs={{0,192},{32,224},{64,128},{96,160},{128,64},{160,96},{192,0},{224,... | collective-permute-start | bytes 589832 | tf_op jit(solution)/shard_map/ppermute | solution.py:424

commit v6 on v5

--- a/solution.py
+++ b/solution.py
@@ -291,7 +291,7 @@
     return a // 2, a % 2, jnp.where(a % 2 == 0, 3, 0)
 
 
-def near_kernel(last, x_ref, s_ref, q1_ref, q3_ref, o_ref, chunks, send_ref):
+def near_kernel(last, x_ref, s_ref, q3_ref, q1_ref, o_ref, chunks, send_ref):
     d = lax.axis_index("row")
     y, core, _ = place()
     t = nt(q1_ref[...], x_ref[0]) + nt(q3_ref[...], s_ref[1])
@@ -316,7 +316,7 @@
     send_ref[...] = chunks[y ^ 2].astype(BF16)
 
 
-def near_part(last, x, s, q1, q3, own):
+def near_part(last, x, s, q3, q1, own):
     return pl.pallas_call(
         functools.partial(near_kernel, last),
         name="near",
@@ -325,10 +325,10 @@
         out_shape=[pltpu.VMEM((4, 192, x.shape[1]), F32), pltpu.VMEM((192, x.shape[1]), BF16)],
         in_specs=[VMEM] * 5,
         out_specs=[VMEM] * 2,
-    )(*on_chip(x, s, q1, q3, own))
-
-
-def off_kernel(last, x_ref, s_ref, q2_ref, q4_ref, chunks, keep_ref, s1_ref, s3_ref, far_ref):
+    )(*on_chip(x, s, q3, q1, own))
+
+
+def off_kernel(last, x_ref, s_ref, q4_ref, q2_ref, chunks, keep_ref, s1_ref, s3_ref, far_ref):
     d = lax.axis_index("row")
     y, core, far = place()
     u = nt(q2_ref[...], x_ref[1]) + nt(q4_ref[...], s_ref[0])
@@ -339,7 +339,7 @@
     far_ref[...] = u.astype(BF16)
 
 
-def off_part(last, x, s, q2, q4, near):
+def off_part(last, x, s, q4, q2, near):
     shape = (192, x.shape[1])
     return pl.pallas_call(
         functools.partial(off_kernel, last),
@@ -349,7 +349,7 @@
         out_shape=[pltpu.VMEM(shape, F32)] + [pltpu.VMEM(shape, BF16)] * 3,
         in_specs=[VMEM] * 5,
         out_specs=[VMEM] * 4,
-    )(*on_chip(x, s, q2, q4, near))
+    )(*on_chip(x, s, q4, q2, near))
 
 
 def add_kernel(at_far, keep_ref, part_ref, out_ref):
@@ -440,9 +440,9 @@
     r2 = move(q2, False, False)
     r4 = move(q4, True, True)
     o = own_part(x, others)
-    near, first = near_part(rows - 1, x, others, r1, r3, o)
+    near, first = near_part(rows - 1, x, others, r3, r1, o)
     first = along_y(first, FIRST)
-    kept, s1, s3, far = off_part(rows - 1, x, others, r2, r4, near)
+    kept, s1, s3, far = off_part(rows - 1, x, others, r4, r2, near)
     kept = add("first", False, kept, first)
     kept = add("far", True, kept, along_y(far, FINAL))
     return sum_parts(scale, kept, exchange(s1, 1), exchange(s3, 3)).T

time: 43.6 us -> 43.7 us (level)
  starting transfers between devices: 14.4 us -> 16.5 us
  waiting for transfers between devices: 21.1 us -> 19.1 us
    ppermute x5, starting transfers between devices: 7.42 us -> 9.77 us  [move(): lax.ppermute(value, ('aux', 'row'), row_moves(rows, chips, core_0_up, cro...]
    ppermute x5, waiting for transfers between devices: 11.9 us -> 9.68 us  [move(): lax.ppermute(value, ('aux', 'row'), row_moves(rows, chips, core_0_up, cro...]
  transfers between devices with their start and end apart: 11 -> 11, of which waited for: 7 -> 8; matrix products, arithmetic and copies ran while one was open for 0% -> 0% of each run, Pallas kernels for 10% -> 10%
where the time goes in v6:
time: 43.7 us; the launch traced here: 43.5 us
  waiting for transfers between devices  19.1 us (44%)
  starting transfers between devices  16.5 us (38%)
  Pallas kernels  7.88 us (18%)
    ppermute x5, starting transfers between devices, move(): lax.ppermute(value, ('aux', 'row'), row_moves(rows, chips, core_0_up, cro...  9.77 us
    ppermute x5, waiting for transfers between devices, move(): lax.ppermute(value, ('aux', 'row'), row_moves(rows, chips, core_0_up, cro...  9.68 us
    ppermute x4, waiting for transfers between devices, along_y(): return lax.ppermute(value, 'aux', pairs)  7.93 us
    ppermute x4, starting transfers between devices, along_y(): return lax.ppermute(value, 'aux', pairs)  6.53 us
    pallas_call x1, Pallas kernels, stage(): pl.pallas_call(stage_kernel, name='stage', cost_estimate=cost(512 * 1024,...  2.51 us
    pallas_call x1, Pallas kernels, half_transform(): pl.pallas_call(half_kernel, name='half', cost_estimate=cost(512 * 1024 *...  1.51 us
    ppermute x2, waiting for transfers between devices, swap(): return lax.ppermute(value, 'aux', [(i, i ^ 1) for i in range(aux_devices)])  1.44 us
    pallas_call x1, Pallas kernels, halo_to_send(): pl.pallas_call(send_kernel, name='send', cost_estimate=cost(512 * 1024, 2...  1.03 us
  transfers between devices with their start and end apart: 11, of which 8 were waited for; matrix products, arithmetic and copies ran while one was open for 0% of the time, Pallas kernels for 10%

profile of v6, /device:TPU:6, one launch (start us, length us, event | category | flops | bytes accessed | tf_op | source)
XLA Modules:
  0.0 43.5 jit_solution(4677285862635069316)
XLA Ops:
  0.0 1.0 %send.1 = bf16[768,128]{1,0:T(8,128)(2,1)S(1)} custom-call(bf16[512,2048]{1,0:T(8,128)(2,1)} %orb_ref.3), custom_call_target="tpu_custom_call" | custom-call | flops 1048576 | bytes 1048576 | tf_op jit(solution)/shard_map/send/pallas_call | solution.py:85
  1.0 2.1 %collective-permute-start = (bf16[768,128]{1,0:T(8,128)(2,1)S(1)}, bf16[768,128]{1,0:T(8,128)(2,1)S(1)}, u32[]{:S(2)}, u32[]{:S(2)}) collective-permute-start(bf16[768,128]{1,0:T(8,128)(2,1)S(1)} %send.1), channel_id=1, source_target_pairs={{0,1},{32,0},{64,65},{96,64},{128,129},{160,128},{192,193},{224,19... | collective-permute-start | bytes 589832 | tf_op jit(solution)/shard_map/ppermute | solution.py:417
  3.1 2.5 %stage.1 = (bf16[512,256]{1,0:T(8,128)(2,1)S(1)}, bf16[4,2,4,256,256]{4,3,2,1,0:T(8,128)(2,1)S(1)}, f32[2,256]{1,0:T(2,128)S(1)}, s32[2,4]{1,0:T(2,128)S(4)}) custom-call(s32[2,4]{1,0:T(2,128)} %cols_hbm.1, s32[32,64]{1,0:T(8,128)} %bitcast.2, bf16[512,2048]{1,0:T(8,128)(2,1)} %orb_ref.3, bf16[4,2,4,256,256]{4,3,2,1,0:T(8,128)(2,1)} %int_ref.1), custom_call_target="tpu_custom_call" | custom-call | flops 1048576 | bytes 9437184 | tf_op jit(solution)/shard_map/stage/pallas_call | solution.py:155
  5.6 5.3 %collective-permute-done.got_ref = bf16[768,128]{1,0:T(8,128)(2,1)S(1)} collective-permute-done((bf16[768,128]{1,0:T(8,128)(2,1)S(1)}, bf16[768,128]{1,0:T(8,128)(2,1)S(1)}, u32[]{:S(2)}, u32[]{:S(2)}) %collective-permute-start) | collective-permute-done | bytes 196640 | tf_op jit(solution)/shard_map/ppermute | solution.py:417
  11.0 0.0 collective-permute-start.1
  11.0 1.4 %collective-permute-done.1.swp_ref = bf16[768,128]{1,0:T(8,128)(2,1)S(1)} collective-permute-done((bf16[768,128]{1,0:T(8,128)(2,1)S(1)}, bf16[768,128]{1,0:T(8,128)(2,1)S(1)}, u32[]{:S(2)}, u32[]{:S(2)}) %collective-permute-start.1) | collective-permute-done | bytes 196640 | tf_op jit(solution)/shard_map/ppermute | solution.py:420
  12.4 1.5 %half.1 = (bf16[2,512,512]{2,1,0:T(8,128)(2,1)S(1)}, bf16[320,512]{1,0:T(8,128)(2,1)S(1)}, bf16[192,512]{1,0:T(8,128)(2,1)S(1)}, bf16[320,512]{1,0:T(8,128)(2,1)S(1)}, bf16[192,512]{1,0:T(8,128)(2,1)S(1)}) custom-call(s32[2,4]{1,0:T(2,128)S(4)} %get-tuple-element.29.cols_ref, f32[2,256]{1,0:T(2,128)S(1)} %get-tuple-element.30.factor_ref, ...), custom_call_target="tpu_custom_call" | custom-call | flops 1073741824 | bytes 8388608 | tf_op jit(solution)/shard_map/half/pallas_call | solution.py:240
  13.9 0.2 collective-permute-start.2
  14.1 2.4 %collective-permute-start.5 = (bf16[320,512]{1,0:T(8,128)(2,1)S(1)}, bf16[320,512]{1,0:T(8,128)(2,1)S(1)}, u32[]{:S(2)}, u32[]{:S(2)}) collective-permute-start(bf16[320,512]{1,0:T(8,128)(2,1)S(1)} %get-tuple-element.37), channel_id=1, source_target_pairs={{0,64},{32,1},{64,128},{96,65},{128,192},{160,129},{192,0},{224,19... | collective-permute-start | bytes 983048 | tf_op jit(solution)/shard_map/ppermute | solution.py:417
  16.6 0.0 collective-permute-start.6
  16.6 0.0 collective-permute-start.3
  16.6 5.3 %collective-permute-start.4 = (bf16[192,512]{1,0:T(8,128)(2,1)S(1)}, bf16[192,512]{1,0:T(8,128)(2,1)S(1)}, u32[]{:S(2)}, u32[]{:S(2)}) collective-permute-start(bf16[192,512]{1,0:T(8,128)(2,1)S(1)} %get-tuple-element.36), channel_id=1, source_target_pairs={{0,32},{32,33},{64,96},{96,97},{128,160},{160,161},{192,224},{224,... | collective-permute-start | bytes 589832 | tf_op jit(solution)/shard_map/ppermute | solution.py:417
  21.9 0.0 collective-permute-done.2.s_ref
  21.9 0.7 %own.1.o_ref = f32[256,512]{1,0:T(8,128)S(1)} custom-call(bf16[2,512,512]{2,1,0:T(8,128)(2,1)S(1)} %get-tuple-element.34.x_ref, bf16[2,512,512]{2,1,0:T(8,128)(2,1)S(1)} %collective-permute-done.2.s_ref), custom_call_target="tpu_custom_call" | custom-call | flops 536870912 | bytes 3145728 | tf_op jit(solution)/shard_map/own/pallas_call | solution.py:278
  22.6 1.2 %collective-permute-done.5.q3_ref = bf16[320,512]{1,0:T(8,128)(2,1)S(1)} collective-permute-done((bf16[320,512]{1,0:T(8,128)(2,1)S(1)}, bf16[320,512]{1,0:T(8,128)(2,1)S(1)}, u32[]{:S(2)}, u32[]{:S(2)}) %collective-permute-start.5) | collective-permute-done | bytes 327712 | tf_op jit(solution)/shard_map/ppermute | solution.py:417
  23.8 3.1 %collective-permute-done.6.q1_ref = bf16[320,512]{1,0:T(8,128)(2,1)S(1)} collective-permute-done((bf16[320,512]{1,0:T(8,128)(2,1)S(1)}, bf16[320,512]{1,0:T(8,128)(2,1)S(1)}, u32[]{:S(2)}, u32[]{:S(2)}) %collective-permute-start.6) | collective-permute-done | bytes 327712 | tf_op jit(solution)/shard_map/ppermute | solution.py:417
  26.9 0.7 %near.1 = (f32[4,192,512]{2,1,0:T(8,128)S(1)}, bf16[192,512]{1,0:T(8,128)(2,1)S(1)}) custom-call(bf16[2,512,512]{2,1,0:T(8,128)(2,1)S(1)} %get-tuple-element.34.x_ref, bf16[2,512,512]{2,1,0:T(8,128)(2,1)S(1)} %collective-permute-done.2.s_ref, bf16[320,512]{1,0:T(8,128)(2,1)S(1)} %collective-permute-done.5.q3_ref, ...), custom_call_target="tpu_custom_call" | custom-call | flops 335544320 | bytes 2097152 | tf_op jit(solution)/shard_map/near/pallas_call | solution.py:320
  27.6 3.3 %collective-permute-start.7 = (bf16[192,512]{1,0:T(8,128)(2,1)S(1)}, bf16[192,512]{1,0:T(8,128)(2,1)S(1)}, u32[]{:S(2)}, u32[]{:S(2)}) collective-permute-start(bf16[192,512]{1,0:T(8,128)(2,1)S(1)} %get-tuple-element.41), channel_id=1, source_target_pairs={{0,128},{32,160},{64,32},{96,224},{128,0},{160,192},{192,64},{224,... | collective-permute-start | bytes 589832 | tf_op jit(solution)/shard_map/ppermute | solution.py:424
  30.9 0.0 collective-permute-done.3.q4_ref
  30.9 0.0 collective-permute-done.4.q2_ref
  30.9 0.5 %off.1 = (f32[192,512]{1,0:T(8,128)S(1)}, bf16[192,512]{1,0:T(8,128)(2,1)S(1)}, bf16[192,512]{1,0:T(8,128)(2,1)S(1)}, bf16[192,512]{1,0:T(8,128)(2,1)S(1)}) custom-call(bf16[2,512,512]{2,1,0:T(8,128)(2,1)S(1)} %get-tuple-element.34.x_ref, bf16[2,512,512]{2,1,0:T(8,128)(2,1)S(1)} %collective-permute-done.2.s_ref, ...), custom_call_target="tpu_custom_call" | custom-call | flops 201326592 | bytes 4194304 | tf_op jit(solution)/shard_map/off/pallas_call | solution.py:344
  31.4 0.7 %collective-permute-start.8 = (bf16[192,512]{1,0:T(8,128)(2,1)S(1)}, bf16[192,512]{1,0:T(8,128)(2,1)S(1)}, u32[]{:S(2)}, u32[]{:S(2)}) collective-permute-start(bf16[192,512]{1,0:T(8,128)(2,1)S(1)} %get-tuple-element.42), channel_id=1, source_target_pairs={{0,96},{32,0},{64,192},{96,64},{128,160},{160,32},{192,224},{224,1... | collective-permute-start | bytes 589832 | tf_op jit(solution)/shard_map/ppermute | solution.py:424
  32.1 1.3 %collective-permute-start.9 = (bf16[192,512]{1,0:T(8,128)(2,1)S(1)}, bf16[192,512]{1,0:T(8,128)(2,1)S(1)}, u32[]{:S(2)}, u32[]{:S(2)}) collective-permute-start(bf16[192,512]{1,0:T(8,128)(2,1)S(1)} %get-tuple-element.43), channel_id=1, source_target_pairs={{0,64},{32,96},{64,0},{96,32},{128,192},{160,224},{192,128},{224,1... | collective-permute-start | bytes 589832 | tf_op jit(solution)/shard_map/ppermute | solution.py:424
  33.4 1.2 %collective-permute-start.10 = (bf16[192,512]{1,0:T(8,128)(2,1)S(1)}, bf16[192,512]{1,0:T(8,128)(2,1)S(1)}, u32[]{:S(2)}, u32[]{:S(2)}) collective-permute-start(bf16[192,512]{1,0:T(8,128)(2,1)S(1)} %get-tuple-element.44), channel_id=1, source_target_pairs={{0,192},{32,224},{64,128},{96,160},{128,64},{160,96},{192,0},{224,... | collective-permute-start | bytes 589832 | tf_op jit(solution)/shard_map/ppermute | solution.py:424
  34.7 2.0 %collective-permute-done.7.part_ref = bf16[192,512]{1,0:T(8,128)(2,1)S(1)} collective-permute-done((bf16[192,512]{1,0:T(8,128)(2,1)S(1)}, bf16[192,512]{1,0:T(8,128)(2,1)S(1)}, u32[]{:S(2)}, u32[]{:S(2)}) %collective-permute-start.7) | collective-permute-done | bytes 196640 | tf_op jit(solution)/shard_map/ppermute | solution.py:424
  36.7 0.1 first.1.keep_ref
  36.7 1.5 %collective-permute-done.8.part_ref = bf16[192,512]{1,0:T(8,128)(2,1)S(1)} collective-permute-done((bf16[192,512]{1,0:T(8,128)(2,1)S(1)}, bf16[192,512]{1,0:T(8,128)(2,1)S(1)}, u32[]{:S(2)}, u32[]{:S(2)}) %collective-permute-start.8) | collective-permute-done | bytes 196640 | tf_op jit(solution)/shard_map/ppermute | solution.py:424
  38.3 0.1 far.1.keep_ref
  38.3 3.0 %collective-permute-done.9.s1_ref = bf16[192,512]{1,0:T(8,128)(2,1)S(1)} collective-permute-done((bf16[192,512]{1,0:T(8,128)(2,1)S(1)}, bf16[192,512]{1,0:T(8,128)(2,1)S(1)}, u32[]{:S(2)}, u32[]{:S(2)}) %collective-permute-start.9) | collective-permute-done | bytes 196640 | tf_op jit(solution)/shard_map/ppermute | solution.py:424
  41.3 1.4 %collective-permute-done.10.s3_ref = bf16[192,512]{1,0:T(8,128)(2,1)S(1)} collective-permute-done((bf16[192,512]{1,0:T(8,128)(2,1)S(1)}, bf16[192,512]{1,0:T(8,128)(2,1)S(1)}, u32[]{:S(2)}, u32[]{:S(2)}) %collective-permute-start.10) | collective-permute-done | bytes 196640 | tf_op jit(solution)/shard_map/ppermute | solution.py:424
  42.7 0.8 %sum.1 = f32[192,512]{1,0:T(8,128)} custom-call(f32[192,512]{1,0:T(8,128)S(1)} %far.1.keep_ref, bf16[192,512]{1,0:T(8,128)(2,1)S(1)} %collective-permute-done.9.s1_ref, bf16[192,512]{1,0:T(8,128)(2,1)S(1)} %collective-permute-done.10.s3_ref), custom_call_target="tpu_custom_call" | custom-call | flops 196608 | bytes 1048576 | tf_op jit(solution)/shard_map/sum/pallas_call | solution.py:378
Async XLA Ops:
  1.0 9.9 %collective-permute-start = (bf16[768,128]{1,0:T(8,128)(2,1)S(1)}, bf16[768,128]{1,0:T(8,128)(2,1)S(1)}, u32[]{:S(2)}, u32[]{:S(2)}) collective-permute-start(bf16[768,128]{1,0:T(8,128)(2,1)S(1)} %send.1), channel_id=1, source_target_pairs={{0,1},{32,0},{64,65},{96,64},{128,129},{160,128},{192,193},{224,19... | collective-permute-start | bytes 589832 | tf_op jit(solution)/shard_map/ppermute | solution.py:417
  11.0 1.4 %collective-permute-start.1 = (bf16[768,128]{1,0:T(8,128)(2,1)S(1)}, bf16[768,128]{1,0:T(8,128)(2,1)S(1)}, u32[]{:S(2)}, u32[]{:S(2)}) collective-permute-start(bf16[768,128]{1,0:T(8,128)(2,1)S(1)} %collective-permute-done.got_ref), channel_id=1, source_target_pairs={{0,32},{32,0},{64,96},{96,64},{128,160},{160,128},{192,224},{224,1... | collective-permute-start | bytes 589832 | tf_op jit(solution)/shard_map/ppermute | solution.py:420
  13.9 7.9 %collective-permute-start.2 = (bf16[2,512,512]{2,1,0:T(8,128)(2,1)S(1)}, bf16[2,512,512]{2,1,0:T(8,128)(2,1)S(1)}, u32[]{:S(2)}, u32[]{:S(2)}) collective-permute-start(bf16[2,512,512]{2,1,0:T(8,128)(2,1)S(1)} %get-tuple-element.34.x_ref), channel_id=1, source_target_pairs={{0,32},{32,0},{64,96},{96,64},{128,160},{160,128},{192,224},{224,1... | collective-permute-start | bytes 3145736 | tf_op jit(solution)/shard_map/ppermute | solution.py:420
  14.1 9.7 %collective-permute-start.5 = (bf16[320,512]{1,0:T(8,128)(2,1)S(1)}, bf16[320,512]{1,0:T(8,128)(2,1)S(1)}, u32[]{:S(2)}, u32[]{:S(2)}) collective-permute-start(bf16[320,512]{1,0:T(8,128)(2,1)S(1)} %get-tuple-element.37), channel_id=1, source_target_pairs={{0,64},{32,1},{64,128},{96,65},{128,192},{160,129},{192,0},{224,19... | collective-permute-start | bytes 983048 | tf_op jit(solution)/shard_map/ppermute | solution.py:417
  16.6 10.4 %collective-permute-start.6 = (bf16[320,512]{1,0:T(8,128)(2,1)S(1)}, bf16[320,512]{1,0:T(8,128)(2,1)S(1)}, u32[]{:S(2)}, u32[]{:S(2)}) collective-permute-start(bf16[320,512]{1,0:T(8,128)(2,1)S(1)} %get-tuple-element.38), channel_id=1, source_target_pairs={{0,1},{32,0},{64,65},{96,64},{128,129},{160,128},{192,193},{224,19... | collective-permute-start | bytes 983048 | tf_op jit(solution)/shard_map/ppermute | solution.py:417
  16.6 14.3 %collective-permute-start.3 = (bf16[192,512]{1,0:T(8,128)(2,1)S(1)}, bf16[192,512]{1,0:T(8,128)(2,1)S(1)}, u32[]{:S(2)}, u32[]{:S(2)}) collective-permute-start(bf16[192,512]{1,0:T(8,128)(2,1)S(1)} %get-tuple-element.35), channel_id=1, source_target_pairs={{0,33},{32,96},{64,97},{96,160},{128,161},{160,224},{192,225},{224... | collective-permute-start | bytes 589832 | tf_op jit(solution)/shard_map/ppermute | solution.py:417
  16.6 14.3 %collective-permute-start.4 = (bf16[192,512]{1,0:T(8,128)(2,1)S(1)}, bf16[192,512]{1,0:T(8,128)(2,1)S(1)}, u32[]{:S(2)}, u32[]{:S(2)}) collective-permute-start(bf16[192,512]{1,0:T(8,128)(2,1)S(1)} %get-tuple-element.36), channel_id=1, source_target_pairs={{0,32},{32,33},{64,96},{96,97},{128,160},{160,161},{192,224},{224,... | collective-permute-start | bytes 589832 | tf_op jit(solution)/shard_map/ppermute | solution.py:417
  27.6 9.1 %collective-permute-start.7 = (bf16[192,512]{1,0:T(8,128)(2,1)S(1)}, bf16[192,512]{1,0:T(8,128)(2,1)S(1)}, u32[]{:S(2)}, u32[]{:S(2)}) collective-permute-start(bf16[192,512]{1,0:T(8,128)(2,1)S(1)} %get-tuple-element.41), channel_id=1, source_target_pairs={{0,128},{32,160},{64,32},{96,224},{128,0},{160,192},{192,64},{224,... | collective-permute-start | bytes 589832 | tf_op jit(solution)/shard_map/ppermute | solution.py:424
  31.4 6.9 %collective-permute-start.8 = (bf16[192,512]{1,0:T(8,128)(2,1)S(1)}, bf16[192,512]{1,0:T(8,128)(2,1)S(1)}, u32[]{:S(2)}, u32[]{:S(2)}) collective-permute-start(bf16[192,512]{1,0:T(8,128)(2,1)S(1)} %get-tuple-element.42), channel_id=1, source_target_pairs={{0,96},{32,0},{64,192},{96,64},{128,160},{160,32},{192,224},{224,1... | collective-permute-start | bytes 589832 | tf_op jit(solution)/shard_map/ppermute | solution.py:424
  32.1 9.2 %collective-permute-start.9 = (bf16[192,512]{1,0:T(8,128)(2,1)S(1)}, bf16[192,512]{1,0:T(8,128)(2,1)S(1)}, u32[]{:S(2)}, u32[]{:S(2)}) collective-permute-start(bf16[192,512]{1,0:T(8,128)(2,1)S(1)} %get-tuple-element.43), channel_id=1, source_target_pairs={{0,64},{32,96},{64,0},{96,32},{128,192},{160,224},{192,128},{224,1... | collective-permute-start | bytes 589832 | tf_op jit(solution)/shard_map/ppermute | solution.py:424
  33.4 9.3 %collective-permute-start.10 = (bf16[192,512]{1,0:T(8,128)(2,1)S(1)}, bf16[192,512]{1,0:T(8,128)(2,1)S(1)}, u32[]{:S(2)}, u32[]{:S(2)}) collective-permute-start(bf16[192,512]{1,0:T(8,128)(2,1)S(1)} %get-tuple-element.44), channel_id=1, source_target_pairs={{0,192},{32,224},{64,128},{96,160},{128,64},{160,96},{192,0},{224,... | collective-permute-start | bytes 589832 | tf_op jit(solution)/shard_map/ppermute | solution.py:424

commit v7 on v6

--- a/solution.py
+++ b/solution.py
@@ -369,20 +369,31 @@
     )(*on_chip(kept, part))
 
 
-def sum_kernel(scale, keep_ref, s1_ref, s3_ref, out_ref):
-    total = keep_ref[...] + s1_ref[...].astype(F32) + s3_ref[...].astype(F32)
-    out_ref[...] = total * scale
+def sum_kernel(scale, keep_ref, s1_ref, s3_ref, out_ref, buf, sems):
+    pieces = sems.shape[0]
+    rows = buf.shape[0] // pieces
+    copies = []
+    for i in range(pieces):
+        at = pl.ds(i * rows, rows)
+        total = keep_ref[at] + s1_ref[at].astype(F32) + s3_ref[at].astype(F32)
+        buf[at] = total * scale
+        copies.append(pltpu.make_async_copy(buf.at[at], out_ref.at[at], sems.at[i]))
+        copies[-1].start()
+    for copy in copies:
+        copy.wait()
 
 
 def sum_parts(scale, *parts):
+    shape = parts[0].shape
     return pl.pallas_call(
         functools.partial(sum_kernel, scale),
         name="sum",
         cost_estimate=cost(192 * 512, 2**20),
         compiler_params=room(4),
-        out_shape=jax.ShapeDtypeStruct(parts[0].shape, F32),
+        out_shape=jax.ShapeDtypeStruct(shape, F32),
         in_specs=[VMEM] * len(parts),
-        out_specs=VMEM,
+        out_specs=ANY,
+        scratch_shapes=[pltpu.VMEM(shape, F32), pltpu.SemaphoreType.DMA((6,))],
     )(*on_chip(*parts))
 
 

time: 43.7 us -> 43.7 us (level)
  no operation moved by 1% of the time
where the time goes in v7:
time: 43.7 us; the launch traced here: 43.5 us
  waiting for transfers between devices  19.1 us (44%)
  starting transfers between devices  16.5 us (38%)
  Pallas kernels  7.86 us (18%)
    ppermute x5, starting transfers between devices, move(): lax.ppermute(value, ('aux', 'row'), row_moves(rows, chips, core_0_up, cro...  9.77 us
    ppermute x5, waiting for transfers between devices, move(): lax.ppermute(value, ('aux', 'row'), row_moves(rows, chips, core_0_up, cro...  9.68 us
    ppermute x4, waiting for transfers between devices, along_y(): return lax.ppermute(value, 'aux', pairs)  7.93 us
    ppermute x4, starting transfers between devices, along_y(): return lax.ppermute(value, 'aux', pairs)  6.53 us
    pallas_call x1, Pallas kernels, stage(): pl.pallas_call(stage_kernel, name='stage', cost_estimate=cost(512 * 1024,...  2.51 us
    pallas_call x1, Pallas kernels, half_transform(): pl.pallas_call(half_kernel, name='half', cost_estimate=cost(512 * 1024 *...  1.51 us
    ppermute x2, waiting for transfers between devices, swap(): return lax.ppermute(value, 'aux', [(i, i ^ 1) for i in range(aux_devices)])  1.44 us
    pallas_call x1, Pallas kernels, halo_to_send(): pl.pallas_call(send_kernel, name='send', cost_estimate=cost(512 * 1024, 2...  1.03 us
  transfers between devices with their start and end apart: 11, of which 8 were waited for; matrix products, arithmetic and copies ran while one was open for 0% of the time, Pallas kernels for 10%

profile of v7, /device:TPU:6, one launch (start us, length us, event | category | flops | bytes accessed | tf_op | source)
XLA Modules:
  0.0 43.5 jit_solution(18360308090616086073)
XLA Ops:
  0.0 1.0 %send.1 = bf16[768,128]{1,0:T(8,128)(2,1)S(1)} custom-call(bf16[512,2048]{1,0:T(8,128)(2,1)} %orb_ref.3), custom_call_target="tpu_custom_call" | custom-call | flops 1048576 | bytes 1048576 | tf_op jit(solution)/shard_map/send/pallas_call | solution.py:85
  1.0 2.1 %collective-permute-start = (bf16[768,128]{1,0:T(8,128)(2,1)S(1)}, bf16[768,128]{1,0:T(8,128)(2,1)S(1)}, u32[]{:S(2)}, u32[]{:S(2)}) collective-permute-start(bf16[768,128]{1,0:T(8,128)(2,1)S(1)} %send.1), channel_id=1, source_target_pairs={{0,1},{32,0},{64,65},{96,64},{128,129},{160,128},{192,193},{224,19... | collective-permute-start | bytes 589832 | tf_op jit(solution)/shard_map/ppermute | solution.py:428
  3.1 2.5 %stage.1 = (bf16[512,256]{1,0:T(8,128)(2,1)S(1)}, bf16[4,2,4,256,256]{4,3,2,1,0:T(8,128)(2,1)S(1)}, f32[2,256]{1,0:T(2,128)S(1)}, s32[2,4]{1,0:T(2,128)S(4)}) custom-call(s32[2,4]{1,0:T(2,128)} %cols_hbm.1, s32[32,64]{1,0:T(8,128)} %bitcast.2, bf16[512,2048]{1,0:T(8,128)(2,1)} %orb_ref.3, bf16[4,2,4,256,256]{4,3,2,1,0:T(8,128)(2,1)} %int_ref.1), custom_call_target="tpu_custom_call" | custom-call | flops 1048576 | bytes 9437184 | tf_op jit(solution)/shard_map/stage/pallas_call | solution.py:155
  5.6 5.3 %collective-permute-done.got_ref = bf16[768,128]{1,0:T(8,128)(2,1)S(1)} collective-permute-done((bf16[768,128]{1,0:T(8,128)(2,1)S(1)}, bf16[768,128]{1,0:T(8,128)(2,1)S(1)}, u32[]{:S(2)}, u32[]{:S(2)}) %collective-permute-start) | collective-permute-done | bytes 196640 | tf_op jit(solution)/shard_map/ppermute | solution.py:428
  11.0 0.0 collective-permute-start.1
  11.0 1.4 %collective-permute-done.1.swp_ref = bf16[768,128]{1,0:T(8,128)(2,1)S(1)} collective-permute-done((bf16[768,128]{1,0:T(8,128)(2,1)S(1)}, bf16[768,128]{1,0:T(8,128)(2,1)S(1)}, u32[]{:S(2)}, u32[]{:S(2)}) %collective-permute-start.1) | collective-permute-done | bytes 196640 | tf_op jit(solution)/shard_map/ppermute | solution.py:431
  12.4 1.5 %half.1 = (bf16[2,512,512]{2,1,0:T(8,128)(2,1)S(1)}, bf16[320,512]{1,0:T(8,128)(2,1)S(1)}, bf16[192,512]{1,0:T(8,128)(2,1)S(1)}, bf16[320,512]{1,0:T(8,128)(2,1)S(1)}, bf16[192,512]{1,0:T(8,128)(2,1)S(1)}) custom-call(s32[2,4]{1,0:T(2,128)S(4)} %get-tuple-element.29.cols_ref, f32[2,256]{1,0:T(2,128)S(1)} %get-tuple-element.30.factor_ref, ...), custom_call_target="tpu_custom_call" | custom-call | flops 1073741824 | bytes 8388608 | tf_op jit(solution)/shard_map/half/pallas_call | solution.py:240
  13.9 0.2 collective-permute-start.2
  14.1 2.4 %collective-permute-start.5 = (bf16[320,512]{1,0:T(8,128)(2,1)S(1)}, bf16[320,512]{1,0:T(8,128)(2,1)S(1)}, u32[]{:S(2)}, u32[]{:S(2)}) collective-permute-start(bf16[320,512]{1,0:T(8,128)(2,1)S(1)} %get-tuple-element.37), channel_id=1, source_target_pairs={{0,64},{32,1},{64,128},{96,65},{128,192},{160,129},{192,0},{224,19... | collective-permute-start | bytes 983048 | tf_op jit(solution)/shard_map/ppermute | solution.py:428
  16.6 0.0 collective-permute-start.6
  16.6 0.0 collective-permute-start.3
  16.6 5.3 %collective-permute-start.4 = (bf16[192,512]{1,0:T(8,128)(2,1)S(1)}, bf16[192,512]{1,0:T(8,128)(2,1)S(1)}, u32[]{:S(2)}, u32[]{:S(2)}) collective-permute-start(bf16[192,512]{1,0:T(8,128)(2,1)S(1)} %get-tuple-element.36), channel_id=1, source_target_pairs={{0,32},{32,33},{64,96},{96,97},{128,160},{160,161},{192,224},{224,... | collective-permute-start | bytes 589832 | tf_op jit(solution)/shard_map/ppermute | solution.py:428
  21.9 0.0 collective-permute-done.2.s_ref
  21.9 0.7 %own.1.o_ref = f32[256,512]{1,0:T(8,128)S(1)} custom-call(bf16[2,512,512]{2,1,0:T(8,128)(2,1)S(1)} %get-tuple-element.34.x_ref, bf16[2,512,512]{2,1,0:T(8,128)(2,1)S(1)} %collective-permute-done.2.s_ref), custom_call_target="tpu_custom_call" | custom-call | flops 536870912 | bytes 3145728 | tf_op jit(solution)/shard_map/own/pallas_call | solution.py:278
  22.6 1.2 %collective-permute-done.5.q3_ref = bf16[320,512]{1,0:T(8,128)(2,1)S(1)} collective-permute-done((bf16[320,512]{1,0:T(8,128)(2,1)S(1)}, bf16[320,512]{1,0:T(8,128)(2,1)S(1)}, u32[]{:S(2)}, u32[]{:S(2)}) %collective-permute-start.5) | collective-permute-done | bytes 327712 | tf_op jit(solution)/shard_map/ppermute | solution.py:428
  23.8 3.1 %collective-permute-done.6.q1_ref = bf16[320,512]{1,0:T(8,128)(2,1)S(1)} collective-permute-done((bf16[320,512]{1,0:T(8,128)(2,1)S(1)}, bf16[320,512]{1,0:T(8,128)(2,1)S(1)}, u32[]{:S(2)}, u32[]{:S(2)}) %collective-permute-start.6) | collective-permute-done | bytes 327712 | tf_op jit(solution)/shard_map/ppermute | solution.py:428
  26.9 0.7 %near.1 = (f32[4,192,512]{2,1,0:T(8,128)S(1)}, bf16[192,512]{1,0:T(8,128)(2,1)S(1)}) custom-call(bf16[2,512,512]{2,1,0:T(8,128)(2,1)S(1)} %get-tuple-element.34.x_ref, bf16[2,512,512]{2,1,0:T(8,128)(2,1)S(1)} %collective-permute-done.2.s_ref, bf16[320,512]{1,0:T(8,128)(2,1)S(1)} %collective-permute-done.5.q3_ref, ...), custom_call_target="tpu_custom_call" | custom-call | flops 335544320 | bytes 2097152 | tf_op jit(solution)/shard_map/near/pallas_call | solution.py:320
  27.6 3.3 %collective-permute-start.7 = (bf16[192,512]{1,0:T(8,128)(2,1)S(1)}, bf16[192,512]{1,0:T(8,128)(2,1)S(1)}, u32[]{:S(2)}, u32[]{:S(2)}) collective-permute-start(bf16[192,512]{1,0:T(8,128)(2,1)S(1)} %get-tuple-element.41), channel_id=1, source_target_pairs={{0,128},{32,160},{64,32},{96,224},{128,0},{160,192},{192,64},{224,... | collective-permute-start | bytes 589832 | tf_op jit(solution)/shard_map/ppermute | solution.py:435
  30.9 0.0 collective-permute-done.3.q4_ref
  30.9 0.0 collective-permute-done.4.q2_ref
  30.9 0.5 %off.1 = (f32[192,512]{1,0:T(8,128)S(1)}, bf16[192,512]{1,0:T(8,128)(2,1)S(1)}, bf16[192,512]{1,0:T(8,128)(2,1)S(1)}, bf16[192,512]{1,0:T(8,128)(2,1)S(1)}) custom-call(bf16[2,512,512]{2,1,0:T(8,128)(2,1)S(1)} %get-tuple-element.34.x_ref, bf16[2,512,512]{2,1,0:T(8,128)(2,1)S(1)} %collective-permute-done.2.s_ref, ...), custom_call_target="tpu_custom_call" | custom-call | flops 201326592 | bytes 4194304 | tf_op jit(solution)/shard_map/off/pallas_call | solution.py:344
  31.4 0.7 %collective-permute-start.8 = (bf16[192,512]{1,0:T(8,128)(2,1)S(1)}, bf16[192,512]{1,0:T(8,128)(2,1)S(1)}, u32[]{:S(2)}, u32[]{:S(2)}) collective-permute-start(bf16[192,512]{1,0:T(8,128)(2,1)S(1)} %get-tuple-element.42), channel_id=1, source_target_pairs={{0,96},{32,0},{64,192},{96,64},{128,160},{160,32},{192,224},{224,1... | collective-permute-start | bytes 589832 | tf_op jit(solution)/shard_map/ppermute | solution.py:435
  32.1 1.3 %collective-permute-start.9 = (bf16[192,512]{1,0:T(8,128)(2,1)S(1)}, bf16[192,512]{1,0:T(8,128)(2,1)S(1)}, u32[]{:S(2)}, u32[]{:S(2)}) collective-permute-start(bf16[192,512]{1,0:T(8,128)(2,1)S(1)} %get-tuple-element.43), channel_id=1, source_target_pairs={{0,64},{32,96},{64,0},{96,32},{128,192},{160,224},{192,128},{224,1... | collective-permute-start | bytes 589832 | tf_op jit(solution)/shard_map/ppermute | solution.py:435
  33.4 1.2 %collective-permute-start.10 = (bf16[192,512]{1,0:T(8,128)(2,1)S(1)}, bf16[192,512]{1,0:T(8,128)(2,1)S(1)}, u32[]{:S(2)}, u32[]{:S(2)}) collective-permute-start(bf16[192,512]{1,0:T(8,128)(2,1)S(1)} %get-tuple-element.44), channel_id=1, source_target_pairs={{0,192},{32,224},{64,128},{96,160},{128,64},{160,96},{192,0},{224,... | collective-permute-start | bytes 589832 | tf_op jit(solution)/shard_map/ppermute | solution.py:435
  34.7 2.0 %collective-permute-done.7.part_ref = bf16[192,512]{1,0:T(8,128)(2,1)S(1)} collective-permute-done((bf16[192,512]{1,0:T(8,128)(2,1)S(1)}, bf16[192,512]{1,0:T(8,128)(2,1)S(1)}, u32[]{:S(2)}, u32[]{:S(2)}) %collective-permute-start.7) | collective-permute-done | bytes 196640 | tf_op jit(solution)/shard_map/ppermute | solution.py:435
  36.7 0.1 first.1.keep_ref
  36.7 1.5 %collective-permute-done.8.part_ref = bf16[192,512]{1,0:T(8,128)(2,1)S(1)} collective-permute-done((bf16[192,512]{1,0:T(8,128)(2,1)S(1)}, bf16[192,512]{1,0:T(8,128)(2,1)S(1)}, u32[]{:S(2)}, u32[]{:S(2)}) %collective-permute-start.8) | collective-permute-done | bytes 196640 | tf_op jit(solution)/shard_map/ppermute | solution.py:435
  38.3 0.1 far.1.keep_ref
  38.3 3.0 %collective-permute-done.9.s1_ref = bf16[192,512]{1,0:T(8,128)(2,1)S(1)} collective-permute-done((bf16[192,512]{1,0:T(8,128)(2,1)S(1)}, bf16[192,512]{1,0:T(8,128)(2,1)S(1)}, u32[]{:S(2)}, u32[]{:S(2)}) %collective-permute-start.9) | collective-permute-done | bytes 196640 | tf_op jit(solution)/shard_map/ppermute | solution.py:435
  41.3 1.4 %collective-permute-done.10.s3_ref = bf16[192,512]{1,0:T(8,128)(2,1)S(1)} collective-permute-done((bf16[192,512]{1,0:T(8,128)(2,1)S(1)}, bf16[192,512]{1,0:T(8,128)(2,1)S(1)}, u32[]{:S(2)}, u32[]{:S(2)}) %collective-permute-start.10) | collective-permute-done | bytes 196640 | tf_op jit(solution)/shard_map/ppermute | solution.py:435
  42.7 0.8 %sum.1 = f32[192,512]{1,0:T(8,128)} custom-call(f32[192,512]{1,0:T(8,128)S(1)} %far.1.keep_ref, bf16[192,512]{1,0:T(8,128)(2,1)S(1)} %collective-permute-done.9.s1_ref, bf16[192,512]{1,0:T(8,128)(2,1)S(1)} %collective-permute-done.10.s3_ref), custom_call_target="tpu_custom_call" | custom-call | flops 196608 | bytes 1048576 | tf_op jit(solution)/shard_map/sum/pallas_call | solution.py:388
Async XLA Ops:
  1.0 9.9 %collective-permute-start = (bf16[768,128]{1,0:T(8,128)(2,1)S(1)}, bf16[768,128]{1,0:T(8,128)(2,1)S(1)}, u32[]{:S(2)}, u32[]{:S(2)}) collective-permute-start(bf16[768,128]{1,0:T(8,128)(2,1)S(1)} %send.1), channel_id=1, source_target_pairs={{0,1},{32,0},{64,65},{96,64},{128,129},{160,128},{192,193},{224,19... | collective-permute-start | bytes 589832 | tf_op jit(solution)/shard_map/ppermute | solution.py:428
  11.0 1.4 %collective-permute-start.1 = (bf16[768,128]{1,0:T(8,128)(2,1)S(1)}, bf16[768,128]{1,0:T(8,128)(2,1)S(1)}, u32[]{:S(2)}, u32[]{:S(2)}) collective-permute-start(bf16[768,128]{1,0:T(8,128)(2,1)S(1)} %collective-permute-done.got_ref), channel_id=1, source_target_pairs={{0,32},{32,0},{64,96},{96,64},{128,160},{160,128},{192,224},{224,1... | collective-permute-start | bytes 589832 | tf_op jit(solution)/shard_map/ppermute | solution.py:431
  13.9 7.9 %collective-permute-start.2 = (bf16[2,512,512]{2,1,0:T(8,128)(2,1)S(1)}, bf16[2,512,512]{2,1,0:T(8,128)(2,1)S(1)}, u32[]{:S(2)}, u32[]{:S(2)}) collective-permute-start(bf16[2,512,512]{2,1,0:T(8,128)(2,1)S(1)} %get-tuple-element.34.x_ref), channel_id=1, source_target_pairs={{0,32},{32,0},{64,96},{96,64},{128,160},{160,128},{192,224},{224,1... | collective-permute-start | bytes 3145736 | tf_op jit(solution)/shard_map/ppermute | solution.py:431
  14.1 9.7 %collective-permute-start.5 = (bf16[320,512]{1,0:T(8,128)(2,1)S(1)}, bf16[320,512]{1,0:T(8,128)(2,1)S(1)}, u32[]{:S(2)}, u32[]{:S(2)}) collective-permute-start(bf16[320,512]{1,0:T(8,128)(2,1)S(1)} %get-tuple-element.37), channel_id=1, source_target_pairs={{0,64},{32,1},{64,128},{96,65},{128,192},{160,129},{192,0},{224,19... | collective-permute-start | bytes 983048 | tf_op jit(solution)/shard_map/ppermute | solution.py:428
  16.6 10.4 %collective-permute-start.6 = (bf16[320,512]{1,0:T(8,128)(2,1)S(1)}, bf16[320,512]{1,0:T(8,128)(2,1)S(1)}, u32[]{:S(2)}, u32[]{:S(2)}) collective-permute-start(bf16[320,512]{1,0:T(8,128)(2,1)S(1)} %get-tuple-element.38), channel_id=1, source_target_pairs={{0,1},{32,0},{64,65},{96,64},{128,129},{160,128},{192,193},{224,19... | collective-permute-start | bytes 983048 | tf_op jit(solution)/shard_map/ppermute | solution.py:428
  16.6 14.3 %collective-permute-start.3 = (bf16[192,512]{1,0:T(8,128)(2,1)S(1)}, bf16[192,512]{1,0:T(8,128)(2,1)S(1)}, u32[]{:S(2)}, u32[]{:S(2)}) collective-permute-start(bf16[192,512]{1,0:T(8,128)(2,1)S(1)} %get-tuple-element.35), channel_id=1, source_target_pairs={{0,33},{32,96},{64,97},{96,160},{128,161},{160,224},{192,225},{224... | collective-permute-start | bytes 589832 | tf_op jit(solution)/shard_map/ppermute | solution.py:428
  16.6 14.3 %collective-permute-start.4 = (bf16[192,512]{1,0:T(8,128)(2,1)S(1)}, bf16[192,512]{1,0:T(8,128)(2,1)S(1)}, u32[]{:S(2)}, u32[]{:S(2)}) collective-permute-start(bf16[192,512]{1,0:T(8,128)(2,1)S(1)} %get-tuple-element.36), channel_id=1, source_target_pairs={{0,32},{32,33},{64,96},{96,97},{128,160},{160,161},{192,224},{224,... | collective-permute-start | bytes 589832 | tf_op jit(solution)/shard_map/ppermute | solution.py:428
  27.6 9.1 %collective-permute-start.7 = (bf16[192,512]{1,0:T(8,128)(2,1)S(1)}, bf16[192,512]{1,0:T(8,128)(2,1)S(1)}, u32[]{:S(2)}, u32[]{:S(2)}) collective-permute-start(bf16[192,512]{1,0:T(8,128)(2,1)S(1)} %get-tuple-element.41), channel_id=1, source_target_pairs={{0,128},{32,160},{64,32},{96,224},{128,0},{160,192},{192,64},{224,... | collective-permute-start | bytes 589832 | tf_op jit(solution)/shard_map/ppermute | solution.py:435
  31.4 6.9 %collective-permute-start.8 = (bf16[192,512]{1,0:T(8,128)(2,1)S(1)}, bf16[192,512]{1,0:T(8,128)(2,1)S(1)}, u32[]{:S(2)}, u32[]{:S(2)}) collective-permute-start(bf16[192,512]{1,0:T(8,128)(2,1)S(1)} %get-tuple-element.42), channel_id=1, source_target_pairs={{0,96},{32,0},{64,192},{96,64},{128,160},{160,32},{192,224},{224,1... | collective-permute-start | bytes 589832 | tf_op jit(solution)/shard_map/ppermute | solution.py:435
  32.1 9.2 %collective-permute-start.9 = (bf16[192,512]{1,0:T(8,128)(2,1)S(1)}, bf16[192,512]{1,0:T(8,128)(2,1)S(1)}, u32[]{:S(2)}, u32[]{:S(2)}) collective-permute-start(bf16[192,512]{1,0:T(8,128)(2,1)S(1)} %get-tuple-element.43), channel_id=1, source_target_pairs={{0,64},{32,96},{64,0},{96,32},{128,192},{160,224},{192,128},{224,1... | collective-permute-start | bytes 589832 | tf_op jit(solution)/shard_map/ppermute | solution.py:435
  33.4 9.3 %collective-permute-start.10 = (bf16[192,512]{1,0:T(8,128)(2,1)S(1)}, bf16[192,512]{1,0:T(8,128)(2,1)S(1)}, u32[]{:S(2)}, u32[]{:S(2)}) collective-permute-start(bf16[192,512]{1,0:T(8,128)(2,1)S(1)} %get-tuple-element.44), channel_id=1, source_target_pairs={{0,192},{32,224},{64,128},{96,160},{128,64},{160,96},{192,0},{224,... | collective-permute-start | bytes 589832 | tf_op jit(solution)/shard_map/ppermute | solution.py:435
